TPU v7x, 256 devices: a whole 4x4x8 slice. The times are simulated.
256 devices in a mesh: seq: 2 (over core), ctx: 64 (over x_lo, y, z), head: 2 (over x_hi).
Axes of the slice: x: 4 (x_hi: 2, x_lo: 2; x = x_hi * 2 + x_lo), y: 4, z: 8, core: 2. Of those that a mesh axis runs over, the one named last changes fastest.
Arguments:
- queries: bfloat16 [16384, 8, 128], P(('seq', 'ctx'), 'head'), parts along dimension 0, may hold values from -8 to 8
- key_rows: bfloat16 [16384, 128], P(('seq', 'ctx')), parts along dimension 0, may hold values from -8 to 8
- value_rows: bfloat16 [16384, 128], P(('seq', 'ctx')), parts along dimension 0, may hold values from -6 to 6
- out_grad: bfloat16 [16384, 8, 128], P(('seq', 'ctx'), 'head'), parts along dimension 0, may hold values from -6 to 6
- doc_lengths: int32 [16], P('seq'), parts along dimension 0, may hold values from 1 to 2048, 8192 in all
- balance: int32 [16384], P('seq'), parts along dimension 0, may hold values from 0 to 8191, as said below
Outputs:
- attended: bfloat16 [16384, 8, 128], P(('seq', 'ctx'), 'head'), parts along dimension 0
- query_grad: bfloat16 [16384, 8, 128], P(('seq', 'ctx'), 'head'), parts along dimension 0
- key_grad: bfloat16 [16384, 128], P(('seq', 'ctx')), parts along dimension 0
- value_grad: bfloat16 [16384, 128], P(('seq', 'ctx')), parts along dimension 0
There are 2 independent parts, one for each index of `seq`. A program takes and returns all parts, laid end to end along the dimension named above; each array names one. Nothing has to cross between parts.
Inputs may be any that keep to these rules, and one draw needn't show every extreme that they name: `doc_lengths`: the lengths sum to 8192 and the longest is exactly 2048. `balance`: A permutation of the positions that moves aligned runs of 64 positions whole and in order.
All inputs are finite; a program needn't handle non-finite values.
Results may differ from a plain program's by a relative error of at most 0.034.
Values may be sent and summed in bfloat16 or wider, within the bound.
A program may use at most 64 MiB of HBM per device.

v0:
```python
import math

import jax
import jax.numpy as jnp
from jax import lax
from jax.sharding import PartitionSpec as P

NEGATIVE = -1e30


def document_of(positions, doc_lengths):
    doc_ends = jnp.cumsum(doc_lengths)
    return jnp.sum((positions[:, None] >= doc_ends[None, :]).astype(jnp.int32), axis=1)


def body(queries, key_rows, value_rows, out_grad, doc_lengths, balance):
    tok_rows = queries.shape[0]
    heads_here = queries.shape[1]
    head_width = queries.shape[2]
    scaling = 1.0 / math.sqrt(head_width)
    seq_total = balance.shape[0]
    block_len = min(512, seq_total)
    block_count = seq_total // block_len
    docs_all = document_of(balance, doc_lengths)
    my_first = lax.axis_index("ctx") * tok_rows
    my_pos = lax.dynamic_slice_in_dim(balance, my_first, tok_rows)
    my_doc = lax.dynamic_slice_in_dim(docs_all, my_first, tok_rows)
    all_keys, all_values = (
        lax.all_gather(key_rows, "ctx", axis=0, tiled=True),
        lax.all_gather(value_rows, "ctx", axis=0, tiled=True),
    )

    def key_block(row_start):
        key_pos = lax.dynamic_slice_in_dim(balance, row_start, block_len)
        key_doc = lax.dynamic_slice_in_dim(docs_all, row_start, block_len)
        visible_pairs = (key_doc[None, :] == my_doc[:, None]) & (
            key_pos[None, :] <= my_pos[:, None]
        )
        key_blk = lax.dynamic_slice_in_dim(all_keys, row_start, block_len)
        value_blk = lax.dynamic_slice_in_dim(all_values, row_start, block_len)
        return (key_blk, value_blk, visible_pairs)

    def forward_step(step_index, state_now):
        key_blk, value_blk, visible_pairs = key_block(step_index * block_len)
        allowed = visible_pairs[:, None, :]
        running_max, weight_sum, weighted = state_now
        scores = (
            jnp.einsum("qhd,kd->qhk", queries, key_blk, preferred_element_type=jnp.float32)
            * scaling
        )
        scores = jnp.where(allowed, scores, NEGATIVE)
        new_max = jnp.maximum(running_max, jnp.max(scores, axis=2))
        raw_weights = jnp.where(allowed, jnp.exp(scores - new_max[:, :, None]), 0.0)
        factor = jnp.exp(running_max - new_max)
        weight_sum = weight_sum * factor + jnp.sum(raw_weights, axis=2)
        weighted = weighted * factor[:, :, None] + jnp.einsum(
            "qhk,kd->qhd",
            raw_weights.astype(jnp.bfloat16),
            value_blk,
            preferred_element_type=jnp.float32,
        )
        return (new_max, weight_sum, weighted)

    start_state = (
        jnp.full((tok_rows, heads_here), NEGATIVE, jnp.float32),
        jnp.zeros((tok_rows, heads_here), jnp.float32),
        jnp.zeros((tok_rows, heads_here, head_width), jnp.float32),
    )
    running_max, weight_sum, weighted = lax.fori_loop(0, block_count, forward_step, start_state)
    attended = (weighted / weight_sum[:, :, None]).astype(jnp.bfloat16)
    log_total = running_max + jnp.log(weight_sum)
    row_inner = jnp.sum(out_grad.astype(jnp.float32) * attended.astype(jnp.float32), axis=2)

    def backward_tile(query_part, grad_part, total_part, inner_part, key_blk, value_blk, allowed):
        scores = (
            jnp.einsum("qhd,kd->qhk", query_part, key_blk, preferred_element_type=jnp.float32)
            * scaling
        )
        weights = jnp.where(allowed, jnp.exp(scores - total_part[:, :, None]), 0.0)
        grad_weights = jnp.einsum(
            "qhd,kd->qhk", grad_part, value_blk, preferred_element_type=jnp.float32
        )
        grad_scores = (weights * (grad_weights - inner_part[:, :, None])).astype(jnp.bfloat16)
        return (weights.astype(jnp.bfloat16), grad_scores)

    def query_step(step_index, state_now):
        row_start = step_index * block_len
        key_blk, value_blk, visible_pairs = key_block(row_start)
        allowed = visible_pairs[:, None, :]
        grad_acc, key_terms = state_now
        weights_b, grad_scores = backward_tile(
            queries, out_grad, log_total, row_inner, key_blk, value_blk, allowed
        )
        grad_acc = grad_acc + jnp.einsum(
            "qhk,kd->qhd", grad_scores, key_blk, preferred_element_type=jnp.float32
        )
        key_part = (
            jnp.einsum("qhk,qhd->kd", grad_scores, queries, preferred_element_type=jnp.float32)
            * scaling
        )
        value_part = jnp.einsum(
            "qhk,qhd->kd", weights_b, out_grad, preferred_element_type=jnp.float32
        )
        key_terms = lax.dynamic_update_slice_in_dim(
            key_terms, jnp.concatenate([key_part, value_part], axis=1), row_start, 0
        )
        return (grad_acc, key_terms)

    grad_start = (
        jnp.zeros((tok_rows, heads_here, head_width), jnp.float32),
        jnp.zeros((seq_total, 2 * head_width), jnp.float32),
    )
    grad_acc, key_terms = lax.fori_loop(0, block_count, query_step, grad_start)
    query_grad = (grad_acc * scaling).astype(jnp.bfloat16)
    shared = lax.psum_scatter(key_terms, "ctx", scatter_dimension=0, tiled=True)
    combined = lax.psum(shared, "head")
    key_grad = combined[:, :head_width].astype(jnp.bfloat16)
    value_grad = combined[:, head_width:].astype(jnp.bfloat16)
    return (attended, query_grad, key_grad, value_grad)


def solution(mesh):
    return jax.shard_map(
        body,
        mesh=mesh,
        in_specs=(
            P(("seq", "ctx"), "head", None),
            P(("seq", "ctx"), None),
            P(("seq", "ctx"), None),
            P(("seq", "ctx"), "head", None),
            P("seq"),
            P("seq"),
        ),
        out_specs=(
            P(("seq", "ctx"), "head", None),
            P(("seq", "ctx"), "head", None),
            P(("seq", "ctx"), None),
            P(("seq", "ctx"), None),
        ),
        check_vma=False,
    )
```

profile of v0, /device:TPU:2, one launch (start us, length us, event | category | flops | bytes accessed | tf_op | source)
XLA Modules:
  0.0 1131.8 jit_solution(8781327198950465208)
XLA Ops:
  14.3 297.5 %all-gather.3.cloned.1.call-done = bf16[8192,128]{1,0:T(8,128)(2,1)} async-done(((bf16[128,128]{1,0:T(8,128)(2,1)}), bf16[8192,128]{1,0:T(8,128)(2,1)}) %all-gather.3.cloned.1.call-update) | async-done | bytes 2097168 | tf_op jit(solution)/shard_map/all_gather | solution.py:29
  311.8 299.0 %all-gather.5.cloned.1.call-done = bf16[8192,128]{1,0:T(8,128)(2,1)} async-done(((bf16[128,128]{1,0:T(8,128)(2,1)}), bf16[8192,128]{1,0:T(8,128)(2,1)}) %all-gather.5.cloned.1.call-update) | async-done | bytes 2097168 | tf_op jit(solution)/shard_map/all_gather | solution.py:30
  610.9 62.5 %while.34 = (s32[]{:T(128)}, f32[128,4]{0,1:T(4,128)S(1)}, f32[128,4]{0,1:T(4,128)S(1)}, f32[128,4,128]{2,0,1:T(8,128)S(1)}, s32[8192]{0:T(1024)S(1)}, /*index=5...) while((s32[]{:T(128)}, f32[128,4]{0,1:T(4,128)S(1)}, ...), condition=%wide.region_5.6_spmd.clone, body=%wide.region_2.5_spmd.clone.sunk | while | flops 136972800 | bytes 4371679 | solution.py:69
  613.4 1.3 convolution_add_fusion.4
  617.3 1.3 convolution_add_fusion.4
  621.2 1.3 convolution_add_fusion.4
  625.1 1.4 convolution_add_fusion.4
  629.0 1.3 convolution_add_fusion.4
  632.9 1.4 convolution_add_fusion.4
  636.8 1.3 convolution_add_fusion.4
  640.7 1.4 convolution_add_fusion.4
  644.6 1.3 convolution_add_fusion.4
  648.5 1.4 convolution_add_fusion.4
  652.4 1.3 convolution_add_fusion.4
  656.3 1.4 convolution_add_fusion.4
  660.2 1.3 convolution_add_fusion.4
  664.1 1.4 convolution_add_fusion.4
  668.0 1.3 convolution_add_fusion.4
  671.9 1.4 convolution_add_fusion.4
  674.4 3.8 broadcast_in_dim.114.clone
  678.2 104.2 %while.35 = (s32[]{:T(128)}, f32[128,4,128]{2,0,1:T(8,128)S(1)}, f32[8192,256]{1,0:T(8,128)}, s32[8192]{0:T(1024)S(1)}, s32[128]{0:T(128)S(1)}, /*index=5*/s32[8...) while((s32[]{:T(128)}, f32[128,4,128]{2,0,1:T(8,128)S(1)}, ...), condition=%wide.region_8.9_spmd.clone, body=%wide.region_7.8_spmd.clone.sunk | while | flops 337903616 | bytes 9979125 | solution.py:113
  682.0 1.3 convolution_add_fusion.5
  688.5 1.3 convolution_add_fusion.5
  695.0 1.3 convolution_add_fusion.5
  701.6 1.3 convolution_add_fusion.5
  708.1 1.3 convolution_add_fusion.5
  714.6 1.3 convolution_add_fusion.5
  721.1 1.3 convolution_add_fusion.5
  727.6 1.3 convolution_add_fusion.5
  740.6 1.3 convolution_add_fusion.5
  783.3 328.7 %reduce-scatter.2.cloned.1.call-done = f32[128,256]{1,0:T(8,128)} async-done(((f32[8192,256]{1,0:T(8,128)}), f32[128,256]{1,0:T(8,128)}) %reduce-scatter.2.cloned.1.call-update) | async-done | bytes 131088 | tf_op jit(solution)/shard_map/reduce_scatter | solution.py:115
  1112.0 12.7 %all-reduce.1 = bf16[128,256]{1,0:T(8,128)(2,1)S(1)} all-reduce(f32[128,256]{1,0:T(8,128)} %reduce-scatter.2.cloned.1.call-done), channel_id=1, replica_groups=mesh['seq'=2,'ctx'=64,'head'=2] {'head'}, use_global_device_ids=true, to_apply=%region_10.11 | all-reduce | flops 32768 | bytes 196608 | tf_op jit(solution)/shard_map/psum | solution.py:116
  (320 shorter events, 141.3 us)
Async XLA Ops:
  7.2 304.7 %all-gather.3.cloned.1.call-start = ((), (), s32[]{:S(2)}) async-start(), calls=%async_computation.1 | async-start | bytes 2129920 | tf_op jit(solution)/shard_map/all_gather | solution.py:29
  7.9 603.0 %all-gather.5.cloned.1.call-start = ((), (), s32[]{:S(2)}) async-start(), calls=%async_computation.2 | async-start | bytes 2129920 | tf_op jit(solution)/shard_map/all_gather | solution.py:30
  8.6 1103.4 %reduce-scatter.2.cloned.1.call-start = ((), (), s32[]{:S(2)}) async-start(), calls=%async_computation.3 | async-start | bytes 8519680 | tf_op jit(solution)/shard_map/reduce_scatter | solution.py:115
  610.9 62.6 %copy-start = (bf16[128,4,128]{2,1,0:T(4,128)(2,1)S(1)}, bf16[128,4,128]{2,1,0:T(4,128)(2,1)}, u32[]{:S(2)}) copy-start(bf16[128,4,128]{2,1,0:T(4,128)(2,1)} %param.13) | copy-start | bytes 393220
Sparse Core Ops, SparseCore 0:
  9.8 301.9 all-gather.2
  313.6 297.2 all-gather.4
  782.6 329.3 reduce-scatter.1
where the time goes:
time: 1130 us
  waiting for transfers between devices  927 us (82%)
  matrix products  110 us (10%)
  local copies, waits for them, and re-layouts  51.9 us (5%)
  other arithmetic  14.3 us (1%)
  between operations  13.8 us (1%)
  blocking collectives  12.7 us (1%)
    reduce_scatter x1, waiting for transfers between devices, body(): shared = lax.psum_scatter(key_terms, 'ctx', scatter_dimension=0, tiled=True)  329 us
    all_gather x1, waiting for transfers between devices, body(): lax.all_gather(value_rows, 'ctx', axis=0, tiled=True)  299 us
    all_gather x1, waiting for transfers between devices, body(): lax.all_gather(key_rows, 'ctx', axis=0, tiled=True)  297 us
    dynamic_slice x32, local copies, waits for them, and re-layouts, key_block(): key_pos = lax.dynamic_slice_in_dim(balance, row_start, block_len)  24.4 us
  transfers between devices with their start and end apart: 3, of which 3 were waited for; matrix products, arithmetic and copies ran while one was open for 1% of the time, Pallas kernels for 0%

commit v1 on v0

v1 whole, which is shorter than its diff:
```python
import math

import jax
import jax.numpy as jnp
from jax import lax
from jax.experimental import pallas as pl
from jax.experimental.pallas import tpu as pltpu
from jax.sharding import PartitionSpec as P

NX, NY, NZ = 4, 4, 8
XLO = 2
RUN = 64
DH = 128
HEADS_HERE = 4
ROWS = RUN * HEADS_HERE
BLK = 2 * RUN
KRUNS = XLO * NZ * 2
QRUNS = NY * 2
TILE = 4
SPANS = 128
DOCS = 8
NEGATIVE = -1e30
FLOOR = -1e29
FAR = 1 << 20
SCALING = 1.0 / math.sqrt(DH)
LOG2E = 1.0 / math.log(2.0)
MESH = pl.DeviceIdType.MESH
F32 = jnp.float32
BF16 = jnp.bfloat16


def here():
    c = lax.axis_index("ctx")
    h = lax.axis_index("head")
    return h, c // (NY * NZ), (c // NZ) % NY, c % NZ


def device(x, y, z):
    return {"ctx": ((x % XLO) * NY + y) * NZ + z, "head": x // XLO}


def meet(targets):
    barrier = pltpu.get_barrier_semaphore()
    for target in targets:
        pl.semaphore_signal(barrier, inc=1, device_id=target, device_id_type=MESH)
    pl.semaphore_wait(barrier, len(targets))


def remote(src, dst, send, recv, target):
    return pltpu.make_async_remote_copy(
        src_ref=src, dst_ref=dst, send_sem=send, recv_sem=recv, device_id=target, device_id_type=MESH
    )


def gather_kernel(q_ref, g_ref, k_ref, v_ref, qg, kg, lsem, ysend, yrecv, zsend, zrecv, xsend, xrecv):
    h, xl, y, z = here()
    x = h * XLO + xl
    first = xl * NZ
    y_up, y_dn = device(x, (y + 1) % NY, z), device(x, (y + NY - 1) % NY, z)
    z_up, z_dn = device(x, y, (z + 1) % NZ), device(x, y, (z + NZ - 1) % NZ)
    x_up, x_dn = device((x + 1) % NX, y, z), device((x + NX - 1) % NX, y, z)
    meet([y_up, y_dn, z_up, z_dn, x_up, x_dn])
    kv = (k_ref, v_ref)
    started = []

    def go(copy):
        copy.start()
        started.append(copy)
        return copy

    def z_send(way, step, part):
        block = (z - (step - 1) + NZ) % NZ if way == 0 else (z + step - 1) % NZ
        dst = kg.at[first + block, part]
        src = kv[part] if step == 1 else dst
        return go(remote(src, dst, zsend.at[way, step - 1, part], zrecv.at[way, step - 1, part], z_up if way == 0 else z_dn))

    def x_send(slot, block, src):
        dst = kg.at[first + block, h]
        for side, target in ((0, x_up), (1, x_dn)):
            sent_x.append(go(remote(src, dst, xsend.at[side, slot], xrecv.at[side, slot], target)))

    sent_x = []
    sent_z = {}
    for part in (0, 1):
        for way in (0, 1):
            sent_z[way, 1, part] = z_send(way, 1, part)
    locals_kv = []
    for part in (0, 1):
        copy = pltpu.make_async_copy(kv[part], kg.at[first + z, part], lsem.at[part])
        copy.start()
        locals_kv.append(copy)
    y_q_up = go(remote(q_ref, qg.at[y, 0], ysend.at[0], yrecv.at[0], y_up))
    y_g_dn = go(remote(g_ref, qg.at[y, 1], ysend.at[2], yrecv.at[2], y_dn))
    y_g_up = go(remote(g_ref, qg.at[y, 1], ysend.at[1], yrecv.at[1], y_up))
    y_q_dn = go(remote(q_ref, qg.at[y, 0], ysend.at[3], yrecv.at[3], y_dn))
    locals_q = []
    for part, ref in ((0, q_ref), (1, g_ref)):
        copy = pltpu.make_async_copy(ref, qg.at[y, part], lsem.at[2 + part])
        copy.start()
        locals_q.append(copy)
    for copy in locals_kv:
        copy.wait()
    x_send(0, z, kg.at[first + z, h])
    for step in (1, 2, 3):
        for part in (0, 1):
            for way in (0, 1):
                sent_z[way, step, part].wait_recv()
                if step < 3 or part == way:
                    sent_z[way, step + 1, part] = z_send(way, step + 1, part)
        for way in (0, 1):
            block = (z - step + NZ) % NZ if way == 0 else (z + step) % NZ
            x_send(2 * step - 1 + way, block, kg.at[first + block, h])
        if step == 2:
            y_q_up.wait_recv()
            q_on = qg.at[(y + NY - 1) % NY, 0]
            y_fwd_up = go(remote(q_on, q_on, ysend.at[4], yrecv.at[4], y_up))
            y_g_dn.wait_recv()
            g_on = qg.at[(y + 1) % NY, 1]
            y_fwd_dn = go(remote(g_on, g_on, ysend.at[5], yrecv.at[5], y_dn))
    sent_z[0, 4, 0].wait_recv()
    sent_z[1, 4, 1].wait_recv()
    block = (z + NZ // 2) % NZ
    x_send(7, block, kg.at[first + block, h])
    for copy in (y_g_up, y_q_dn, y_fwd_up, y_fwd_dn):
        copy.wait_recv()
    for copy in sent_x:
        copy.wait_recv()
    for copy in started:
        copy.wait_send()
    for copy in locals_q:
        copy.wait()


def gather(q, g, k, v):
    any_spec = pl.BlockSpec(memory_space=pl.ANY)
    dma = pltpu.SemaphoreType.DMA
    return pl.pallas_call(
        gather_kernel,
        out_shape=(
            jax.ShapeDtypeStruct((NY, 2, 2 * ROWS, DH), BF16),
            jax.ShapeDtypeStruct((XLO * NZ, 2, BLK, DH), BF16),
        ),
        in_specs=[any_spec] * 4,
        out_specs=(any_spec, any_spec),
        scratch_shapes=[dma((4,)), dma((6,)), dma((6,)), dma((2, 4, 2)), dma((2, 4, 2)), dma((2, 8)), dma((2, 8))],
        compiler_params=pltpu.CompilerParams(collective_id=0, has_side_effects=True),
        name="gather_rows",
    )(q, g, k, v)


def order_keys(spans, y, table, order, place, counts):
    def clear(p, _):
        table[p] = -1
        return 0

    lax.fori_loop(0, SPANS, clear, 0, unroll=8)
    for i in range(KRUNS):
        block, half = i // 2, i % 2
        table[spans[(((block // NZ) * NY + y) * NZ + block % NZ) * 2 + half]] = i

    def walk(p, n):
        counts[p] = n
        order[n] = table[p]
        place[n] = p * RUN
        return n + jnp.where(table[p] >= 0, 1, 0)

    lax.fori_loop(0, SPANS, walk, 0, unroll=8)
    counts[SPANS] = KRUNS
    for i in range(TILE):
        place[KRUNS + i] = FAR


def sort_keys(kg, order, ks, vs):
    def move(i, _):
        run = order[i]
        dst = pl.ds(pl.multiple_of(i * RUN, RUN), RUN)
        src = pl.ds(pl.multiple_of((run % 2) * RUN, RUN), RUN)
        ks[dst, :] = kg[run // 2, 0, src, :]
        vs[dst, :] = kg[run // 2, 1, src, :]
        return 0

    lax.fori_loop(0, KRUNS, move, 0)
    tail = pl.ds(KRUNS * RUN, TILE * RUN)
    ks[tail, :] = jnp.zeros((TILE * RUN, DH), BF16)
    vs[tail, :] = jnp.zeros((TILE * RUN, DH), BF16)


def query_rows(q_run, spans, lengths, counts, xl, z):
    span = spans[((xl * NY + q_run // 2) * NZ + z) * 2 + q_run % 2]
    low = span * RUN
    pos = low + lax.broadcasted_iota(jnp.int32, (1, ROWS), 1) // HEADS_HERE
    start = jnp.zeros((1, ROWS), jnp.int32)
    first = 0
    end = 0
    for d in range(DOCS):
        end = end + lengths[d]
        first = jnp.where(end <= low, end, first)
        start = jnp.where(pos >= end, end, start)
    low_run = counts[first // RUN]
    high_run = counts[span + 1]
    return pos, start, low_run, (high_run - low_run + TILE - 1) // TILE


def masked_scores(ks, q, row, run, place, pos, start):
    scores = lax.dot_general(ks[pl.ds(row, TILE * RUN), :], q, (((1,), (1,)), ((), ())), preferred_element_type=F32)
    offset = lax.broadcasted_iota(jnp.int32, (RUN, ROWS), 0)
    parts = []
    for u in range(TILE):
        base = place[run + u]
        seen = (offset <= pos - base) & (offset >= start - base)
        parts.append(jnp.where(seen, scores[u * RUN : (u + 1) * RUN] * (SCALING * LOG2E), NEGATIVE))
    return jnp.concatenate(parts, axis=0)


def forward_kernel(spans, lengths, qg, kg, stats, out, table, order, place, counts, ks, vs, held):
    h, xl, y, z = here()
    order_keys(spans, y, table, order, place, counts)
    sort_keys(kg, order, ks, vs)

    def one_run(q_run, _):
        pos, start, low_run, tiles = query_rows(q_run, spans, lengths, counts, xl, z)
        rows = pl.ds(pl.multiple_of((q_run % 2) * ROWS, ROWS), ROWS)
        q = qg[q_run // 2, 0, rows, :]
        g = qg[q_run // 2, 1, rows, :]

        def score(t, top):
            run = low_run + t * TILE
            row = pl.multiple_of(run * RUN, RUN)
            s = masked_scores(ks, q, row, run, place, pos, start)
            held[t] = s
            return jnp.maximum(top, jnp.max(s, axis=0, keepdims=True))

        top = lax.fori_loop(0, tiles, score, jnp.full((1, ROWS), FLOOR, F32))

        def weigh(t, state):
            total, inner, acc = state
            row = pl.multiple_of((low_run + t * TILE) * RUN, RUN)
            v = vs[pl.ds(row, TILE * RUN), :]
            raw = jnp.exp2(held[t] - top)
            gw = lax.dot_general(v, g, (((1,), (1,)), ((), ())), preferred_element_type=F32)
            total = total + jnp.sum(raw, axis=0, keepdims=True)
            inner = inner + jnp.sum(raw * gw, axis=0, keepdims=True)
            acc = acc + lax.dot_general(v, raw.astype(BF16), (((0,), (0,)), ((), ())), preferred_element_type=F32)
            return total, inner, acc

        zero = jnp.zeros((1, ROWS), F32)
        total, inner, acc = lax.fori_loop(0, tiles, weigh, (zero, zero, jnp.zeros((DH, ROWS), F32)))
        stats[q_run] = jnp.concatenate([top, total, inner, jnp.zeros((5, ROWS), F32)], axis=0)
        out[q_run] = acc
        return 0

    lax.fori_loop(0, QRUNS, one_run, 0)


SMEM_SCRATCH = [
    pltpu.SMEM((SPANS,), jnp.int32),
    pltpu.SMEM((KRUNS + TILE,), jnp.int32),
    pltpu.SMEM((KRUNS + TILE,), jnp.int32),
    pltpu.SMEM((SPANS + 1,), jnp.int32),
]
SORTED = (KRUNS + TILE) * RUN


def forward(spans, lengths, qg, kg):
    smem = pl.BlockSpec(memory_space=pltpu.SMEM)
    vmem = pl.BlockSpec(memory_space=pltpu.VMEM)
    return pl.pallas_call(
        forward_kernel,
        out_shape=(
            jax.ShapeDtypeStruct((QRUNS, 8, ROWS), F32),
            jax.ShapeDtypeStruct((QRUNS, DH, ROWS), F32),
        ),
        in_specs=[smem, smem, vmem, vmem],
        out_specs=(vmem, vmem),
        scratch_shapes=SMEM_SCRATCH
        + [
            pltpu.VMEM((SORTED, DH), BF16),
            pltpu.VMEM((SORTED, DH), BF16),
            pltpu.VMEM((KRUNS // TILE, TILE * RUN, ROWS), F32),
        ],
        compiler_params=pltpu.CompilerParams(vmem_limit_bytes=40 << 20),
        name="forward_stats",
    )(spans, lengths, qg, kg)


def exchange_kernel(mine, out, lsem, send, recv):
    h, xl, y, z = here()
    x = h * XLO + xl
    targets = [device(x, (y + d) % NY, z) for d in range(1, NY)]
    meet(targets)
    copies = []
    for d, target in enumerate(targets):
        copy = remote(mine, out.at[y], send.at[d], recv.at[d], target)
        copy.start()
        copies.append(copy)
    own = pltpu.make_async_copy(mine, out.at[y], lsem)
    own.start()
    own.wait()
    for copy in copies:
        copy.wait()


def exchange(stats):
    vmem = pl.BlockSpec(memory_space=pltpu.VMEM)
    dma = pltpu.SemaphoreType.DMA
    return pl.pallas_call(
        exchange_kernel,
        out_shape=jax.ShapeDtypeStruct((NY,) + stats.shape, F32),
        in_specs=[vmem],
        out_specs=vmem,
        scratch_shapes=[dma, dma((NY - 1,)), dma((NY - 1,))],
        compiler_params=pltpu.CompilerParams(collective_id=1, has_side_effects=True),
        name="exchange_stats",
    )(stats)


def backward_kernel(
    spans, lengths, qg, kg, stats, acc_out, rows_out, keys_out, table, order, place, counts, ks, vs, key_acc, value_acc
):
    h, xl, y, z = here()
    order_keys(spans, y, table, order, place, counts)
    sort_keys(kg, order, ks, vs)
    key_acc[...] = jnp.zeros_like(key_acc)
    value_acc[...] = jnp.zeros_like(value_acc)

    def one_run(q_run, _):
        pos, start, low_run, tiles = query_rows(q_run, spans, lengths, counts, xl, z)
        rows = pl.ds(pl.multiple_of((q_run % 2) * ROWS, ROWS), ROWS)
        q = qg[q_run // 2, 0, rows, :]
        g = qg[q_run // 2, 1, rows, :]
        each = [stats[i, q_run] for i in range(NY)]
        tops = [e[0:1] for e in each]
        top = jnp.maximum(jnp.maximum(tops[0], tops[1]), jnp.maximum(tops[2], tops[3]))
        shares = [jnp.exp2(t - top) for t in tops]
        total = sum(e[1:2] * s for e, s in zip(each, shares))
        inner = sum(e[2:3] * s for e, s in zip(each, shares)) / total
        log_total = top + jnp.log(total) * LOG2E
        own_top = stats[y, q_run][0:1]

        def tile(t, grad):
            run = low_run + t * TILE
            row = pl.multiple_of(run * RUN, RUN)
            here_rows = pl.ds(row, TILE * RUN)
            s = masked_scores(ks, q, row, run, place, pos, start)
            weights = jnp.exp2(s - log_total)
            gw = lax.dot_general(vs[here_rows, :], g, (((1,), (1,)), ((), ())), preferred_element_type=F32)
            gs = (weights * (gw - inner)).astype(BF16)
            value_acc[here_rows, :] += jnp.dot(weights.astype(BF16), g, preferred_element_type=F32)
            key_acc[here_rows, :] += jnp.dot(gs, q, preferred_element_type=F32)
            return grad + lax.dot_general(ks[here_rows, :], gs, (((0,), (0,)), ((), ())), preferred_element_type=F32)

        grad = lax.fori_loop(0, tiles, tile, jnp.zeros((DH, ROWS), F32))
        attended = acc_out[q_run] * jnp.exp2(own_top - log_total)
        rows_out[q_run // 2, 0, rows, :] = attended.T.astype(BF16)
        rows_out[q_run // 2, 1, rows, :] = (grad * SCALING).T.astype(BF16)
        return 0

    lax.fori_loop(0, QRUNS, one_run, 0)

    def put(i, _):
        run = order[i]
        src = pl.ds(pl.multiple_of(i * RUN, RUN), RUN)
        dst = pl.ds(pl.multiple_of((run % 2) * RUN, RUN), RUN)
        keys_out[run // 2, 0, dst, :] = (key_acc[src, :] * SCALING).astype(BF16)
        keys_out[run // 2, 1, dst, :] = value_acc[src, :].astype(BF16)
        return 0

    lax.fori_loop(0, KRUNS, put, 0)


def backward(spans, lengths, qg, kg, stats, acc):
    smem = pl.BlockSpec(memory_space=pltpu.SMEM)
    vmem = pl.BlockSpec(memory_space=pltpu.VMEM)
    return pl.pallas_call(
        backward_kernel,
        out_shape=(
            jax.ShapeDtypeStruct((NY, 2, 2 * ROWS, DH), BF16),
            jax.ShapeDtypeStruct((XLO * NZ, 2, BLK, DH), BF16),
        ),
        in_specs=[smem, smem, vmem, vmem, vmem, vmem],
        out_specs=(vmem, vmem),
        scratch_shapes=SMEM_SCRATCH
        + [
            pltpu.VMEM((SORTED, DH), BF16),
            pltpu.VMEM((SORTED, DH), BF16),
            pltpu.VMEM((SORTED, DH), F32),
            pltpu.VMEM((SORTED, DH), F32),
        ],
        compiler_params=pltpu.CompilerParams(vmem_limit_bytes=40 << 20),
        name="backward_terms",
    )(spans, lengths, qg, kg, stats, acc)


def reduce_kernel(
    rows, keys, att, qgrad, kgrad, vgrad,
    ybuf, ysum, xbuf, xsum, zbuf, zown, zsum, last, ysend, yrecv, xsend, xrecv, zsend, zrecv, hsend, hrecv,
):
    h, xl, y, z = here()
    x = h * XLO + xl
    half = NZ // 2
    y_up, y_dn = device(x, (y + 1) % NY, z), device(x, (y + NY - 1) % NY, z)
    x_up, x_dn, x_far = (device((x + d) % NX, y, z) for d in (1, NX - 1, 2))
    z_all = [device(x, y, (z + d) % NZ) for d in range(1, NZ)]
    meet([y_up, y_dn, x_up, x_dn, x_far] + z_all)
    started = []

    def go(copy):
        copy.start()
        started.append(copy)
        return copy

    def piece(ring):
        return (ring % XLO) * NZ, ring // XLO

    up, dn, far = (x + 1) % NX, (x + NX - 1) % NX, (x + 2) % NX
    far_first, far_part = piece(far)
    up_first, up_part = piece(up)
    dn_first, dn_part = piece(dn)
    my_first, my_part = piece(x)
    lo, hi = pl.ds(0, half), pl.ds(half, half)
    x_a = go(remote(keys.at[pl.ds(far_first, half), far_part], xbuf.at[0], xsend.at[0], xrecv.at[0], x_up))
    x_b = go(remote(keys.at[pl.ds(far_first + half, half), far_part], xbuf.at[1], xsend.at[1], xrecv.at[1], x_dn))
    y_far = (y + 2) % NY
    y_a = go(remote(rows.at[y_far, 0], ybuf.at[0], ysend.at[0], yrecv.at[0], y_up))
    y_b = go(remote(rows.at[y_far, 1], ybuf.at[1], ysend.at[1], yrecv.at[1], y_dn))
    x_c = go(remote(keys.at[pl.ds(up_first + half, half), up_part], xbuf.at[2], xsend.at[2], xrecv.at[2], x_up))
    x_d = go(remote(keys.at[pl.ds(dn_first, half), dn_part], xbuf.at[3], xsend.at[3], xrecv.at[3], x_dn))
    y_c = go(remote(rows.at[(y + 1) % NY, 1], ybuf.at[2], ysend.at[2], yrecv.at[2], y_up))
    y_d = go(remote(rows.at[(y + NY - 1) % NY, 0], ybuf.at[3], ysend.at[3], yrecv.at[3], y_dn))
    x_a.wait_recv()
    xsum[0] = (xbuf[0].astype(F32) + keys[pl.ds(up_first, half), up_part].astype(F32)).astype(BF16)
    x_e = go(remote(xsum.at[0], xbuf.at[4], xsend.at[4], xrecv.at[4], x_up))
    x_b.wait_recv()
    xsum[1] = (xbuf[1].astype(F32) + keys[pl.ds(dn_first + half, half), dn_part].astype(F32)).astype(BF16)
    x_f = go(remote(xsum.at[1], xbuf.at[5], xsend.at[5], xrecv.at[5], x_dn))
    y_a.wait_recv()
    ysum[0] = (ybuf[0].astype(F32) + rows[(y + 1) % NY, 0].astype(F32)).astype(BF16)
    y_e = go(remote(ysum.at[0], ybuf.at[4], ysend.at[4], yrecv.at[4], y_up))
    y_b.wait_recv()
    ysum[1] = (ybuf[1].astype(F32) + rows[(y + NY - 1) % NY, 1].astype(F32)).astype(BF16)
    y_f = go(remote(ysum.at[1], ybuf.at[5], ysend.at[5], yrecv.at[5], y_dn))
    x_d.wait_recv()
    x_e.wait_recv()
    zown[lo] = keys[pl.ds(my_first, half), my_part].astype(F32) + xbuf[3].astype(F32) + xbuf[4].astype(F32)
    x_c.wait_recv()
    x_f.wait_recv()
    zown[hi] = keys[pl.ds(my_first + half, half), my_part].astype(F32) + xbuf[2].astype(F32) + xbuf[5].astype(F32)
    zsum[...] = zown[...].astype(BF16)
    z_copies = []
    for d in (4, 3, 5, 2, 6, 1, 7):
        block = (z + d) % NZ
        z_copies.append(
            go(remote(zsum.at[block], zbuf.at[d - 1], zsend.at[d - 1], zrecv.at[d - 1], z_all[d - 1]))
        )
    y_d.wait_recv()
    y_e.wait_recv()
    att[...] = (rows[y, 0].astype(F32) + ybuf[3].astype(F32) + ybuf[4].astype(F32)).astype(BF16)
    y_c.wait_recv()
    y_f.wait_recv()
    qgrad[...] = (rows[y, 1].astype(F32) + ybuf[2].astype(F32) + ybuf[5].astype(F32)).astype(BF16)
    total = zown[z]
    for copy in z_copies:
        copy.wait_recv()
    for d in range(NZ - 1):
        total = total + zbuf[d].astype(F32)
    last[0] = total.astype(BF16)
    final = go(remote(last.at[0], last.at[1], hsend, hrecv, x_far))
    final.wait_recv()
    mine, other = last[0], last[1]
    kgrad[...] = jnp.where(h == 0, mine, other)
    vgrad[...] = jnp.where(h == 0, other, mine)
    for copy in started:
        copy.wait_send()


def reduce(rows, keys):
    vmem = pl.BlockSpec(memory_space=pltpu.VMEM)
    dma = pltpu.SemaphoreType.DMA
    half = NZ // 2
    return pl.pallas_call(
        reduce_kernel,
        out_shape=(
            jax.ShapeDtypeStruct((2 * ROWS, DH), BF16),
            jax.ShapeDtypeStruct((2 * ROWS, DH), BF16),
            jax.ShapeDtypeStruct((BLK, DH), BF16),
            jax.ShapeDtypeStruct((BLK, DH), BF16),
        ),
        in_specs=[vmem, vmem],
        out_specs=(vmem,) * 4,
        scratch_shapes=[
            pltpu.VMEM((6, 2 * ROWS, DH), BF16),
            pltpu.VMEM((2, 2 * ROWS, DH), BF16),
            pltpu.VMEM((6, half, BLK, DH), BF16),
            pltpu.VMEM((2, half, BLK, DH), BF16),
            pltpu.VMEM((NZ - 1, BLK, DH), BF16),
            pltpu.VMEM((NZ, BLK, DH), F32),
            pltpu.VMEM((NZ, BLK, DH), BF16),
            pltpu.VMEM((2, BLK, DH), BF16),
            dma((6,)), dma((6,)), dma((6,)), dma((6,)), dma((NZ - 1,)), dma((NZ - 1,)), dma, dma,
        ],
        compiler_params=pltpu.CompilerParams(collective_id=2, has_side_effects=True, vmem_limit_bytes=40 << 20),
        name="reduce_terms",
    )(rows, keys)


def body(queries, key_rows, value_rows, out_grad, doc_lengths, balance):
    flat = (2 * ROWS, DH)
    spans = balance.reshape(SPANS, RUN)[:, 0] // RUN
    qg, kg = gather(queries.reshape(flat), out_grad.reshape(flat), key_rows, value_rows)
    stats, acc = forward(spans, doc_lengths, qg, kg)
    stats = exchange(stats)
    rows, keys = backward(spans, doc_lengths, qg, kg, stats, acc)
    attended, query_grad, key_grad, value_grad = reduce(rows, keys)
    return attended.reshape(queries.shape), query_grad.reshape(queries.shape), key_grad, value_grad


def solution(mesh):
    return jax.shard_map(
        body,
        mesh=mesh,
        in_specs=(
            P(("seq", "ctx"), "head", None),
            P(("seq", "ctx"), None),
            P(("seq", "ctx"), None),
            P(("seq", "ctx"), "head", None),
            P("seq"),
            P("seq"),
        ),
        out_specs=(
            P(("seq", "ctx"), "head", None),
            P(("seq", "ctx"), "head", None),
            P(("seq", "ctx"), None),
            P(("seq", "ctx"), None),
        ),
        check_vma=False,
    )
```

time: 1130 us -> 83.5 us (0.07)
  waiting for transfers between devices: 927 us -> 0 us
  matrix products: 110 us -> 0 us
  Pallas kernels: 0 us -> 74.1 us
  local copies, waits for them, and re-layouts: 51.9 us -> 8.15 us
  other arithmetic: 14.3 us -> 0.01 us
  between operations: 13.8 us -> 0.73 us
  blocking collectives: 12.7 us -> 0 us
    all_gather x2 -> x0, waiting for transfers between devices: 597 us -> none  [the longest x1 299 us: body(): lax.all_gather(value_rows, 'ctx', axis=0, tiled=True)]
    reduce_scatter x1 -> x0, waiting for transfers between devices: 329 us -> none  [body(): shared = lax.psum_scatter(key_terms, 'ctx', scatter_dimension=0, tiled=True)]
    dot_general x112 -> x0, matrix products: 110 us -> none  [the longest x16 21.6 us: forward_step(): jnp.einsum('qhk,kd->qhd', raw_weights.astype(jnp.bfloat16), value_blk, pr...]
    pallas_call x0 -> x5, Pallas kernels: none -> 74.1 us  [the longest x1 26 us: gather(): pl.pallas_call(gather_kernel, out_shape=(jax.ShapeDtypeStruct((NY, 2, 2 *...]
    dynamic_slice x66 -> x0, local copies, waits for them, and re-layouts: 27.6 us -> none  [the longest x32 24.4 us: key_block(): key_pos = lax.dynamic_slice_in_dim(balance, row_start, block_len)]
    dynamic_update_slice x32 -> x0, local copies, waits for them, and re-layouts: 16.7 us -> none  [query_step(): lax.dynamic_update_slice_in_dim(key_terms, jnp.concatenate([key_part, val...]
    psum x1 -> x0, blocking collectives: 12.7 us -> none  [body(): combined = lax.psum(shared, 'head')]
  transfers between devices with their start and end apart: 3 -> 0, of which waited for: 3 -> 0; matrix products, arithmetic and copies ran while one was open for 1% -> 0% of each run, Pallas kernels for 0% -> 0%
where the time goes in v1:
time: 83.5 us; the launch traced here: 83 us
  Pallas kernels  74.1 us (89%)
  local copies, waits for them, and re-layouts  8.15 us (10%)
    pallas_call x1, Pallas kernels, gather(): pl.pallas_call(gather_kernel, out_shape=(jax.ShapeDtypeStruct((NY, 2, 2 *...  26 us
    pallas_call x1, Pallas kernels, reduce(): pl.pallas_call(reduce_kernel, out_shape=(jax.ShapeDtypeStruct((2 * ROWS,...  24.2 us
    pallas_call x1, Pallas kernels, exchange(): pl.pallas_call(exchange_kernel, out_shape=jax.ShapeDtypeStruct((NY,) + st...  8.73 us
    pallas_call x1, Pallas kernels, backward(): pl.pallas_call(backward_kernel, out_shape=(jax.ShapeDtypeStruct((NY, 2, 2...  8.26 us
    unnamed x18, local copies, waits for them, and re-layouts  7.21 us
    pallas_call x1, Pallas kernels, forward(): pl.pallas_call(forward_kernel, out_shape=(jax.ShapeDtypeStruct((QRUNS, 8,...  6.9 us

profile of v1, /device:TPU:2, one launch (start us, length us, event | category | flops | bytes accessed | tf_op | source)
XLA Modules:
  0.0 83.0 jit_solution(2162122162573274351)
XLA Ops:
  0.6 0.8 %reshape.23 = s32[128,64]{1,0:T(8,128)S(1)} reshape(s32[8192]{0:T(1024)} %param.11) | data formatting | bytes 65536 | tf_op jit(solution)/shard_map/reshape | solution.py:508
  1.5 0.1 slice_reduce_fusion
  1.6 26.0 %gather_rows.1 = (bf16[4,2,512,128]{3,2,1,0:T(8,128)(2,1)}, bf16[16,2,128,128]{3,2,1,0:T(8,128)(2,1)}) custom-call(bf16[512,128]{1,0:T(8,128)(2,1)} %bitcast.6, bf16[512,128]{1,0:T(8,128)(2,1)} %bitcast.7, bf16[128,128]{1,0:T(8,128)(2,1)} %k_ref.1, bf16[128,128]{1,0:T(8,128)(2,1)} %v_ref.1), custom_call_target="tpu_custom_call" | custom-call | tf_op jit(solution)/shard_map/gather_rows/pallas_call | solution.py:137
  27.6 0.0 copy-start.6
  27.7 0.6 copy-done.6
  28.3 0.0 copy-start
  28.3 1.2 %copy-done = bf16[4,2,512,128]{3,2,1,0:T(8,128)(2,1)S(1)} copy-done((bf16[4,2,512,128]{3,2,1,0:T(8,128)(2,1)S(1)}, bf16[4,2,512,128]{3,2,1,0:T(8,128)(2,1)}, u32[]{:S(2)}) %copy-start) | copy-done | bytes 1048600
  29.5 0.0 copy-start.2
  29.5 1.2 %copy-done.2 = bf16[16,2,128,128]{3,2,1,0:T(8,128)(2,1)S(1)} copy-done((bf16[16,2,128,128]{3,2,1,0:T(8,128)(2,1)S(1)}, bf16[16,2,128,128]{3,2,1,0:T(8,128)(2,1)}, u32[]{:S(2)}) %copy-start.2) | copy-done | bytes 1048600
  30.8 0.0 copy-start.1
  30.8 0.0 copy-start.3
  30.8 6.9 %forward_stats.1 = (f32[8,8,256]{2,1,0:T(8,128)S(1)}, f32[8,128,256]{2,1,0:T(8,128)S(1)}) custom-call(s32[128]{0:T(128)S(1)} %and_select_fusion.spans, s32[8]{0:T(128)S(1)} %copy-done.6, bf16[4,2,512,128]{3,2,1,0:T(8,128)(2,1)S(1)} %copy-done, bf16[16,2,128,128]{3,2,1,0:T(8,128)(2,1)S(1)} %copy-done.2), custom_call_target="tpu_custom_call" | custom-call | tf_op jit(solution)/shard_map/forward_stats/pallas_call | solution.py:267
  37.7 0.0 copy-start.5
  37.7 0.6 copy-done.5
  38.3 8.7 %exchange_stats.1.stats = f32[4,8,8,256]{3,2,1,0:T(8,128)} custom-call(f32[8,8,256]{2,1,0:T(8,128)} %copy-done.5), custom_call_target="tpu_custom_call" | custom-call | tf_op jit(solution)/shard_map/exchange_stats/pallas_call | solution.py:306
  47.0 0.0 copy-done.1
  47.0 0.0 copy-done.3
  47.1 0.0 copy-start.4
  47.1 0.9 %copy-done.4 = f32[4,8,8,256]{3,2,1,0:T(8,128)S(1)} copy-done((f32[4,8,8,256]{3,2,1,0:T(8,128)S(1)}, f32[4,8,8,256]{3,2,1,0:T(8,128)}, u32[]{:S(2)}) %copy-start.4) | copy-done | bytes 262168
  48.0 8.3 %backward_terms.1 = (bf16[4,2,512,128]{3,2,1,0:T(8,128)(2,1)S(1)}, bf16[16,2,128,128]{3,2,1,0:T(8,128)(2,1)S(1)}) custom-call(s32[128]{0:T(128)S(1)} %and_select_fusion.spans, s32[8]{0:T(128)S(1)} %copy-done.6, bf16[4,2,512,128]{3,2,1,0:T(8,128)(2,1)S(1)} %copy-done.1, bf16[16,2,128,128]{3,2,1,0:T(8,128)(2,1)S(1)} %copy-done.3, ...), custom_call_target="tpu_custom_call" | custom-call | tf_op jit(solution)/shard_map/backward_terms/pallas_call | solution.py:374
  56.3 24.2 %reduce_terms.1 = (bf16[512,128]{1,0:T(8,128)(2,1)S(1)}, bf16[512,128]{1,0:T(8,128)(2,1)S(1)}, bf16[128,128]{1,0:T(8,128)(2,1)S(1)}, bf16[128,128]{1,0:T(8,128)(2,1)S(1)}) custom-call(bf16[4,2,512,128]{3,2,1,0:T(8,128)(2,1)S(1)} %get-tuple-element.18.rows, bf16[16,2,128,128]{3,2,1,0:T(8,128)(2,1)S(1)} %get-tuple-element.19.keys), custom_call_target="tpu_custom_call" | custom-call | tf_op jit(solution)/shard_map/reduce_terms/pallas_call | solution.py:480
  80.5 0.7 copy.14
  81.1 0.7 copy.15
  81.8 0.6 copy.16
  82.4 0.6 copy.17
  (1 shorter events, 0.0 us)
Async XLA Ops:
  27.6 0.7 copy-start.6
  28.3 1.2 %copy-start = (bf16[4,2,512,128]{3,2,1,0:T(8,128)(2,1)S(1)}, bf16[4,2,512,128]{3,2,1,0:T(8,128)(2,1)}, u32[]{:S(2)}) copy-start(bf16[4,2,512,128]{3,2,1,0:T(8,128)(2,1)} %get-tuple-element.14.qg) | copy-start | bytes 3145732
  29.5 1.2 %copy-start.2 = (bf16[16,2,128,128]{3,2,1,0:T(8,128)(2,1)S(1)}, bf16[16,2,128,128]{3,2,1,0:T(8,128)(2,1)}, u32[]{:S(2)}) copy-start(bf16[16,2,128,128]{3,2,1,0:T(8,128)(2,1)} %get-tuple-element.15.kg) | copy-start | bytes 3145732
  30.8 16.3 %copy-start.1 = (bf16[4,2,512,128]{3,2,1,0:T(8,128)(2,1)S(1)}, bf16[4,2,512,128]{3,2,1,0:T(8,128)(2,1)}, u32[]{:S(2)}) copy-start(bf16[4,2,512,128]{3,2,1,0:T(8,128)(2,1)} %get-tuple-element.14.qg) | copy-start | bytes 3145732
  30.8 16.3 %copy-start.3 = (bf16[16,2,128,128]{3,2,1,0:T(8,128)(2,1)S(1)}, bf16[16,2,128,128]{3,2,1,0:T(8,128)(2,1)}, u32[]{:S(2)}) copy-start(bf16[16,2,128,128]{3,2,1,0:T(8,128)(2,1)} %get-tuple-element.15.kg) | copy-start | bytes 3145732
  37.7 0.6 copy-start.5
  47.1 1.0 %copy-start.4 = (f32[4,8,8,256]{3,2,1,0:T(8,128)S(1)}, f32[4,8,8,256]{3,2,1,0:T(8,128)}, u32[]{:S(2)}) copy-start(f32[4,8,8,256]{3,2,1,0:T(8,128)} %exchange_stats.1.stats) | copy-start | bytes 786436

commit v2 on v1

v2 whole, which is shorter than its diff:
```python
import math

import jax
import jax.numpy as jnp
from jax import lax
from jax.experimental import pallas as pl
from jax.experimental.pallas import tpu as pltpu
from jax.sharding import PartitionSpec as P

NX, NY, NZ = 4, 4, 8
XLO = 2
RUN = 64
DH = 128
HEADS_HERE = 4
ROWS = RUN * HEADS_HERE
BLK = 2 * RUN
KRUNS = XLO * NZ * 2
QRUNS = NY * 2
TILE = 4
SPANS = 128
QTAB = 40
DOCS = 8
NEGATIVE = -1e30
FLOOR = -1e29
FAR = 1 << 20
SCALING = 1.0 / math.sqrt(DH)
LOG2E = 1.0 / math.log(2.0)
MESH = pl.DeviceIdType.MESH
F32 = jnp.float32
BF16 = jnp.bfloat16


def here():
    c = lax.axis_index("ctx")
    h = lax.axis_index("head")
    return h, c // (NY * NZ), (c // NZ) % NY, c % NZ


def device(x, y, z):
    return {"ctx": ((x % XLO) * NY + y) * NZ + z, "head": x // XLO}


def meet(targets):
    barrier = pltpu.get_barrier_semaphore()
    for target in targets:
        pl.semaphore_signal(barrier, inc=1, device_id=target, device_id_type=MESH)
    pl.semaphore_wait(barrier, len(targets))


def remote(src, dst, send, recv, target):
    return pltpu.make_async_remote_copy(
        src_ref=src, dst_ref=dst, send_sem=send, recv_sem=recv, device_id=target, device_id_type=MESH
    )


def tables(bal, lengths, tab, row_tab, xl, y, z):
    lane = lax.broadcasted_iota(jnp.int32, (1, SPANS), 1)
    slabs = [bal[pl.ds(pl.multiple_of((i * NY + y) * NZ, NZ), NZ), :] for i in range(XLO)]
    held = [slab[:, half * RUN : half * RUN + 1] // RUN for half in (0, 1) for slab in slabs]
    held = jnp.concatenate(held, axis=0)
    index = lax.broadcasted_iota(jnp.int32, (KRUNS, 1), 0)
    match = held == lane
    has = jnp.sum(jnp.where(match, 1, 0), axis=0, keepdims=True)
    which = jnp.sum(jnp.where(match, index, 0), axis=0, keepdims=True)
    before = jnp.sum(jnp.where(held < lane, 1, 0), axis=0, keepdims=True)
    rank = jnp.where(has > 0, before, -1)
    pick = lax.broadcasted_iota(jnp.int32, (QTAB, 1), 0)
    hit = rank == pick
    place = jnp.sum(jnp.where(hit, lane * RUN, 0), axis=1, keepdims=True)
    order = jnp.sum(jnp.where(hit, which, 0), axis=1, keepdims=True)
    place = jnp.where(pick < KRUNS, place, FAR)
    tab[pl.ds(0, QTAB), :] = jnp.where(lane == 0, place, order)
    q_rows = [bal[pl.ds((xl * NY + i) * NZ + z, 1), :] for i in range(NY)]
    low = jnp.concatenate([r[:, half * RUN : half * RUN + 1] for r in q_rows for half in (0, 1)], axis=0)
    pos = low + lax.broadcasted_iota(jnp.int32, (QRUNS, ROWS), 1) // HEADS_HERE
    start = jnp.zeros((QRUNS, ROWS), jnp.int32)
    first = jnp.zeros((QRUNS, 1), jnp.int32)
    end = 0
    for d in range(DOCS):
        end = end + lengths[d]
        first = jnp.where(low >= end, end, first)
        start = jnp.where(pos >= end, end, start)
    row_tab[0] = pos
    row_tab[1] = start
    low_run = jnp.sum(jnp.where((lane < first // RUN) & (has > 0), 1, 0), axis=1, keepdims=True)
    high_run = jnp.sum(jnp.where((lane <= low // RUN) & (has > 0), 1, 0), axis=1, keepdims=True)
    tiles = (high_run - low_run + TILE - 1) // TILE
    tab[pl.ds(QTAB, QRUNS), :] = jnp.where(lane == 0, low_run, tiles)


def gather_kernel(
    q_ref, g_ref, k_ref, v_ref, bal_ref, len_ref, qg, kg, tab, row_tab, bal, lengths, lsem, ysend, yrecv, zsend, zrecv, xsend, xrecv
):
    h, xl, y, z = here()
    x = h * XLO + xl
    first = xl * NZ
    y_up, y_dn = device(x, (y + 1) % NY, z), device(x, (y + NY - 1) % NY, z)
    z_to = {d: device(x, y, (z + d + NZ) % NZ) for d in (1, 2, -1, -2)}
    x_up, x_dn = device((x + 1) % NX, y, z), device((x + NX - 1) % NX, y, z)
    meet([y_up, y_dn, x_up, x_dn] + list(z_to.values()))
    kv = (k_ref, v_ref)
    started = []

    def go(copy):
        copy.start()
        started.append(copy)
        return copy

    sent_z = {}

    def z_send(sign, hops, dist, part):
        block = (z - sign * (dist - hops) + NZ) % NZ
        dst = kg.at[first + block, part]
        src = kv[part] if dist == hops else dst
        way = 0 if sign > 0 else 1
        sems = zsend.at[way, dist - 1, part], zrecv.at[way, dist - 1, part]
        sent_z[sign, dist, part] = go(remote(src, dst, *sems, z_to[sign * hops]))

    sent_x = []

    def x_send(slot, block):
        dst = kg.at[first + block, h]
        for side, target in ((0, x_up), (1, x_dn)):
            sent_x.append(go(remote(dst, dst, xsend.at[side, slot], xrecv.at[side, slot], target)))

    def local(src, dst, slot):
        copy = pltpu.make_async_copy(src, dst, lsem.at[slot])
        copy.start()
        return copy

    own_tab = [local(bal_ref, bal, 4), local(len_ref, lengths, 5)]
    for part in (0, 1):
        for sign in (1, -1):
            z_send(sign, 2, 2, part)
    y_q_up = go(remote(q_ref, qg.at[y, 0], ysend.at[0], yrecv.at[0], y_up))
    y_g_dn = go(remote(g_ref, qg.at[y, 1], ysend.at[2], yrecv.at[2], y_dn))
    own_kv = [local(kv[part], kg.at[first + z, part], part) for part in (0, 1)]
    for part in (0, 1):
        for sign in (1, -1):
            z_send(sign, 1, 1, part)
    y_g_up = go(remote(g_ref, qg.at[y, 1], ysend.at[1], yrecv.at[1], y_up))
    y_q_dn = go(remote(q_ref, qg.at[y, 0], ysend.at[3], yrecv.at[3], y_dn))
    own_q = [local(ref, qg.at[y, part], 2 + part) for part, ref in ((0, q_ref), (1, g_ref))]
    for copy in own_kv:
        copy.wait()
    x_send(0, z)
    for copy in own_tab:
        copy.wait()
    tables(bal, lengths, tab, row_tab, xl, y, z)
    for part in (0, 1):
        for sign in (1, -1):
            sent_z[sign, 2, part].wait_recv()
            z_send(sign, 1, 3, part)
            if part == (0 if sign > 0 else 1):
                z_send(sign, 2, 4, part)
    x_send(1, (z - 2 + NZ) % NZ)
    x_send(2, (z + 2) % NZ)
    y_q_up.wait_recv()
    q_on = qg.at[(y + NY - 1) % NY, 0]
    y_fwd_up = go(remote(q_on, q_on, ysend.at[4], yrecv.at[4], y_up))
    y_g_dn.wait_recv()
    g_on = qg.at[(y + 1) % NY, 1]
    y_fwd_dn = go(remote(g_on, g_on, ysend.at[5], yrecv.at[5], y_dn))
    slot = 3
    for dist in (1, 3):
        for sign in (1, -1):
            for part in (0, 1):
                sent_z[sign, dist, part].wait_recv()
            x_send(slot, (z - sign * dist + NZ) % NZ)
            slot += 1
    sent_z[1, 4, 0].wait_recv()
    sent_z[-1, 4, 1].wait_recv()
    x_send(7, (z + NZ // 2) % NZ)
    for copy in (y_g_up, y_q_dn, y_fwd_up, y_fwd_dn):
        copy.wait_recv()
    for copy in sent_x:
        copy.wait_recv()
    for copy in started:
        copy.wait_send()
    for copy in own_q:
        copy.wait()


def gather(q, g, k, v, bal, lengths):
    hbm = pl.BlockSpec(memory_space=pltpu.HBM)
    vmem = pl.BlockSpec(memory_space=pltpu.VMEM)
    dma = pltpu.SemaphoreType.DMA
    return pl.pallas_call(
        gather_kernel,
        out_shape=(
            jax.ShapeDtypeStruct((NY, 2, 2 * ROWS, DH), BF16),
            jax.ShapeDtypeStruct((XLO * NZ, 2, BLK, DH), BF16),
            jax.ShapeDtypeStruct((QTAB + QRUNS, SPANS), jnp.int32),
            jax.ShapeDtypeStruct((2, QRUNS, ROWS), jnp.int32),
        ),
        in_specs=[hbm] * 6,
        out_specs=(vmem,) * 4,
        scratch_shapes=[
            pltpu.VMEM((SPANS // 2, BLK), jnp.int32),
            pltpu.SMEM((DOCS,), jnp.int32),
            dma((6,)), dma((6,)), dma((6,)), dma((2, 4, 2)), dma((2, 4, 2)), dma((2, 8)), dma((2, 8)),
        ],
        compiler_params=pltpu.CompilerParams(collective_id=0, has_side_effects=True, vmem_limit_bytes=8 << 20),
        name="gather_rows",
    )(*(pltpu.with_memory_space_constraint(a, pltpu.HBM) for a in (q, g, k, v, bal, lengths)))


def tile_runs(tab, low_run, t):
    runs = [low_run + t * TILE + u for u in range(TILE)]
    return [tab[r, 1] for r in runs], [tab[r, 0] for r in runs]


def run_rows(index):
    return index % (XLO * NZ), pl.ds(pl.multiple_of(index // (XLO * NZ) * RUN, RUN), RUN)


def tile_rows(kg, indices, part):
    pieces = []
    for index in indices:
        block, rows = run_rows(index)
        pieces.append(kg[block, part, rows, :])
    return jnp.concatenate(pieces, axis=0)


def masked_scores(k, q, places, pos, start):
    scores = lax.dot_general(k, q, (((1,), (1,)), ((), ())), preferred_element_type=F32)
    offset = lax.broadcasted_iota(jnp.int32, (RUN, ROWS), 0)
    parts = []
    for u, base in enumerate(places):
        seen = (offset <= pos - base) & (offset >= start - base)
        parts.append(jnp.where(seen, scores[u * RUN : (u + 1) * RUN] * (SCALING * LOG2E), NEGATIVE))
    return jnp.concatenate(parts, axis=0)


def forward_kernel(tab, row_tab, qg, kg, stats, out, held):
    def one_run(q_run, _):
        low_run, tiles = tab[QTAB + q_run, 0], tab[QTAB + q_run, 1]
        pos, start = row_tab[0, pl.ds(q_run, 1), :], row_tab[1, pl.ds(q_run, 1), :]
        rows = pl.ds(pl.multiple_of((q_run % 2) * ROWS, ROWS), ROWS)
        q = qg[q_run // 2, 0, rows, :]
        g = qg[q_run // 2, 1, rows, :]

        def score(t, top):
            indices, places = tile_runs(tab, low_run, t)
            s = masked_scores(tile_rows(kg, indices, 0), q, places, pos, start)
            held[t] = s
            return jnp.maximum(top, jnp.max(s, axis=0, keepdims=True))

        top = lax.fori_loop(0, tiles, score, jnp.full((1, ROWS), FLOOR, F32))

        def weigh(t, state):
            total, inner, acc = state
            indices, _ = tile_runs(tab, low_run, t)
            v = tile_rows(kg, indices, 1)
            raw = jnp.exp2(held[t] - top)
            gw = lax.dot_general(v, g, (((1,), (1,)), ((), ())), preferred_element_type=F32)
            total = total + jnp.sum(raw, axis=0, keepdims=True)
            inner = inner + jnp.sum(raw * gw, axis=0, keepdims=True)
            acc = acc + lax.dot_general(v, raw.astype(BF16), (((0,), (0,)), ((), ())), preferred_element_type=F32)
            return total, inner, acc

        zero = jnp.zeros((1, ROWS), F32)
        total, inner, acc = lax.fori_loop(0, tiles, weigh, (zero, zero, jnp.zeros((DH, ROWS), F32)))
        stats[q_run] = jnp.concatenate([top, total, inner, jnp.zeros((5, ROWS), F32)], axis=0)
        out[q_run] = acc
        return 0

    lax.fori_loop(0, QRUNS, one_run, 0)


def forward(tab, row_tab, qg, kg):
    smem = pl.BlockSpec(memory_space=pltpu.SMEM)
    vmem = pl.BlockSpec(memory_space=pltpu.VMEM)
    return pl.pallas_call(
        forward_kernel,
        out_shape=(
            jax.ShapeDtypeStruct((QRUNS, 8, ROWS), F32),
            jax.ShapeDtypeStruct((QRUNS, DH, ROWS), F32),
        ),
        in_specs=[smem, vmem, vmem, vmem],
        out_specs=(vmem, vmem),
        scratch_shapes=[pltpu.VMEM((KRUNS // TILE, TILE * RUN, ROWS), F32)],
        compiler_params=pltpu.CompilerParams(vmem_limit_bytes=16 << 20),
        name="forward_stats",
    )(tab, row_tab, qg, kg)


def exchange_kernel(mine, out, lsem, send, recv):
    h, xl, y, z = here()
    x = h * XLO + xl
    targets = [device(x, (y + d) % NY, z) for d in range(1, NY)]
    meet(targets)
    copies = []
    for d, target in enumerate(targets):
        copy = remote(mine, out.at[y], send.at[d], recv.at[d], target)
        copy.start()
        copies.append(copy)
    own = pltpu.make_async_copy(mine, out.at[y], lsem)
    own.start()
    own.wait()
    for copy in copies:
        copy.wait()


def exchange(stats):
    vmem = pl.BlockSpec(memory_space=pltpu.VMEM)
    dma = pltpu.SemaphoreType.DMA
    return pl.pallas_call(
        exchange_kernel,
        out_shape=jax.ShapeDtypeStruct((NY,) + stats.shape, F32),
        in_specs=[vmem],
        out_specs=vmem,
        scratch_shapes=[dma, dma((NY - 1,)), dma((NY - 1,))],
        compiler_params=pltpu.CompilerParams(collective_id=1, has_side_effects=True, vmem_limit_bytes=1 << 20),
        name="exchange_stats",
    )(stats)


def backward_kernel(tab, row_tab, qg, kg, stats, acc_out, own, rows_out, keys_out, key_acc, value_acc):
    key_acc[...] = jnp.zeros_like(key_acc)
    value_acc[...] = jnp.zeros_like(value_acc)

    def one_run(q_run, _):
        low_run, tiles = tab[QTAB + q_run, 0], tab[QTAB + q_run, 1]
        pos, start = row_tab[0, pl.ds(q_run, 1), :], row_tab[1, pl.ds(q_run, 1), :]
        rows = pl.ds(pl.multiple_of((q_run % 2) * ROWS, ROWS), ROWS)
        q = qg[q_run // 2, 0, rows, :]
        g = qg[q_run // 2, 1, rows, :]
        each = [stats[i, q_run] for i in range(NY)]
        tops = [e[0:1] for e in each]
        top = jnp.maximum(jnp.maximum(tops[0], tops[1]), jnp.maximum(tops[2], tops[3]))
        shares = [jnp.exp2(t - top) for t in tops]
        total = sum(e[1:2] * s for e, s in zip(each, shares))
        inner = sum(e[2:3] * s for e, s in zip(each, shares)) / total
        log_total = top + jnp.log(total) * LOG2E
        own_top = own[q_run][0:1]

        def tile(t, grad):
            indices, places = tile_runs(tab, low_run, t)
            k = tile_rows(kg, indices, 0)
            s = masked_scores(k, q, places, pos, start)
            weights = jnp.exp2(s - log_total)
            gw = lax.dot_general(
                tile_rows(kg, indices, 1), g, (((1,), (1,)), ((), ())), preferred_element_type=F32
            )
            gs = (weights * (gw - inner)).astype(BF16)
            value_part = jnp.dot(weights.astype(BF16), g, preferred_element_type=F32)
            key_part = jnp.dot(gs, q, preferred_element_type=F32)
            for u, index in enumerate(indices):
                block, to = run_rows(index)
                value_acc[block, to, :] += value_part[u * RUN : (u + 1) * RUN]
                key_acc[block, to, :] += key_part[u * RUN : (u + 1) * RUN]
            return grad + lax.dot_general(k, gs, (((0,), (0,)), ((), ())), preferred_element_type=F32)

        grad = lax.fori_loop(0, tiles, tile, jnp.zeros((DH, ROWS), F32))
        attended = acc_out[q_run] * jnp.exp2(own_top - log_total)
        rows_out[q_run // 2, 0, rows, :] = attended.T.astype(BF16)
        rows_out[q_run // 2, 1, rows, :] = (grad * SCALING).T.astype(BF16)
        return 0

    lax.fori_loop(0, QRUNS, one_run, 0)
    for block in range(XLO * NZ):
        keys_out[block, 0] = (key_acc[block] * SCALING).astype(BF16)
        keys_out[block, 1] = value_acc[block].astype(BF16)


def backward(tab, row_tab, qg, kg, stats, acc, own):
    smem = pl.BlockSpec(memory_space=pltpu.SMEM)
    vmem = pl.BlockSpec(memory_space=pltpu.VMEM)
    return pl.pallas_call(
        backward_kernel,
        out_shape=(
            jax.ShapeDtypeStruct((NY, 2, 2 * ROWS, DH), BF16),
            jax.ShapeDtypeStruct((XLO * NZ, 2, BLK, DH), BF16),
        ),
        in_specs=[smem] + [vmem] * 6,
        out_specs=(vmem, vmem),
        scratch_shapes=[pltpu.VMEM((XLO * NZ, BLK, DH), F32), pltpu.VMEM((XLO * NZ, BLK, DH), F32)],
        compiler_params=pltpu.CompilerParams(vmem_limit_bytes=16 << 20),
        name="backward_terms",
    )(tab, row_tab, qg, kg, stats, acc, own)


def reduce_kernel(
    rows, keys, att, qgrad, kgrad, vgrad,
    ybuf, ysum, xbuf, xsum, zbuf, zown, zsum, last, ysend, yrecv, xsend, xrecv, zsend, zrecv, hsend, hrecv,
):
    h, xl, y, z = here()
    x = h * XLO + xl
    half = NZ // 2
    y_up, y_dn = device(x, (y + 1) % NY, z), device(x, (y + NY - 1) % NY, z)
    x_up, x_dn, x_far = (device((x + d) % NX, y, z) for d in (1, NX - 1, 2))
    z_all = [device(x, y, (z + d) % NZ) for d in range(1, NZ)]
    meet([y_up, y_dn, x_up, x_dn, x_far] + z_all)
    started = []

    def go(copy):
        copy.start()
        started.append(copy)
        return copy

    def piece(ring):
        return (ring % XLO) * NZ, ring // XLO

    up, dn, far = (x + 1) % NX, (x + NX - 1) % NX, (x + 2) % NX
    far_first, far_part = piece(far)
    up_first, up_part = piece(up)
    dn_first, dn_part = piece(dn)
    my_first, my_part = piece(x)
    lo, hi = pl.ds(0, half), pl.ds(half, half)
    x_a = go(remote(keys.at[pl.ds(far_first, half), far_part], xbuf.at[0], xsend.at[0], xrecv.at[0], x_up))
    x_b = go(remote(keys.at[pl.ds(far_first + half, half), far_part], xbuf.at[1], xsend.at[1], xrecv.at[1], x_dn))
    y_far = (y + 2) % NY
    y_a = go(remote(rows.at[y_far, 0], ybuf.at[0], ysend.at[0], yrecv.at[0], y_up))
    y_b = go(remote(rows.at[y_far, 1], ybuf.at[1], ysend.at[1], yrecv.at[1], y_dn))
    x_c = go(remote(keys.at[pl.ds(up_first + half, half), up_part], xbuf.at[2], xsend.at[2], xrecv.at[2], x_up))
    x_d = go(remote(keys.at[pl.ds(dn_first, half), dn_part], xbuf.at[3], xsend.at[3], xrecv.at[3], x_dn))
    y_c = go(remote(rows.at[(y + 1) % NY, 1], ybuf.at[2], ysend.at[2], yrecv.at[2], y_up))
    y_d = go(remote(rows.at[(y + NY - 1) % NY, 0], ybuf.at[3], ysend.at[3], yrecv.at[3], y_dn))
    x_a.wait_recv()
    xsum[0] = (xbuf[0].astype(F32) + keys[pl.ds(up_first, half), up_part].astype(F32)).astype(BF16)
    x_e = go(remote(xsum.at[0], xbuf.at[4], xsend.at[4], xrecv.at[4], x_up))
    x_b.wait_recv()
    xsum[1] = (xbuf[1].astype(F32) + keys[pl.ds(dn_first + half, half), dn_part].astype(F32)).astype(BF16)
    x_f = go(remote(xsum.at[1], xbuf.at[5], xsend.at[5], xrecv.at[5], x_dn))
    y_a.wait_recv()
    ysum[0] = (ybuf[0].astype(F32) + rows[(y + 1) % NY, 0].astype(F32)).astype(BF16)
    y_e = go(remote(ysum.at[0], ybuf.at[4], ysend.at[4], yrecv.at[4], y_up))
    y_b.wait_recv()
    ysum[1] = (ybuf[1].astype(F32) + rows[(y + NY - 1) % NY, 1].astype(F32)).astype(BF16)
    y_f = go(remote(ysum.at[1], ybuf.at[5], ysend.at[5], yrecv.at[5], y_dn))
    x_d.wait_recv()
    x_e.wait_recv()
    zown[lo] = keys[pl.ds(my_first, half), my_part].astype(F32) + xbuf[3].astype(F32) + xbuf[4].astype(F32)
    x_c.wait_recv()
    x_f.wait_recv()
    zown[hi] = keys[pl.ds(my_first + half, half), my_part].astype(F32) + xbuf[2].astype(F32) + xbuf[5].astype(F32)
    zsum[...] = zown[...].astype(BF16)
    z_copies = []
    for d in (4, 3, 5, 2, 6, 1, 7):
        block = (z + d) % NZ
        z_copies.append(
            go(remote(zsum.at[block], zbuf.at[d - 1], zsend.at[d - 1], zrecv.at[d - 1], z_all[d - 1]))
        )
    y_d.wait_recv()
    y_e.wait_recv()
    att[...] = (rows[y, 0].astype(F32) + ybuf[3].astype(F32) + ybuf[4].astype(F32)).astype(BF16)
    y_c.wait_recv()
    y_f.wait_recv()
    qgrad[...] = (rows[y, 1].astype(F32) + ybuf[2].astype(F32) + ybuf[5].astype(F32)).astype(BF16)
    total = zown[z]
    for copy in z_copies:
        copy.wait_recv()
    for d in range(NZ - 1):
        total = total + zbuf[d].astype(F32)
    last[0] = total.astype(BF16)
    final = go(remote(last.at[0], last.at[1], hsend, hrecv, x_far))
    final.wait_recv()
    mine, other = last[0], last[1]
    kgrad[...] = jnp.where(h == 0, mine, other)
    vgrad[...] = jnp.where(h == 0, other, mine)
    for copy in started:
        copy.wait_send()


def reduce(rows, keys):
    vmem = pl.BlockSpec(memory_space=pltpu.VMEM)
    dma = pltpu.SemaphoreType.DMA
    half = NZ // 2
    return pl.pallas_call(
        reduce_kernel,
        out_shape=(
            jax.ShapeDtypeStruct((2 * ROWS, DH), BF16),
            jax.ShapeDtypeStruct((2 * ROWS, DH), BF16),
            jax.ShapeDtypeStruct((BLK, DH), BF16),
            jax.ShapeDtypeStruct((BLK, DH), BF16),
        ),
        in_specs=[vmem, vmem],
        out_specs=(vmem,) * 4,
        scratch_shapes=[
            pltpu.VMEM((6, 2 * ROWS, DH), BF16),
            pltpu.VMEM((2, 2 * ROWS, DH), BF16),
            pltpu.VMEM((6, half, BLK, DH), BF16),
            pltpu.VMEM((2, half, BLK, DH), BF16),
            pltpu.VMEM((NZ - 1, BLK, DH), BF16),
            pltpu.VMEM((NZ, BLK, DH), F32),
            pltpu.VMEM((NZ, BLK, DH), BF16),
            pltpu.VMEM((2, BLK, DH), BF16),
            dma((6,)), dma((6,)), dma((6,)), dma((6,)), dma((NZ - 1,)), dma((NZ - 1,)), dma, dma,
        ],
        compiler_params=pltpu.CompilerParams(collective_id=2, has_side_effects=True, vmem_limit_bytes=16 << 20),
        name="reduce_terms",
    )(rows, keys)


def store_kernel(*refs):
    count = len(refs) // 2
    copies = [pltpu.make_async_copy(refs[i], refs[count + i], refs[-1].at[i]) for i in range(count)]
    for copy in copies:
        copy.start()
    for copy in copies:
        copy.wait()


def store(*arrays):
    return pl.pallas_call(
        store_kernel,
        out_shape=tuple(jax.ShapeDtypeStruct(a.shape, a.dtype) for a in arrays),
        in_specs=[pl.BlockSpec(memory_space=pltpu.VMEM)] * len(arrays),
        out_specs=(pl.BlockSpec(memory_space=pl.ANY),) * len(arrays),
        scratch_shapes=[pltpu.SemaphoreType.DMA((len(arrays),))],
        compiler_params=pltpu.CompilerParams(vmem_limit_bytes=1 << 20),
        name="store_outputs",
    )(*arrays)


def body(queries, key_rows, value_rows, out_grad, doc_lengths, balance):
    flat = (2 * ROWS, DH)
    bal = balance.reshape(SPANS // 2, BLK)
    qg, kg, tab, row_tab = gather(
        queries.reshape(flat), out_grad.reshape(flat), key_rows, value_rows, bal, doc_lengths
    )
    own, acc = forward(tab, row_tab, qg, kg)
    stats = exchange(own)
    rows, keys = backward(tab, row_tab, qg, kg, stats, acc, own)
    attended, query_grad, key_grad, value_grad = store(*reduce(rows, keys))
    return attended.reshape(queries.shape), query_grad.reshape(queries.shape), key_grad, value_grad


def solution(mesh):
    return jax.shard_map(
        body,
        mesh=mesh,
        in_specs=(
            P(("seq", "ctx"), "head", None),
            P(("seq", "ctx"), None),
            P(("seq", "ctx"), None),
            P(("seq", "ctx"), "head", None),
            P("seq"),
            P("seq"),
        ),
        out_specs=(
            P(("seq", "ctx"), "head", None),
            P(("seq", "ctx"), "head", None),
            P(("seq", "ctx"), None),
            P(("seq", "ctx"), None),
        ),
        check_vma=False,
    )
```

time: 83.5 us -> 68.3 us (0.82)
  local copies, waits for them, and re-layouts: 8.15 us -> 0 us
  Pallas kernels: 74.1 us -> 67.1 us
    unnamed x18 -> x0, local copies, waits for them, and re-layouts: 7.21 us -> none
    pallas_call x1, Pallas kernels: 26 us -> 21.7 us  [gather(): pl.pallas_call(gather_kernel, out_shape=(jax.ShapeDtypeStruct((NY, 2, 2 *...]
    pallas_call x1, Pallas kernels: 8.26 us -> 5.2 us  [backward(): pl.pallas_call(backward_kernel, out_shape=(jax.ShapeDtypeStruct((NY, 2, 2...]
    pallas_call x1, Pallas kernels: 6.9 us -> 4.1 us  [forward(): pl.pallas_call(forward_kernel, out_shape=(jax.ShapeDtypeStruct((QRUNS, 8,...]
    pallas_call x1, Pallas kernels: 24.2 us -> 26.3 us  [reduce(): pl.pallas_call(reduce_kernel, out_shape=(jax.ShapeDtypeStruct((2 * ROWS,...]
where the time goes in v2:
time: 68.3 us; the launch traced here: 67.8 us
  Pallas kernels  67.1 us (98%)
    pallas_call x1, Pallas kernels, reduce(): pl.pallas_call(reduce_kernel, out_shape=(jax.ShapeDtypeStruct((2 * ROWS,...  26.3 us
    pallas_call x1, Pallas kernels, gather(): pl.pallas_call(gather_kernel, out_shape=(jax.ShapeDtypeStruct((NY, 2, 2 *...  21.7 us
    pallas_call x1, Pallas kernels, exchange(): pl.pallas_call(exchange_kernel, out_shape=jax.ShapeDtypeStruct((NY,) + st...  9.09 us
    pallas_call x1, Pallas kernels, backward(): pl.pallas_call(backward_kernel, out_shape=(jax.ShapeDtypeStruct((NY, 2, 2...  5.2 us
    pallas_call x1, Pallas kernels, forward(): pl.pallas_call(forward_kernel, out_shape=(jax.ShapeDtypeStruct((QRUNS, 8,...  4.1 us

profile of v2, /device:TPU:2, one launch (start us, length us, event | category | flops | bytes accessed | tf_op | source)
XLA Modules:
  0.0 67.8 jit_solution(15640891892125235534)
XLA Ops:
  0.6 21.7 %gather_rows.1 = (bf16[4,2,512,128]{3,2,1,0:T(8,128)(2,1)S(1)}, bf16[16,2,128,128]{3,2,1,0:T(8,128)(2,1)S(1)}, s32[48,128]{1,0:T(8,128)S(1)}, s32[2,8,256]{2,1,0:T(8,128)S(1)}) custom-call(bf16[512,128]{1,0:T(8,128)(2,1)} %bitcast.5, bf16[512,128]{1,0:T(8,128)(2,1)} %bitcast.6, bf16[128,128]{1,0:T(8,128)(2,1)} %k_ref.1, bf16[128,128]{1,0:T(8,128)(2,1)} %v_ref.1, ...), custom_call_target="tpu_custom_call" | custom-call | tf_op jit(solution)/shard_map/gather_rows/pallas_call | solution.py:188
  22.4 4.1 %forward_stats.1 = (f32[8,8,256]{2,1,0:T(8,128)S(1)}, f32[8,128,256]{2,1,0:T(8,128)S(1)}) custom-call(s32[48,128]{1,0:T(8,128)S(1)} %get-tuple-element.20.tab, s32[2,8,256]{2,1,0:T(8,128)S(1)} %get-tuple-element.21.row_tab, bf16[4,2,512,128]{3,2,1,0:T(8,128)(2,1)S(1)} %get-tuple-element.22.qg, bf16[16,2,128,128]{3,2,1,0:T(8,128)(2,1)S(1)} %get-tuple-element.23.kg), custom_call_target="tpu_custom_call" | custom-call | tf_op jit(solution)/shard_map/forward_stats/pallas_call | solution.py:274
  26.5 9.1 %exchange_stats.1.stats = f32[4,8,8,256]{3,2,1,0:T(8,128)S(1)} custom-call(f32[8,8,256]{2,1,0:T(8,128)S(1)} %get-tuple-element.24.mine.own), custom_call_target="tpu_custom_call" | custom-call | tf_op jit(solution)/shard_map/exchange_stats/pallas_call | solution.py:308
  35.6 5.2 %backward_terms.1 = (bf16[4,2,512,128]{3,2,1,0:T(8,128)(2,1)S(1)}, bf16[16,2,128,128]{3,2,1,0:T(8,128)(2,1)S(1)}) custom-call(s32[48,128]{1,0:T(8,128)S(1)} %get-tuple-element.20.tab, s32[2,8,256]{2,1,0:T(8,128)S(1)} %get-tuple-element.21.row_tab, bf16[4,2,512,128]{3,2,1,0:T(8,128)(2,1)S(1)} %get-tuple-element.22.qg, ...), custom_call_target="tpu_custom_call" | custom-call | tf_op jit(solution)/shard_map/backward_terms/pallas_call | solution.py:370
  40.8 26.3 %reduce_terms.1 = (bf16[512,128]{1,0:T(8,128)(2,1)S(1)}, bf16[512,128]{1,0:T(8,128)(2,1)S(1)}, bf16[128,128]{1,0:T(8,128)(2,1)S(1)}, bf16[128,128]{1,0:T(8,128)(2,1)S(1)}) custom-call(bf16[4,2,512,128]{3,2,1,0:T(8,128)(2,1)S(1)} %get-tuple-element.26.rows, bf16[16,2,128,128]{3,2,1,0:T(8,128)(2,1)S(1)} %get-tuple-element.27.keys), custom_call_target="tpu_custom_call" | custom-call | tf_op jit(solution)/shard_map/reduce_terms/pallas_call | solution.py:470
  67.1 0.7 %store_outputs.1 = (bf16[512,128]{1,0:T(8,128)(2,1)}, bf16[512,128]{1,0:T(8,128)(2,1)}, bf16[128,128]{1,0:T(8,128)(2,1)}, bf16[128,128]{1,0:T(8,128)(2,1)}) custom-call(bf16[512,128]{1,0:T(8,128)(2,1)S(1)} %get-tuple-element.28.refs_0_, bf16[512,128]{1,0:T(8,128)(2,1)S(1)} %get-tuple-element.29.refs_1_, bf16[128,128]{1,0:T(8,128)(2,1)S(1)} %get-tuple-element.30.refs_2_, ...), custom_call_target="tpu_custom_call" | custom-call | tf_op jit(solution)/shard_map/store_outputs/pallas_call | solution.py:506

commit v3 on v2

v3 whole, which is shorter than its diff:
```python
import math

import jax
import jax.numpy as jnp
from jax import lax
from jax.experimental import pallas as pl
from jax.experimental.pallas import tpu as pltpu
from jax.sharding import PartitionSpec as P

NX, NY, NZ = 4, 4, 8
XLO = 2
RUN = 64
DH = 128
HEADS_HERE = 4
ROWS = RUN * HEADS_HERE
BLK = 2 * RUN
KRUNS = XLO * NZ * 2
QRUNS = NY * 2
TILE = 4
SPANS = 128
ITEMS = QRUNS * (KRUNS // TILE)
DOCS = 8
NEGATIVE = -1e30
FLOOR = -1e29
FAR = 1 << 20
SCALING = 1.0 / math.sqrt(DH)
LOG2E = 1.0 / math.log(2.0)
MESH = pl.DeviceIdType.MESH
F32 = jnp.float32
BF16 = jnp.bfloat16


def here():
    c = lax.axis_index("ctx")
    h = lax.axis_index("head")
    return h, c // (NY * NZ), (c // NZ) % NY, c % NZ


def device(x, y, z):
    return {"ctx": ((x % XLO) * NY + y) * NZ + z, "head": x // XLO}


def greet(targets):
    barrier = pltpu.get_barrier_semaphore()
    for target in targets:
        pl.semaphore_signal(barrier, inc=1, device_id=target, device_id_type=MESH)
    return lambda: pl.semaphore_wait(barrier, len(targets))


def remote(src, dst, send, recv, target):
    return pltpu.make_async_remote_copy(
        src_ref=src, dst_ref=dst, send_sem=send, recv_sem=recv, device_id=target, device_id_type=MESH
    )


def tables(bal, lengths, tab, row_tab, xl, y, z):
    lane = lax.broadcasted_iota(jnp.int32, (1, SPANS), 1)
    slabs = [bal[pl.ds(pl.multiple_of((i * NY + y) * NZ, NZ), NZ), :] for i in range(XLO)]
    held = [slab[:, half * RUN : half * RUN + 1] // RUN for half in (0, 1) for slab in slabs]
    held = jnp.concatenate(held, axis=0)
    index = lax.broadcasted_iota(jnp.int32, (KRUNS, 1), 0)
    match = held == lane
    has = jnp.sum(jnp.where(match, 1, 0), axis=0, keepdims=True)
    which = jnp.sum(jnp.where(match, index, 0), axis=0, keepdims=True)
    before = jnp.sum(jnp.where(held < lane, 1, 0), axis=0, keepdims=True)
    rank = jnp.where(has > 0, before, -1)
    hit = jnp.where(rank == lax.broadcasted_iota(jnp.int32, (SPANS, 1), 0), 1.0, 0.0).astype(BF16)
    row = lax.broadcasted_iota(jnp.int32, (8, 1), 0)
    found = jnp.where(row == 0, lane, jnp.where(row == 1, which, 0)).astype(F32).astype(BF16)
    sorted_runs = lax.dot_general(found, hit, (((1,), (1,)), ((), ())), preferred_element_type=F32)
    sorted_runs = jnp.where((row == 0) & (lane >= KRUNS), F32(FAR // RUN), sorted_runs).astype(jnp.int32)
    q_rows = [bal[pl.ds((xl * NY + i) * NZ + z, 1), :] for i in range(NY)]
    low = jnp.concatenate([r[:, half * RUN : half * RUN + 1] for r in q_rows for half in (0, 1)], axis=0)
    pos = low + lax.broadcasted_iota(jnp.int32, (QRUNS, ROWS), 1) // HEADS_HERE
    start = jnp.zeros((QRUNS, ROWS), jnp.int32)
    first = jnp.zeros((QRUNS, 1), jnp.int32)
    end = 0
    for d in range(DOCS):
        end = end + lengths[d]
        first = jnp.where(low >= end, end, first)
        start = jnp.where(pos >= end, end, start)
    row_tab[0] = pos
    row_tab[1] = start
    low_run = jnp.sum(jnp.where((lane < first // RUN) & (has > 0), 1, 0), axis=1, keepdims=True)
    high_run = jnp.sum(jnp.where((lane <= low // RUN) & (has > 0), 1, 0), axis=1, keepdims=True)
    tiles = jnp.maximum((high_run - low_run + TILE - 1) // TILE, 1)
    own_lane = lax.broadcasted_iota(jnp.int32, (QRUNS, 1), 0) == lane
    low_row = jnp.sum(jnp.where(own_lane, low_run, 0), axis=0, keepdims=True)
    tiles_row = jnp.sum(jnp.where(own_lane, tiles, 0), axis=0, keepdims=True)
    tab[...] = jnp.where(row == 2, low_row, jnp.where(row == 3, tiles_row, sorted_runs))


def gather_kernel(
    q_ref, g_ref, k_ref, v_ref, bal_ref, len_ref, qg, kg, tab, row_tab, bal, lengths, lsem, ysend, yrecv, zsend, zrecv, xsend, xrecv
):
    h, xl, y, z = here()
    x = h * XLO + xl
    first = xl * NZ
    y_up, y_dn = device(x, (y + 1) % NY, z), device(x, (y + NY - 1) % NY, z)
    z_to = {d: device(x, y, (z + d + NZ) % NZ) for d in (1, 2, -1, -2)}
    x_up, x_dn = device((x + 1) % NX, y, z), device((x + NX - 1) % NX, y, z)
    meet = greet([y_up, y_dn, x_up, x_dn] + list(z_to.values()))
    kv = (k_ref, v_ref)
    started = []

    def go(copy):
        copy.start()
        started.append(copy)
        return copy

    sent_z = {}

    def z_send(sign, hops, dist, part):
        block = (z - sign * (dist - hops) + NZ) % NZ
        dst = kg.at[first + block, part]
        src = kv[part] if dist == hops else dst
        way = 0 if sign > 0 else 1
        sems = zsend.at[way, dist - 1, part], zrecv.at[way, dist - 1, part]
        sent_z[sign, dist, part] = go(remote(src, dst, *sems, z_to[sign * hops]))

    sent_x = []

    def x_send(slot, block):
        dst = kg.at[first + block, h]
        for side, target in ((0, x_up), (1, x_dn)):
            sent_x.append(go(remote(dst, dst, xsend.at[side, slot], xrecv.at[side, slot], target)))

    def local(src, dst, slot):
        copy = pltpu.make_async_copy(src, dst, lsem.at[slot])
        copy.start()
        return copy

    own_kv = [local(kv[part], kg.at[first + z, part], part) for part in (0, 1)]
    own_tab = [local(bal_ref, bal, 4), local(len_ref, lengths, 5)]
    meet()
    for part in (0, 1):
        for sign in (1, -1):
            z_send(sign, 2, 2, part)
    y_q_up = go(remote(q_ref, qg.at[y, 0], ysend.at[0], yrecv.at[0], y_up))
    y_g_dn = go(remote(g_ref, qg.at[y, 1], ysend.at[2], yrecv.at[2], y_dn))
    for part in (0, 1):
        for sign in (1, -1):
            z_send(sign, 1, 1, part)
    y_g_up = go(remote(g_ref, qg.at[y, 1], ysend.at[1], yrecv.at[1], y_up))
    y_q_dn = go(remote(q_ref, qg.at[y, 0], ysend.at[3], yrecv.at[3], y_dn))
    own_q = [local(ref, qg.at[y, part], 2 + part) for part, ref in ((0, q_ref), (1, g_ref))]
    for copy in own_kv:
        copy.wait()
    x_send(0, z)
    for copy in own_tab:
        copy.wait()
    tables(bal, lengths, tab, row_tab, xl, y, z)
    for part in (0, 1):
        for sign in (1, -1):
            sent_z[sign, 2, part].wait_recv()
            z_send(sign, 1, 3, part)
            if part == (0 if sign > 0 else 1):
                z_send(sign, 2, 4, part)
    x_send(1, (z - 2 + NZ) % NZ)
    x_send(2, (z + 2) % NZ)
    y_q_up.wait_recv()
    q_on = qg.at[(y + NY - 1) % NY, 0]
    y_fwd_up = go(remote(q_on, q_on, ysend.at[4], yrecv.at[4], y_up))
    y_g_dn.wait_recv()
    g_on = qg.at[(y + 1) % NY, 1]
    y_fwd_dn = go(remote(g_on, g_on, ysend.at[5], yrecv.at[5], y_dn))
    slot = 3
    for dist in (1, 3):
        for sign in (1, -1):
            for part in (0, 1):
                sent_z[sign, dist, part].wait_recv()
            x_send(slot, (z - sign * dist + NZ) % NZ)
            slot += 1
    sent_z[1, 4, 0].wait_recv()
    sent_z[-1, 4, 1].wait_recv()
    x_send(7, (z + NZ // 2) % NZ)
    for copy in (y_g_up, y_q_dn, y_fwd_up, y_fwd_dn):
        copy.wait_recv()
    for copy in sent_x:
        copy.wait_recv()
    for copy in started:
        copy.wait_send()
    for copy in own_q:
        copy.wait()


def gather(q, g, k, v, bal, lengths):
    hbm = pl.BlockSpec(memory_space=pltpu.HBM)
    vmem = pl.BlockSpec(memory_space=pltpu.VMEM)
    dma = pltpu.SemaphoreType.DMA
    return pl.pallas_call(
        gather_kernel,
        out_shape=(
            jax.ShapeDtypeStruct((NY, 2, 2 * ROWS, DH), BF16),
            jax.ShapeDtypeStruct((XLO * NZ, 2, BLK, DH), BF16),
            jax.ShapeDtypeStruct((8, SPANS), jnp.int32),
            jax.ShapeDtypeStruct((2, QRUNS, ROWS), jnp.int32),
        ),
        in_specs=[hbm] * 6,
        out_specs=(vmem,) * 4,
        scratch_shapes=[
            pltpu.VMEM((SPANS // 2, BLK), jnp.int32),
            pltpu.SMEM((DOCS,), jnp.int32),
            dma((6,)), dma((6,)), dma((6,)), dma((2, 4, 2)), dma((2, 4, 2)), dma((2, 8)), dma((2, 8)),
        ],
        compiler_params=pltpu.CompilerParams(collective_id=0, has_side_effects=True, vmem_limit_bytes=8 << 20),
        name="gather_rows",
    )(*(pltpu.with_memory_space_constraint(a, pltpu.HBM) for a in (q, g, k, v, bal, lengths)))


def tile_runs(tab, low_run, t):
    runs = [low_run + t * TILE + u for u in range(TILE)]
    return [tab[1, r] for r in runs], [tab[0, r] * RUN for r in runs]


def run_rows(index):
    return index % (XLO * NZ), pl.ds(pl.multiple_of(index // (XLO * NZ) * RUN, RUN), RUN)


def tile_rows(kg, indices, part):
    pieces = []
    for index in indices:
        block, rows = run_rows(index)
        pieces.append(kg[block, part, rows, :])
    return jnp.concatenate(pieces, axis=0)


def masked_scores(k, q, places, pos, start):
    scores = lax.dot_general(k, q, (((1,), (1,)), ((), ())), preferred_element_type=F32)
    offset = lax.broadcasted_iota(jnp.int32, (RUN, ROWS), 0)
    parts = []
    for u, base in enumerate(places):
        seen = (offset <= pos - base) & (offset >= start - base)
        parts.append(jnp.where(seen, scores[u * RUN : (u + 1) * RUN] * (SCALING * LOG2E), NEGATIVE))
    return jnp.concatenate(parts, axis=0)


def each_item(tab, process):
    total = sum(tab[3, i] for i in range(QRUNS))

    def step(i, state):
        q_run, t = state
        for u in range(2):
            process(q_run, t, 2 * i + u)
            more = (t + 1 < tab[3, q_run]) | (q_run == QRUNS - 1)
            q_run, t = jnp.where(more, q_run, q_run + 1), jnp.where(more, t + 1, 0)
        return q_run, t

    lax.fori_loop(0, (total + 1) // 2, step, (0, 0))


def query_rows(qg, q_run, part):
    return qg[q_run // 2, part, pl.ds(pl.multiple_of((q_run % 2) * ROWS, ROWS), ROWS), :]


def forward_kernel(tab, row_tab, qg, kg, stats, out, held, held_gw):
    stats[0] = jnp.full((QRUNS, ROWS), FLOOR, F32)
    stats[1] = jnp.zeros((QRUNS, ROWS), F32)
    stats[2] = jnp.zeros((QRUNS, ROWS), F32)
    out[...] = jnp.zeros_like(out)

    def process(q_run, t, item):
        at = pl.ds(q_run, 1)
        indices, places = tile_runs(tab, tab[2, q_run], t)
        s = masked_scores(
            tile_rows(kg, indices, 0), query_rows(qg, q_run, 0), places, row_tab[0, at, :], row_tab[1, at, :]
        )
        held[item] = s
        v = tile_rows(kg, indices, 1)
        gw = lax.dot_general(
            v, query_rows(qg, q_run, 1), (((1,), (1,)), ((), ())), preferred_element_type=F32
        )
        held_gw[item] = gw
        top = jnp.maximum(jnp.max(s, axis=0, keepdims=True), FLOOR)
        raw = jnp.exp2(s - top)
        total = jnp.sum(raw, axis=0, keepdims=True)
        inner = jnp.sum(raw * gw, axis=0, keepdims=True)
        acc = lax.dot_general(v, raw.astype(BF16), (((0,), (0,)), ((), ())), preferred_element_type=F32)
        old_top = stats[0, at, :]
        new_top = jnp.maximum(old_top, top)
        old_share, share = jnp.exp2(old_top - new_top), jnp.exp2(top - new_top)
        stats[0, at, :] = new_top
        stats[1, at, :] = stats[1, at, :] * old_share + total * share
        stats[2, at, :] = stats[2, at, :] * old_share + inner * share
        out[q_run] = out[q_run] * old_share + acc * share

    each_item(tab, process)


def forward(tab, row_tab, qg, kg):
    smem = pl.BlockSpec(memory_space=pltpu.SMEM)
    vmem = pl.BlockSpec(memory_space=pltpu.VMEM)
    return pl.pallas_call(
        forward_kernel,
        out_shape=(
            jax.ShapeDtypeStruct((3, QRUNS, ROWS), F32),
            jax.ShapeDtypeStruct((QRUNS, DH, ROWS), F32),
            jax.ShapeDtypeStruct((ITEMS, TILE * RUN, ROWS), F32),
            jax.ShapeDtypeStruct((ITEMS, TILE * RUN, ROWS), F32),
        ),
        in_specs=[smem, vmem, vmem, vmem],
        out_specs=(vmem,) * 4,
        compiler_params=pltpu.CompilerParams(vmem_limit_bytes=8 << 20),
        name="forward_stats",
    )(tab, row_tab, qg, kg)


def exchange_kernel(mine, out, lsem, send, recv):
    h, xl, y, z = here()
    x = h * XLO + xl
    targets = [device(x, (y + d) % NY, z) for d in range(1, NY)]
    greet(targets)()
    copies = []
    for d, target in enumerate(targets):
        copy = remote(mine, out.at[y], send.at[d], recv.at[d], target)
        copy.start()
        copies.append(copy)
    own = pltpu.make_async_copy(mine, out.at[y], lsem)
    own.start()
    own.wait()
    for copy in copies:
        copy.wait()


def exchange(stats):
    vmem = pl.BlockSpec(memory_space=pltpu.VMEM)
    dma = pltpu.SemaphoreType.DMA
    return pl.pallas_call(
        exchange_kernel,
        out_shape=jax.ShapeDtypeStruct((NY,) + stats.shape, F32),
        in_specs=[vmem],
        out_specs=vmem,
        scratch_shapes=[dma, dma((NY - 1,)), dma((NY - 1,))],
        compiler_params=pltpu.CompilerParams(collective_id=1, has_side_effects=True, vmem_limit_bytes=1 << 20),
        name="exchange_stats",
    )(stats)


def backward_kernel(
    tab, qg, kg, stats, held, held_gw, share_out, grad_acc, kv_acc, row_stats
):
    y = here()[2]
    kv_acc[...] = jnp.zeros_like(kv_acc)
    grad_acc[...] = jnp.zeros_like(grad_acc)
    top = jnp.maximum(jnp.maximum(stats[0, 0], stats[1, 0]), jnp.maximum(stats[2, 0], stats[3, 0]))
    shares = [jnp.exp2(stats[i, 0] - top) for i in range(NY)]
    total = sum(stats[i, 1] * shares[i] for i in range(NY))
    log_total = top + jnp.log(total) * LOG2E
    row_stats[0] = log_total
    row_stats[1] = sum(stats[i, 2] * shares[i] for i in range(NY)) / total
    share_out[...] = jnp.exp2(stats[y, 0] - log_total)

    def process(q_run, t, item):
        at = pl.ds(q_run, 1)
        indices, _ = tile_runs(tab, tab[2, q_run], t)
        weights = jnp.exp2(held[item] - row_stats[0, at, :])
        gs = (weights * (held_gw[item] - row_stats[1, at, :])).astype(BF16)
        value_part = jnp.dot(weights.astype(BF16), query_rows(qg, q_run, 1), preferred_element_type=F32)
        key_part = jnp.dot(gs, query_rows(qg, q_run, 0), preferred_element_type=F32)
        grad = lax.dot_general(
            tile_rows(kg, indices, 0), gs, (((0,), (0,)), ((), ())), preferred_element_type=F32
        )
        for u, index in enumerate(indices):
            block, to = run_rows(index)
            kv_acc[1, block, to, :] += value_part[u * RUN : (u + 1) * RUN]
            kv_acc[0, block, to, :] += key_part[u * RUN : (u + 1) * RUN]
        grad_acc[q_run] += grad

    each_item(tab, process)


def backward(tab, qg, kg, stats, held, held_gw):
    smem = pl.BlockSpec(memory_space=pltpu.SMEM)
    vmem = pl.BlockSpec(memory_space=pltpu.VMEM)
    return pl.pallas_call(
        backward_kernel,
        out_shape=(
            jax.ShapeDtypeStruct((QRUNS, ROWS), F32),
            jax.ShapeDtypeStruct((QRUNS, DH, ROWS), F32),
            jax.ShapeDtypeStruct((2, XLO * NZ, BLK, DH), F32),
        ),
        in_specs=[smem] + [vmem] * 5,
        out_specs=(vmem,) * 3,
        scratch_shapes=[pltpu.VMEM((2, QRUNS, ROWS), F32)],
        compiler_params=pltpu.CompilerParams(vmem_limit_bytes=8 << 20),
        name="backward_terms",
    )(tab, qg, kg, stats, held, held_gw)


AHEAD = (4, 3, 2, 1)
BEHIND = (5, 6, 7, 0)


def reduce_kernel(
    acc, share, grad, kv, att, qgrad, kgrad, vgrad,
    rows, ybuf, ysum, xout, xbuf, xsum, zsum, zbuf, last,
    ysend, yrecv, xsend, xrecv, zsend, zrecv, hsend, hrecv,
):
    h, xl, y, z = here()
    x = h * XLO + xl
    y_up, y_dn = device(x, (y + 1) % NY, z), device(x, (y + NY - 1) % NY, z)
    x_to = tuple(device((x + d) % NX, y, z) for d in (1, NX - 1, 2))
    z_all = [device(x, y, (z + d) % NZ) for d in range(1, NZ)]
    meet = greet([y_up, y_dn, *x_to, *z_all])
    started = []

    def go(copy):
        copy.start()
        started.append(copy)
        return copy

    def term(step, offset):
        ring = (x + step) % NX
        part = ring // XLO
        block = kv[part, (ring % XLO) * NZ + (z + offset) % NZ]
        return block * jnp.where(part == 0, F32(SCALING), F32(1.0))

    def put_rows(yy):
        for half in (0, 1):
            q_run = yy * 2 + half
            to = pl.ds(half * ROWS, ROWS)
            rows[yy, 0, to, :] = (acc[q_run] * share[pl.ds(q_run, 1), :]).T.astype(BF16)
            rows[yy, 1, to, :] = (grad[q_run] * SCALING).T.astype(BF16)

    def x_copy(kind, way, i, src):
        return go(remote(src, xbuf.at[kind, way, i], xsend.at[kind, way, i], xrecv.at[kind, way, i], x_to[way]))

    offsets = (AHEAD, BEHIND)
    sent = {}
    for i in range(4):
        for way in (0, 1):
            xout[0, way, i] = term(2, offsets[way][i]).astype(BF16)
    meet()
    for i in range(4):
        for way in (0, 1):
            sent[0, way, i] = x_copy(0, way, i, xout.at[0, way, i])
    y_far, y_next, y_prev = (y + 2) % NY, (y + 1) % NY, (y + NY - 1) % NY
    put_rows(y_far)
    y_a = go(remote(rows.at[y_far, 0], ybuf.at[0], ysend.at[0], yrecv.at[0], y_up))
    y_b = go(remote(rows.at[y_far, 1], ybuf.at[1], ysend.at[1], yrecv.at[1], y_dn))
    for i in range(4):
        for way in (0, 1):
            xout[1, way, i] = term(1 if way == 0 else 3, offsets[1 - way][i]).astype(BF16)
            sent[1, way, i] = x_copy(1, way, i, xout.at[1, way, i])
    put_rows(y_next)
    put_rows(y_prev)
    y_c = go(remote(rows.at[y_next, 1], ybuf.at[2], ysend.at[2], yrecv.at[2], y_up))
    y_d = go(remote(rows.at[y_prev, 0], ybuf.at[3], ysend.at[3], yrecv.at[3], y_dn))
    for i in range(4):
        for way in (0, 1):
            sent[0, way, i].wait_recv()
            own = term(1 if way == 0 else 3, offsets[way][i])
            xsum[way, i] = (xbuf[0, way, i].astype(F32) + own).astype(BF16)
            sent[2, way, i] = x_copy(2, way, i, xsum.at[way, i])
    y_a.wait_recv()
    ysum[0] = (ybuf[0].astype(F32) + rows[y_next, 0].astype(F32)).astype(BF16)
    y_e = go(remote(ysum.at[0], ybuf.at[4], ysend.at[4], yrecv.at[4], y_up))
    y_b.wait_recv()
    ysum[1] = (ybuf[1].astype(F32) + rows[y_prev, 1].astype(F32)).astype(BF16)
    y_f = go(remote(ysum.at[1], ybuf.at[5], ysend.at[5], yrecv.at[5], y_dn))
    total = None
    z_copies = []
    for i in range(4):
        for way in (0, 1):
            sent[2, way, i].wait_recv()
            sent[1, 1 - way, i].wait_recv()
            offset = offsets[way][i]
            block = term(0, offset) + xbuf[2, way, i].astype(F32) + xbuf[1, 1 - way, i].astype(F32)
            if offset == 0:
                total = block
            else:
                zsum[offset - 1] = block.astype(BF16)
                z_copies.append(
                    go(
                        remote(
                            zsum.at[offset - 1], zbuf.at[offset - 1],
                            zsend.at[offset - 1], zrecv.at[offset - 1], z_all[offset - 1],
                        )
                    )
                )
    put_rows(y)
    y_d.wait_recv()
    y_e.wait_recv()
    att[...] = (rows[y, 0].astype(F32) + ybuf[3].astype(F32) + ybuf[4].astype(F32)).astype(BF16)
    y_c.wait_recv()
    y_f.wait_recv()
    qgrad[...] = (rows[y, 1].astype(F32) + ybuf[2].astype(F32) + ybuf[5].astype(F32)).astype(BF16)
    for copy in z_copies:
        copy.wait_recv()
    for d in range(NZ - 1):
        total = total + zbuf[d].astype(F32)
    last[0] = total.astype(BF16)
    final = go(remote(last.at[0], last.at[1], hsend, hrecv, x_to[2]))
    final.wait_recv()
    mine, other = last[0], last[1]
    kgrad[...] = jnp.where(h == 0, mine, other)
    vgrad[...] = jnp.where(h == 0, other, mine)
    for copy in started:
        copy.wait_send()


def reduce(acc, share, grad, kv):
    vmem = pl.BlockSpec(memory_space=pltpu.VMEM)
    dma = pltpu.SemaphoreType.DMA
    block = (BLK, DH)
    return pl.pallas_call(
        reduce_kernel,
        out_shape=(
            jax.ShapeDtypeStruct((2 * ROWS, DH), BF16),
            jax.ShapeDtypeStruct((2 * ROWS, DH), BF16),
            jax.ShapeDtypeStruct(block, BF16),
            jax.ShapeDtypeStruct(block, BF16),
        ),
        in_specs=[vmem] * 4,
        out_specs=(vmem,) * 4,
        scratch_shapes=[
            pltpu.VMEM((NY, 2, 2 * ROWS, DH), BF16),
            pltpu.VMEM((6, 2 * ROWS, DH), BF16),
            pltpu.VMEM((2, 2 * ROWS, DH), BF16),
            pltpu.VMEM((2, 2, 4) + block, BF16),
            pltpu.VMEM((3, 2, 4) + block, BF16),
            pltpu.VMEM((2, 4) + block, BF16),
            pltpu.VMEM((NZ - 1,) + block, BF16),
            pltpu.VMEM((NZ - 1,) + block, BF16),
            pltpu.VMEM((2,) + block, BF16),
            dma((6,)), dma((6,)), dma((3, 2, 4)), dma((3, 2, 4)), dma((NZ - 1,)), dma((NZ - 1,)), dma, dma,
        ],
        compiler_params=pltpu.CompilerParams(collective_id=2, has_side_effects=True, vmem_limit_bytes=8 << 20),
        name="reduce_terms",
    )(acc, share, grad, kv)


def store_kernel(*refs):
    count = len(refs) // 2
    copies = [pltpu.make_async_copy(refs[i], refs[count + i], refs[-1].at[i]) for i in range(count)]
    for copy in copies:
        copy.start()
    for copy in copies:
        copy.wait()


def store(*arrays):
    return pl.pallas_call(
        store_kernel,
        out_shape=tuple(jax.ShapeDtypeStruct(a.shape, a.dtype) for a in arrays),
        in_specs=[pl.BlockSpec(memory_space=pltpu.VMEM)] * len(arrays),
        out_specs=(pl.BlockSpec(memory_space=pl.ANY),) * len(arrays),
        scratch_shapes=[pltpu.SemaphoreType.DMA((len(arrays),))],
        compiler_params=pltpu.CompilerParams(vmem_limit_bytes=1 << 20),
        name="store_outputs",
    )(*arrays)


def body(queries, key_rows, value_rows, out_grad, doc_lengths, balance):
    flat = (2 * ROWS, DH)
    bal = balance.reshape(SPANS // 2, BLK)
    qg, kg, tab, row_tab = gather(
        queries.reshape(flat), out_grad.reshape(flat), key_rows, value_rows, bal, doc_lengths
    )
    own, acc, held, held_gw = forward(tab, row_tab, qg, kg)
    share, grad, kv = backward(tab, qg, kg, exchange(own), held, held_gw)
    attended, query_grad, key_grad, value_grad = store(*reduce(acc, share, grad, kv))
    return attended.reshape(queries.shape), query_grad.reshape(queries.shape), key_grad, value_grad


def solution(mesh):
    return jax.shard_map(
        body,
        mesh=mesh,
        in_specs=(
            P(("seq", "ctx"), "head", None),
            P(("seq", "ctx"), None),
            P(("seq", "ctx"), None),
            P(("seq", "ctx"), "head", None),
            P("seq"),
            P("seq"),
        ),
        out_specs=(
            P(("seq", "ctx"), "head", None),
            P(("seq", "ctx"), "head", None),
            P(("seq", "ctx"), None),
            P(("seq", "ctx"), None),
        ),
        check_vma=False,
    )
```

time: 68.3 us -> 58.5 us (0.86)
  Pallas kernels: 67.1 us -> 57.7 us
    pallas_call x1, Pallas kernels: 26.3 us -> 22.2 us  [reduce(): pl.pallas_call(reduce_kernel, out_shape=(jax.ShapeDtypeStruct((2 * ROWS,...]
    pallas_call x1, Pallas kernels: 9.09 us -> 5.84 us  [exchange(): pl.pallas_call(exchange_kernel, out_shape=jax.ShapeDtypeStruct((NY,) + st...]
    pallas_call x2, Pallas kernels: 9.3 us -> 7.23 us  [the longest x1 4.26 us: forward(): pl.pallas_call(forward_kernel, out_shape=(jax.ShapeDtypeStruct((3, QRUNS,...]
where the time goes in v3:
time: 58.5 us; the launch traced here: 58.4 us
  Pallas kernels  57.7 us (99%)
  between operations  0.67 us (1%)
    pallas_call x1, Pallas kernels, reduce(): pl.pallas_call(reduce_kernel, out_shape=(jax.ShapeDtypeStruct((2 * ROWS,...  22.2 us
    pallas_call x1, Pallas kernels, gather(): pl.pallas_call(gather_kernel, out_shape=(jax.ShapeDtypeStruct((NY, 2, 2 *...  21.7 us
    pallas_call x1, Pallas kernels, exchange(): pl.pallas_call(exchange_kernel, out_shape=jax.ShapeDtypeStruct((NY,) + st...  5.84 us
    pallas_call x1, Pallas kernels, forward(): pl.pallas_call(forward_kernel, out_shape=(jax.ShapeDtypeStruct((3, QRUNS,...  4.26 us
    pallas_call x1, Pallas kernels, backward(): pl.pallas_call(backward_kernel, out_shape=(jax.ShapeDtypeStruct((QRUNS, R...  2.97 us

profile of v3, /device:TPU:2, one launch (start us, length us, event | category | flops | bytes accessed | tf_op | source)
XLA Modules:
  0.0 58.4 jit_solution(5249829819106016550)
XLA Ops:
  0.6 21.7 %gather_rows.1 = (bf16[4,2,512,128]{3,2,1,0:T(8,128)(2,1)S(1)}, bf16[16,2,128,128]{3,2,1,0:T(8,128)(2,1)S(1)}, s32[8,128]{1,0:T(8,128)S(1)}, s32[2,8,256]{2,1,0:T(8,128)S(1)}) custom-call(bf16[512,128]{1,0:T(8,128)(2,1)} %bitcast.5, bf16[512,128]{1,0:T(8,128)(2,1)} %bitcast.6, bf16[128,128]{1,0:T(8,128)(2,1)} %k_ref.1, bf16[128,128]{1,0:T(8,128)(2,1)} %v_ref.1, ...), custom_call_target="tpu_custom_call" | custom-call | tf_op jit(solution)/shard_map/gather_rows/pallas_call | solution.py:191
  22.4 4.3 %forward_stats.1 = (f32[3,8,256]{2,1,0:T(8,128)S(1)}, f32[8,128,256]{2,1,0:T(8,128)S(1)}, f32[64,256,256]{2,1,0:T(8,128)S(1)}, f32[64,256,256]{2,1,0:T(8,128)S(1)}) custom-call(s32[8,128]{1,0:T(8,128)S(1)} %get-tuple-element.23.tab, s32[2,8,256]{2,1,0:T(8,128)S(1)} %get-tuple-element.24.row_tab, bf16[4,2,512,128]{3,2,1,0:T(8,128)(2,1)S(1)} %get-tuple-element.25.qg, ...), custom_call_target="tpu_custom_call" | custom-call | tf_op jit(solution)/shard_map/forward_stats/pallas_call | solution.py:293
  26.6 5.8 %exchange_stats.1.stats = f32[4,3,8,256]{3,2,1,0:T(8,128)S(1)} custom-call(f32[3,8,256]{2,1,0:T(8,128)S(1)} %get-tuple-element.28.mine), custom_call_target="tpu_custom_call" | custom-call | tf_op jit(solution)/shard_map/exchange_stats/pallas_call | solution.py:328
  32.5 3.0 %backward_terms.1 = (f32[8,256]{1,0:T(8,128)S(1)}, f32[8,128,256]{2,1,0:T(8,128)S(1)}, f32[2,16,128,128]{3,2,1,0:T(8,128)S(1)}) custom-call(s32[8,128]{1,0:T(8,128)S(1)} %get-tuple-element.23.tab, bf16[4,2,512,128]{3,2,1,0:T(8,128)(2,1)S(1)} %get-tuple-element.25.qg, bf16[16,2,128,128]{3,2,1,0:T(8,128)(2,1)S(1)} %get-tuple-element.26.kg, ...), custom_call_target="tpu_custom_call" | custom-call | tf_op jit(solution)/shard_map/backward_terms/pallas_call | solution.py:375
  35.5 22.2 %reduce_terms.1 = (bf16[512,128]{1,0:T(8,128)(2,1)S(1)}, bf16[512,128]{1,0:T(8,128)(2,1)S(1)}, bf16[128,128]{1,0:T(8,128)(2,1)S(1)}, bf16[128,128]{1,0:T(8,128)(2,1)S(1)}) custom-call(f32[8,128,256]{2,1,0:T(8,128)S(1)} %get-tuple-element.27.acc, f32[8,256]{1,0:T(8,128)S(1)} %get-tuple-element.31.share, f32[8,128,256]{2,1,0:T(8,128)S(1)} %get-tuple-element.32.grad, ...), custom_call_target="tpu_custom_call" | custom-call | tf_op jit(solution)/shard_map/reduce_terms/pallas_call | solution.py:506
  57.7 0.7 %store_outputs.1 = (bf16[512,128]{1,0:T(8,128)(2,1)}, bf16[512,128]{1,0:T(8,128)(2,1)}, bf16[128,128]{1,0:T(8,128)(2,1)}, bf16[128,128]{1,0:T(8,128)(2,1)}) custom-call(bf16[512,128]{1,0:T(8,128)(2,1)S(1)} %get-tuple-element.34.refs_0_, bf16[512,128]{1,0:T(8,128)(2,1)S(1)} %get-tuple-element.35.refs_1_, bf16[128,128]{1,0:T(8,128)(2,1)S(1)} %get-tuple-element.36.refs_2_, ...), custom_call_target="tpu_custom_call" | custom-call | tf_op jit(solution)/shard_map/store_outputs/pallas_call | solution.py:543

commit v4 on v3

--- a/solution.py
+++ b/solution.py
@@ -1,3 +1,4 @@
+import functools
 import math
 
 import jax
@@ -18,7 +19,8 @@
 QRUNS = NY * 2
 TILE = 4
 SPANS = 128
-ITEMS = QRUNS * (KRUNS // TILE)
+ITEMS = QRUNS * (KRUNS // TILE - 1)
+UNROLL = 4
 DOCS = 8
 NEGATIVE = -1e30
 FLOOR = -1e29
@@ -66,7 +68,9 @@
     rank = jnp.where(has > 0, before, -1)
     hit = jnp.where(rank == lax.broadcasted_iota(jnp.int32, (SPANS, 1), 0), 1.0, 0.0).astype(BF16)
     row = lax.broadcasted_iota(jnp.int32, (8, 1), 0)
-    found = jnp.where(row == 0, lane, jnp.where(row == 1, which, 0)).astype(F32).astype(BF16)
+    block, half = which % (XLO * NZ), which // (XLO * NZ)
+    found = jnp.where(row == 0, lane, jnp.where(row == 1, block, jnp.where(row == 6, half, 0)))
+    found = found.astype(F32).astype(BF16)
     sorted_runs = lax.dot_general(found, hit, (((1,), (1,)), ((), ())), preferred_element_type=F32)
     sorted_runs = jnp.where((row == 0) & (lane >= KRUNS), F32(FAR // RUN), sorted_runs).astype(jnp.int32)
     q_rows = [bal[pl.ds((xl * NY + i) * NZ + z, 1), :] for i in range(NY)]
@@ -86,8 +90,20 @@
     tiles = jnp.maximum((high_run - low_run + TILE - 1) // TILE, 1)
     own_lane = lax.broadcasted_iota(jnp.int32, (QRUNS, 1), 0) == lane
     low_row = jnp.sum(jnp.where(own_lane, low_run, 0), axis=0, keepdims=True)
-    tiles_row = jnp.sum(jnp.where(own_lane, tiles, 0), axis=0, keepdims=True)
-    tab[...] = jnp.where(row == 2, low_row, jnp.where(row == 3, tiles_row, sorted_runs))
+    more = tiles - 1
+    upper = lax.broadcasted_iota(jnp.int32, (QRUNS, 1), 0) >= lax.broadcasted_iota(jnp.int32, (1, SPANS), 1)
+    more_row = jnp.sum(jnp.where(own_lane, more, 0), axis=0, keepdims=True)
+    ends = jnp.sum(jnp.where(upper, more_row, 0), axis=1, keepdims=True)
+    passed = lane >= ends
+    run_row = jnp.minimum(jnp.sum(jnp.where(passed, 1, 0), axis=0, keepdims=True), QRUNS - 1)
+    tile_row = lane + 1 - jnp.sum(jnp.where(passed, more, 0), axis=0, keepdims=True)
+    count = jnp.sum(more, axis=0, keepdims=True)
+    tile_row = jnp.where(lane >= count, KRUNS // TILE, tile_row)
+    values = [None, None, low_row, run_row, tile_row, jnp.where(lane == 0, count, 0)]
+    out = sorted_runs
+    for i in range(2, 6):
+        out = jnp.where(row == i, values[i], out)
+    tab[...] = out
 
 
 def gather_kernel(
@@ -192,7 +208,7 @@
         gather_kernel,
         out_shape=(
             jax.ShapeDtypeStruct((NY, 2, 2 * ROWS, DH), BF16),
-            jax.ShapeDtypeStruct((XLO * NZ, 2, BLK, DH), BF16),
+            jax.ShapeDtypeStruct((XLO * NZ, 2, 2, RUN, DH), BF16),
             jax.ShapeDtypeStruct((8, SPANS), jnp.int32),
             jax.ShapeDtypeStruct((2, QRUNS, ROWS), jnp.int32),
         ),
@@ -210,19 +226,11 @@
 
 def tile_runs(tab, low_run, t):
     runs = [low_run + t * TILE + u for u in range(TILE)]
-    return [tab[1, r] for r in runs], [tab[0, r] * RUN for r in runs]
-
-
-def run_rows(index):
-    return index % (XLO * NZ), pl.ds(pl.multiple_of(index // (XLO * NZ) * RUN, RUN), RUN)
+    return [(tab[1, r], tab[6, r]) for r in runs], [tab[0, r] * RUN for r in runs]
 
 
 def tile_rows(kg, indices, part):
-    pieces = []
-    for index in indices:
-        block, rows = run_rows(index)
-        pieces.append(kg[block, part, rows, :])
-    return jnp.concatenate(pieces, axis=0)
+    return jnp.concatenate([kg[block, part, half] for block, half in indices], axis=0)
 
 
 def masked_scores(k, q, places, pos, start):
@@ -235,22 +243,60 @@
     return jnp.concatenate(parts, axis=0)
 
 
-def each_item(tab, process):
-    total = sum(tab[3, i] for i in range(QRUNS))
-
-    def step(i, state):
-        q_run, t = state
-        for u in range(2):
-            process(q_run, t, 2 * i + u)
-            more = (t + 1 < tab[3, q_run]) | (q_run == QRUNS - 1)
-            q_run, t = jnp.where(more, q_run, q_run + 1), jnp.where(more, t + 1, 0)
-        return q_run, t
-
-    lax.fori_loop(0, (total + 1) // 2, step, (0, 0))
+def together(process, items):
+    for end in [process(*item) for item in items]:
+        end()
+
+
+def first_tiles(process):
+    def step(i, _):
+        together(process, [(UNROLL * i + u, 0, UNROLL * i + u) for u in range(UNROLL)])
+        return 0
+
+    lax.fori_loop(0, QRUNS // UNROLL, step, 0)
+
+
+def further_tiles(tab, process):
+    def step(i, _):
+        slots = [UNROLL * i + u for u in range(UNROLL)]
+        together(process, [(tab[3, slot], tab[4, slot], slot) for slot in slots])
+        return 0
+
+    lax.fori_loop(0, (tab[5, 0] + UNROLL - 1) // UNROLL, step, 0)
 
 
 def query_rows(qg, q_run, part):
     return qg[q_run // 2, part, pl.ds(pl.multiple_of((q_run % 2) * ROWS, ROWS), ROWS), :]
+
+
+def forward_tile(tab, row_tab, qg, kg, held, held_gw, combine):
+    def process(q_run, t, slot):
+        at = pl.ds(q_run, 1)
+        indices, places = tile_runs(tab, tab[2, q_run], t)
+        s = masked_scores(
+            tile_rows(kg, indices, 0), query_rows(qg, q_run, 0), places, row_tab[0, at, :], row_tab[1, at, :]
+        )
+        held[slot] = s
+        v = tile_rows(kg, indices, 1)
+        gw = lax.dot_general(
+            v, query_rows(qg, q_run, 1), (((1,), (1,)), ((), ())), preferred_element_type=F32
+        )
+        held_gw[slot] = gw
+        top = jnp.maximum(jnp.max(s, axis=0, keepdims=True), FLOOR)
+        raw = jnp.exp2(s - top)
+        total = jnp.sum(raw, axis=0, keepdims=True)
+        inner = jnp.sum(raw * gw, axis=0, keepdims=True)
+        acc = lax.dot_general(v, raw.astype(BF16), (((0,), (0,)), ((), ())), preferred_element_type=F32)
+        return lambda: combine(q_run, top, total, inner, acc)
+
+    return process
+
+
+def combined(old, old_acc, top, total, inner, acc):
+    new_top = jnp.maximum(old[0], top)
+    old_share, share = jnp.exp2(old[0] - new_top), jnp.exp2(top - new_top)
+    stats = new_top, old[1] * old_share + total * share, old[2] * old_share + inner * share
+    return stats, old_acc * old_share + acc * share
 
 
 def forward_kernel(tab, row_tab, qg, kg, stats, out, held, held_gw):
@@ -259,32 +305,13 @@
     stats[2] = jnp.zeros((QRUNS, ROWS), F32)
     out[...] = jnp.zeros_like(out)
 
-    def process(q_run, t, item):
+    def combine(q_run, *new):
         at = pl.ds(q_run, 1)
-        indices, places = tile_runs(tab, tab[2, q_run], t)
-        s = masked_scores(
-            tile_rows(kg, indices, 0), query_rows(qg, q_run, 0), places, row_tab[0, at, :], row_tab[1, at, :]
-        )
-        held[item] = s
-        v = tile_rows(kg, indices, 1)
-        gw = lax.dot_general(
-            v, query_rows(qg, q_run, 1), (((1,), (1,)), ((), ())), preferred_element_type=F32
-        )
-        held_gw[item] = gw
-        top = jnp.maximum(jnp.max(s, axis=0, keepdims=True), FLOOR)
-        raw = jnp.exp2(s - top)
-        total = jnp.sum(raw, axis=0, keepdims=True)
-        inner = jnp.sum(raw * gw, axis=0, keepdims=True)
-        acc = lax.dot_general(v, raw.astype(BF16), (((0,), (0,)), ((), ())), preferred_element_type=F32)
-        old_top = stats[0, at, :]
-        new_top = jnp.maximum(old_top, top)
-        old_share, share = jnp.exp2(old_top - new_top), jnp.exp2(top - new_top)
-        stats[0, at, :] = new_top
-        stats[1, at, :] = stats[1, at, :] * old_share + total * share
-        stats[2, at, :] = stats[2, at, :] * old_share + inner * share
-        out[q_run] = out[q_run] * old_share + acc * share
-
-    each_item(tab, process)
+        rows, out[q_run] = combined([stats[i, at, :] for i in range(3)], out[q_run], *new)
+        for i in range(3):
+            stats[i, at, :] = rows[i]
+
+    further_tiles(tab, forward_tile(tab, row_tab, qg, kg, held, held_gw, combine))
 
 
 def forward(tab, row_tab, qg, kg):
@@ -305,11 +332,20 @@
     )(tab, row_tab, qg, kg)
 
 
-def exchange_kernel(mine, out, lsem, send, recv):
+def exchange_kernel(tab, row_tab, qg, kg, part, part_acc, out, acc_out, held, held_gw, mine, lsem, send, recv):
     h, xl, y, z = here()
     x = h * XLO + xl
     targets = [device(x, (y + d) % NY, z) for d in range(1, NY)]
-    greet(targets)()
+    meet = greet(targets)
+
+    def combine(q_run, *new):
+        at = pl.ds(q_run, 1)
+        rows, acc_out[q_run] = combined([part[i, at, :] for i in range(3)], part_acc[q_run], *new)
+        for i in range(3):
+            mine[i, at, :] = rows[i]
+
+    first_tiles(forward_tile(tab, row_tab, qg, kg, held, held_gw, combine))
+    meet()
     copies = []
     for d, target in enumerate(targets):
         copy = remote(mine, out.at[y], send.at[d], recv.at[d], target)
@@ -322,22 +358,28 @@
         copy.wait()
 
 
-def exchange(stats):
+def exchange(tab, row_tab, qg, kg, part, part_acc):
+    smem = pl.BlockSpec(memory_space=pltpu.SMEM)
     vmem = pl.BlockSpec(memory_space=pltpu.VMEM)
     dma = pltpu.SemaphoreType.DMA
     return pl.pallas_call(
         exchange_kernel,
-        out_shape=jax.ShapeDtypeStruct((NY,) + stats.shape, F32),
-        in_specs=[vmem],
-        out_specs=vmem,
-        scratch_shapes=[dma, dma((NY - 1,)), dma((NY - 1,))],
-        compiler_params=pltpu.CompilerParams(collective_id=1, has_side_effects=True, vmem_limit_bytes=1 << 20),
+        out_shape=(
+            jax.ShapeDtypeStruct((NY,) + part.shape, F32),
+            jax.ShapeDtypeStruct(part_acc.shape, F32),
+            jax.ShapeDtypeStruct((QRUNS, TILE * RUN, ROWS), F32),
+            jax.ShapeDtypeStruct((QRUNS, TILE * RUN, ROWS), F32),
+        ),
+        in_specs=[smem] + [vmem] * 5,
+        out_specs=(vmem,) * 4,
+        scratch_shapes=[pltpu.VMEM(part.shape, F32), dma, dma((NY - 1,)), dma((NY - 1,))],
+        compiler_params=pltpu.CompilerParams(collective_id=1, has_side_effects=True, vmem_limit_bytes=8 << 20),
         name="exchange_stats",
-    )(stats)
+    )(tab, row_tab, qg, kg, part, part_acc)
 
 
 def backward_kernel(
-    tab, qg, kg, stats, held, held_gw, share_out, grad_acc, kv_acc, row_stats
+    tab, qg, kg, stats, held, held_gw, more, more_gw, share_out, grad_acc, kv_acc, row_stats
 ):
     y = here()[2]
     kv_acc[...] = jnp.zeros_like(kv_acc)
@@ -350,26 +392,30 @@
     row_stats[1] = sum(stats[i, 2] * shares[i] for i in range(NY)) / total
     share_out[...] = jnp.exp2(stats[y, 0] - log_total)
 
-    def process(q_run, t, item):
+    def process(held, held_gw, q_run, t, slot):
         at = pl.ds(q_run, 1)
         indices, _ = tile_runs(tab, tab[2, q_run], t)
-        weights = jnp.exp2(held[item] - row_stats[0, at, :])
-        gs = (weights * (held_gw[item] - row_stats[1, at, :])).astype(BF16)
+        weights = jnp.exp2(held[slot] - row_stats[0, at, :])
+        gs = (weights * (held_gw[slot] - row_stats[1, at, :])).astype(BF16)
         value_part = jnp.dot(weights.astype(BF16), query_rows(qg, q_run, 1), preferred_element_type=F32)
         key_part = jnp.dot(gs, query_rows(qg, q_run, 0), preferred_element_type=F32)
         grad = lax.dot_general(
             tile_rows(kg, indices, 0), gs, (((0,), (0,)), ((), ())), preferred_element_type=F32
         )
-        for u, index in enumerate(indices):
-            block, to = run_rows(index)
-            kv_acc[1, block, to, :] += value_part[u * RUN : (u + 1) * RUN]
-            kv_acc[0, block, to, :] += key_part[u * RUN : (u + 1) * RUN]
-        grad_acc[q_run] += grad
-
-    each_item(tab, process)
-
-
-def backward(tab, qg, kg, stats, held, held_gw):
+
+        def end():
+            for u, (block, half) in enumerate(indices):
+                kv_acc[1, block, half] += value_part[u * RUN : (u + 1) * RUN]
+                kv_acc[0, block, half] += key_part[u * RUN : (u + 1) * RUN]
+            grad_acc[q_run] += grad
+
+        return end
+
+    first_tiles(functools.partial(process, held, held_gw))
+    further_tiles(tab, functools.partial(process, more, more_gw))
+
+
+def backward(tab, qg, kg, stats, held, held_gw, more, more_gw):
     smem = pl.BlockSpec(memory_space=pltpu.SMEM)
     vmem = pl.BlockSpec(memory_space=pltpu.VMEM)
     return pl.pallas_call(
@@ -377,31 +423,32 @@
         out_shape=(
             jax.ShapeDtypeStruct((QRUNS, ROWS), F32),
             jax.ShapeDtypeStruct((QRUNS, DH, ROWS), F32),
-            jax.ShapeDtypeStruct((2, XLO * NZ, BLK, DH), F32),
+            jax.ShapeDtypeStruct((2, XLO * NZ, 2, RUN, DH), F32),
         ),
-        in_specs=[smem] + [vmem] * 5,
+        in_specs=[smem] + [vmem] * 7,
         out_specs=(vmem,) * 3,
         scratch_shapes=[pltpu.VMEM((2, QRUNS, ROWS), F32)],
         compiler_params=pltpu.CompilerParams(vmem_limit_bytes=8 << 20),
         name="backward_terms",
-    )(tab, qg, kg, stats, held, held_gw)
-
-
-AHEAD = (4, 3, 2, 1)
-BEHIND = (5, 6, 7, 0)
+    )(tab, qg, kg, stats, held, held_gw, more, more_gw)
+
+
+AHEAD = (4, 3, 2)
+BEHIND = (5, 6)
+LATE = AHEAD + BEHIND
 
 
 def reduce_kernel(
     acc, share, grad, kv, att, qgrad, kgrad, vgrad,
-    rows, ybuf, ysum, xout, xbuf, xsum, zsum, zbuf, last,
-    ysend, yrecv, xsend, xrecv, zsend, zrecv, hsend, hrecv,
+    rows, ybuf, ysum, nout, nbuf, oout, obuf, xout, xbuf, xsum, zsum, zbuf, last,
+    ysend, yrecv, nsend, nrecv, osend, orecv, xsend, xrecv, zsend, zrecv, hsend, hrecv,
 ):
     h, xl, y, z = here()
     x = h * XLO + xl
     y_up, y_dn = device(x, (y + 1) % NY, z), device(x, (y + NY - 1) % NY, z)
-    x_to = tuple(device((x + d) % NX, y, z) for d in (1, NX - 1, 2))
-    z_all = [device(x, y, (z + d) % NZ) for d in range(1, NZ)]
-    meet = greet([y_up, y_dn, *x_to, *z_all])
+    x_to = tuple(device((x + d) % NX, y, z) for d in (1, 2, 3))
+    z_to = {d: device(x, y, (z + d) % NZ) for d in range(1, NZ)}
+    meet = greet([*z_to.values(), x_to[1], x_to[0], x_to[2], y_up, y_dn])
     started = []
 
     def go(copy):
@@ -409,11 +456,17 @@
         started.append(copy)
         return copy
 
+    def scaled(part, block):
+        return kv[part, block] * jnp.where(part == 0, F32(SCALING), F32(1.0))
+
     def term(step, offset):
         ring = (x + step) % NX
-        part = ring // XLO
-        block = kv[part, (ring % XLO) * NZ + (z + offset) % NZ]
-        return block * jnp.where(part == 0, F32(SCALING), F32(1.0))
+        return scaled(ring // XLO, (ring % XLO) * NZ + (z + offset) % NZ)
+
+    def near_term(step):
+        ring = (x + step) % NX
+        sides = [nbuf[side, ring % XLO, ring // XLO].astype(F32) for side in (0, 1)]
+        return term(step, 0) + sides[0] + sides[1]
 
     def put_rows(yy):
         for half in (0, 1):
@@ -423,74 +476,90 @@
             rows[yy, 1, to, :] = (grad[q_run] * SCALING).T.astype(BF16)
 
     def x_copy(kind, way, i, src):
-        return go(remote(src, xbuf.at[kind, way, i], xsend.at[kind, way, i], xrecv.at[kind, way, i], x_to[way]))
+        target = x_to[0] if way == 0 else x_to[2]
+        return go(remote(src, xbuf.at[kind, way, i], xsend.at[kind, way, i], xrecv.at[kind, way, i], target))
 
     offsets = (AHEAD, BEHIND)
     sent = {}
-    for i in range(4):
+    for side, offset in ((0, 1), (1, NZ - 1)):
+        for lo in range(XLO):
+            for part in (0, 1):
+                nout[side, lo, part] = scaled(part, lo * NZ + (z + offset) % NZ).astype(BF16)
+    for way in (0, 1):
+        for i, offset in enumerate(offsets[way]):
+            xout[0, way, i] = term(2, offset).astype(BF16)
+    meet()
+    near = []
+    for lo in range(XLO):
+        for side, offset in ((0, 1), (1, NZ - 1)):
+            sems = nsend.at[side, lo], nrecv.at[side, lo]
+            near.append(go(remote(nout.at[side, lo], nbuf.at[side, lo], *sems, z_to[offset])))
+    for i in range(len(AHEAD)):
         for way in (0, 1):
-            xout[0, way, i] = term(2, offsets[way][i]).astype(BF16)
-    meet()
-    for i in range(4):
-        for way in (0, 1):
-            sent[0, way, i] = x_copy(0, way, i, xout.at[0, way, i])
+            if i < len(offsets[way]):
+                sent[0, way, i] = x_copy(0, way, i, xout.at[0, way, i])
     y_far, y_next, y_prev = (y + 2) % NY, (y + 1) % NY, (y + NY - 1) % NY
     put_rows(y_far)
     y_a = go(remote(rows.at[y_far, 0], ybuf.at[0], ysend.at[0], yrecv.at[0], y_up))
     y_b = go(remote(rows.at[y_far, 1], ybuf.at[1], ysend.at[1], yrecv.at[1], y_dn))
-    for i in range(4):
+    for i in range(len(AHEAD)):
         for way in (0, 1):
-            xout[1, way, i] = term(1 if way == 0 else 3, offsets[1 - way][i]).astype(BF16)
-            sent[1, way, i] = x_copy(1, way, i, xout.at[1, way, i])
+            if i < len(offsets[1 - way]):
+                xout[1, way, i] = term(1 if way == 0 else 3, offsets[1 - way][i]).astype(BF16)
+                sent[1, way, i] = x_copy(1, way, i, xout.at[1, way, i])
     put_rows(y_next)
     put_rows(y_prev)
     y_c = go(remote(rows.at[y_next, 1], ybuf.at[2], ysend.at[2], yrecv.at[2], y_up))
     y_d = go(remote(rows.at[y_prev, 0], ybuf.at[3], ysend.at[3], yrecv.at[3], y_dn))
-    for i in range(4):
+    for i in range(len(AHEAD)):
         for way in (0, 1):
-            sent[0, way, i].wait_recv()
-            own = term(1 if way == 0 else 3, offsets[way][i])
-            xsum[way, i] = (xbuf[0, way, i].astype(F32) + own).astype(BF16)
-            sent[2, way, i] = x_copy(2, way, i, xsum.at[way, i])
+            if i < len(offsets[way]):
+                sent[0, way, i].wait_recv()
+                own = term(1 if way == 0 else 3, offsets[way][i])
+                xsum[way, i] = (xbuf[0, way, i].astype(F32) + own).astype(BF16)
+                sent[2, way, i] = x_copy(2, way, i, xsum.at[way, i])
+    for copy in near:
+        copy.wait_recv()
+    across = []
+    for step in (2, 1, 3):
+        oout[step - 1] = near_term(step).astype(BF16)
+        sems = osend.at[step - 1], orecv.at[step - 1]
+        across.append(go(remote(oout.at[step - 1], obuf.at[step - 1], *sems, x_to[step - 1])))
+    z_copies = []
+    for i in range(len(AHEAD)):
+        for way in (0, 1):
+            if i < len(offsets[way]):
+                sent[2, way, i].wait_recv()
+                sent[1, 1 - way, i].wait_recv()
+                offset = offsets[way][i]
+                slot = LATE.index(offset)
+                block = term(0, offset) + xbuf[2, way, i].astype(F32) + xbuf[1, 1 - way, i].astype(F32)
+                zsum[slot] = block.astype(BF16)
+                sems = zsend.at[slot], zrecv.at[slot]
+                z_copies.append(go(remote(zsum.at[slot], zbuf.at[slot], *sems, z_to[offset])))
     y_a.wait_recv()
     ysum[0] = (ybuf[0].astype(F32) + rows[y_next, 0].astype(F32)).astype(BF16)
     y_e = go(remote(ysum.at[0], ybuf.at[4], ysend.at[4], yrecv.at[4], y_up))
     y_b.wait_recv()
     ysum[1] = (ybuf[1].astype(F32) + rows[y_prev, 1].astype(F32)).astype(BF16)
     y_f = go(remote(ysum.at[1], ybuf.at[5], ysend.at[5], yrecv.at[5], y_dn))
-    total = None
-    z_copies = []
-    for i in range(4):
-        for way in (0, 1):
-            sent[2, way, i].wait_recv()
-            sent[1, 1 - way, i].wait_recv()
-            offset = offsets[way][i]
-            block = term(0, offset) + xbuf[2, way, i].astype(F32) + xbuf[1, 1 - way, i].astype(F32)
-            if offset == 0:
-                total = block
-            else:
-                zsum[offset - 1] = block.astype(BF16)
-                z_copies.append(
-                    go(
-                        remote(
-                            zsum.at[offset - 1], zbuf.at[offset - 1],
-                            zsend.at[offset - 1], zrecv.at[offset - 1], z_all[offset - 1],
-                        )
-                    )
-                )
     put_rows(y)
+    total = near_term(0)
+    for copy in across:
+        copy.wait_recv()
+    total = total + obuf[0].astype(F32) + obuf[1].astype(F32) + obuf[2].astype(F32)
+    for copy in z_copies:
+        copy.wait_recv()
+    for slot in range(len(LATE)):
+        total = total + zbuf[slot].astype(F32)
+    last[0] = total.astype(BF16)
+    final = go(remote(last.at[0], last.at[1], hsend, hrecv, x_to[1]))
     y_d.wait_recv()
     y_e.wait_recv()
     att[...] = (rows[y, 0].astype(F32) + ybuf[3].astype(F32) + ybuf[4].astype(F32)).astype(BF16)
     y_c.wait_recv()
     y_f.wait_recv()
     qgrad[...] = (rows[y, 1].astype(F32) + ybuf[2].astype(F32) + ybuf[5].astype(F32)).astype(BF16)
-    for copy in z_copies:
-        copy.wait_recv()
-    for d in range(NZ - 1):
-        total = total + zbuf[d].astype(F32)
-    last[0] = total.astype(BF16)
-    final = go(remote(last.at[0], last.at[1], hsend, hrecv, x_to[2]))
     final.wait_recv()
     mine, other = last[0], last[1]
     kgrad[...] = jnp.where(h == 0, mine, other)
@@ -503,6 +572,7 @@
     vmem = pl.BlockSpec(memory_space=pltpu.VMEM)
     dma = pltpu.SemaphoreType.DMA
     block = (BLK, DH)
+    late = len(LATE)
     return pl.pallas_call(
         reduce_kernel,
         out_shape=(
@@ -517,15 +587,20 @@
             pltpu.VMEM((NY, 2, 2 * ROWS, DH), BF16),
             pltpu.VMEM((6, 2 * ROWS, DH), BF16),
             pltpu.VMEM((2, 2 * ROWS, DH), BF16),
-            pltpu.VMEM((2, 2, 4) + block, BF16),
-            pltpu.VMEM((3, 2, 4) + block, BF16),
-            pltpu.VMEM((2, 4) + block, BF16),
-            pltpu.VMEM((NZ - 1,) + block, BF16),
-            pltpu.VMEM((NZ - 1,) + block, BF16),
+            pltpu.VMEM((2, XLO, 2) + block, BF16),
+            pltpu.VMEM((2, XLO, 2) + block, BF16),
+            pltpu.VMEM((3,) + block, BF16),
+            pltpu.VMEM((3,) + block, BF16),
+            pltpu.VMEM((2, 2, 3) + block, BF16),
+            pltpu.VMEM((3, 2, 3) + block, BF16),
+            pltpu.VMEM((2, 3) + block, BF16),
+            pltpu.VMEM((late,) + block, BF16),
+            pltpu.VMEM((late,) + block, BF16),
             pltpu.VMEM((2,) + block, BF16),
-            dma((6,)), dma((6,)), dma((3, 2, 4)), dma((3, 2, 4)), dma((NZ - 1,)), dma((NZ - 1,)), dma, dma,
+            dma((6,)), dma((6,)), dma((2, XLO)), dma((2, XLO)), dma((3,)), dma((3,)),
+            dma((3, 2, 3)), dma((3, 2, 3)), dma((late,)), dma((late,)), dma, dma,
         ],
-        compiler_params=pltpu.CompilerParams(collective_id=2, has_side_effects=True, vmem_limit_bytes=8 << 20),
+        compiler_params=pltpu.CompilerParams(collective_id=2, has_side_effects=True, vmem_limit_bytes=10 << 20),
         name="reduce_terms",
     )(acc, share, grad, kv)
 
@@ -555,10 +630,17 @@
     flat = (2 * ROWS, DH)
     bal = balance.reshape(SPANS // 2, BLK)
     qg, kg, tab, row_tab = gather(
-        queries.reshape(flat), out_grad.reshape(flat), key_rows, value_rows, bal, doc_lengths
+        queries.reshape(flat),
+        out_grad.reshape(flat),
+        key_rows.reshape(2, RUN, DH),
+        value_rows.reshape(2, RUN, DH),
+        bal,
+        doc_lengths,
     )
-    own, acc, held, held_gw = forward(tab, row_tab, qg, kg)
-    share, grad, kv = backward(tab, qg, kg, exchange(own), held, held_gw)
+    part, part_acc, more, more_gw = forward(tab, row_tab, qg, kg)
+    stats, acc, held, held_gw = exchange(tab, row_tab, qg, kg, part, part_acc)
+    share, grad, kv = backward(tab, qg, kg, stats, held, held_gw, more, more_gw)
+    kv = kv.reshape(2, XLO * NZ, BLK, DH)
     attended, query_grad, key_grad, value_grad = store(*reduce(acc, share, grad, kv))
     return attended.reshape(queries.shape), query_grad.reshape(queries.shape), key_grad, value_grad
 

time: 58.5 us -> 55.3 us (0.945); the launches traced: 58.4 us -> 54.6 us
  Pallas kernels: 57.7 us -> 53.9 us
    pallas_call x1, Pallas kernels: 4.26 us -> 1.69 us  [forward(): pl.pallas_call(forward_kernel, out_shape=(jax.ShapeDtypeStruct((3, QRUNS,...]
    pallas_call x1, Pallas kernels: 22.2 us -> 20.4 us  [reduce(): pl.pallas_call(reduce_kernel, out_shape=(jax.ShapeDtypeStruct((2 * ROWS,...]
    pallas_call x1, Pallas kernels: 5.84 us -> 6.84 us  [exchange(): pl.pallas_call(exchange_kernel, out_shape=(jax.ShapeDtypeStruct((NY,) + p...]
where the time goes in v4:
time: 55.3 us; the launch traced here: 54.6 us
  Pallas kernels  53.9 us (97%)
  between operations  0.67 us (1%)
    pallas_call x1, Pallas kernels, gather(): pl.pallas_call(gather_kernel, out_shape=(jax.ShapeDtypeStruct((NY, 2, 2 *...  21.7 us
    pallas_call x1, Pallas kernels, reduce(): pl.pallas_call(reduce_kernel, out_shape=(jax.ShapeDtypeStruct((2 * ROWS,...  20.4 us
    pallas_call x1, Pallas kernels, exchange(): pl.pallas_call(exchange_kernel, out_shape=(jax.ShapeDtypeStruct((NY,) + p...  6.84 us
    pallas_call x1, Pallas kernels, backward(): pl.pallas_call(backward_kernel, out_shape=(jax.ShapeDtypeStruct((QRUNS, R...  2.53 us
    pallas_call x1, Pallas kernels, forward(): pl.pallas_call(forward_kernel, out_shape=(jax.ShapeDtypeStruct((3, QRUNS,...  1.69 us

profile of v4, /device:TPU:2, one launch (start us, length us, event | category | flops | bytes accessed | tf_op | source)
XLA Modules:
  0.0 54.6 jit_solution(9393555926160276455)
XLA Ops:
  0.6 21.7 %gather_rows.1 = (bf16[4,2,512,128]{3,2,1,0:T(8,128)(2,1)S(1)}, bf16[16,2,2,64,128]{4,3,2,1,0:T(8,128)(2,1)S(1)}, s32[8,128]{1,0:T(8,128)S(1)}, s32[2,8,256]{2,1,0:T(8,128)S(1)}) custom-call(bf16[512,128]{1,0:T(8,128)(2,1)} %bitcast.9, bf16[512,128]{1,0:T(8,128)(2,1)} %bitcast.10, bf16[2,64,128]{2,1,0:T(8,128)(2,1)} %bitcast.11, ...), custom_call_target="tpu_custom_call" | custom-call | tf_op jit(solution)/shard_map/gather_rows/pallas_call | solution.py:207
  22.4 1.7 %forward_stats.1 = (f32[3,8,256]{2,1,0:T(8,128)S(1)}, f32[8,128,256]{2,1,0:T(8,128)S(1)}, f32[56,256,256]{2,1,0:T(8,128)S(1)}, f32[56,256,256]{2,1,0:T(8,128)S(1)}) custom-call(s32[8,128]{1,0:T(8,128)S(1)} %get-tuple-element.27.tab, s32[2,8,256]{2,1,0:T(8,128)S(1)} %get-tuple-element.28.row_tab, bf16[4,2,512,128]{3,2,1,0:T(8,128)(2,1)S(1)} %get-tuple-element.29.qg, ...), custom_call_target="tpu_custom_call" | custom-call | tf_op jit(solution)/shard_map/forward_stats/pallas_call | solution.py:320
  24.1 6.8 %exchange_stats.1 = (f32[4,3,8,256]{3,2,1,0:T(8,128)S(1)}, f32[8,128,256]{2,1,0:T(8,128)S(1)}, f32[8,256,256]{2,1,0:T(8,128)S(1)}, f32[8,256,256]{2,1,0:T(8,128)S(1)}) custom-call(s32[8,128]{1,0:T(8,128)S(1)} %get-tuple-element.27.tab, s32[2,8,256]{2,1,0:T(8,128)S(1)} %get-tuple-element.28.row_tab, bf16[4,2,512,128]{3,2,1,0:T(8,128)(2,1)S(1)} %get-tuple-element.29.qg, ...), custom_call_target="tpu_custom_call" | custom-call | tf_op jit(solution)/shard_map/exchange_stats/pallas_call | solution.py:365
  30.9 2.5 %backward_terms.1 = (f32[8,256]{1,0:T(8,128)S(1)}, f32[8,128,256]{2,1,0:T(8,128)S(1)}, f32[2,16,2,64,128]{4,3,2,1,0:T(8,128)S(1)}) custom-call(s32[8,128]{1,0:T(8,128)S(1)} %get-tuple-element.27.tab, bf16[4,2,512,128]{3,2,1,0:T(8,128)(2,1)S(1)} %get-tuple-element.29.qg, bf16[16,2,2,64,128]{4,3,2,1,0:T(8,128)(2,1)S(1)} %get-tuple-element.30.kg, ...), custom_call_target="tpu_custom_call" | custom-call | tf_op jit(solution)/shard_map/backward_terms/pallas_call | solution.py:421
  33.5 20.4 %reduce_terms.1 = (bf16[512,128]{1,0:T(8,128)(2,1)S(1)}, bf16[512,128]{1,0:T(8,128)(2,1)S(1)}, bf16[128,128]{1,0:T(8,128)(2,1)S(1)}, bf16[128,128]{1,0:T(8,128)(2,1)S(1)}) custom-call(f32[8,128,256]{2,1,0:T(8,128)S(1)} %get-tuple-element.33.acc, f32[8,256]{1,0:T(8,128)S(1)} %get-tuple-element.39.share, f32[8,128,256]{2,1,0:T(8,128)S(1)} %get-tuple-element.40.grad, ...), custom_call_target="tpu_custom_call" | custom-call | tf_op jit(solution)/shard_map/reduce_terms/pallas_call | solution.py:576
  53.8 0.7 %store_outputs.1 = (bf16[512,128]{1,0:T(8,128)(2,1)}, bf16[512,128]{1,0:T(8,128)(2,1)}, bf16[128,128]{1,0:T(8,128)(2,1)}, bf16[128,128]{1,0:T(8,128)(2,1)}) custom-call(bf16[512,128]{1,0:T(8,128)(2,1)S(1)} %get-tuple-element.42.refs_0_, bf16[512,128]{1,0:T(8,128)(2,1)S(1)} %get-tuple-element.43.refs_1_, bf16[128,128]{1,0:T(8,128)(2,1)S(1)} %get-tuple-element.44.refs_2_, ...), custom_call_target="tpu_custom_call" | custom-call | tf_op jit(solution)/shard_map/store_outputs/pallas_call | solution.py:618

commit v5 on v4

--- a/solution.py
+++ b/solution.py
@@ -107,7 +107,7 @@
 
 
 def gather_kernel(
-    q_ref, g_ref, k_ref, v_ref, bal_ref, len_ref, qg, kg, tab, row_tab, bal, lengths, lsem, ysend, yrecv, zsend, zrecv, xsend, xrecv
+    q_ref, g_ref, k_ref, v_ref, bal_ref, len_ref, qg, kg, tab, row_tab, zeros_acc, zeros_grad, zeros_kv, bal, lengths, lsem, ysend, yrecv, zsend, zrecv, xsend, xrecv
 ):
     h, xl, y, z = here()
     x = h * XLO + xl
@@ -166,6 +166,8 @@
     for copy in own_tab:
         copy.wait()
     tables(bal, lengths, tab, row_tab, xl, y, z)
+    for ref in (zeros_acc, zeros_grad, zeros_kv):
+        ref[...] = jnp.zeros_like(ref)
     for part in (0, 1):
         for sign in (1, -1):
             sent_z[sign, 2, part].wait_recv()
@@ -200,6 +202,13 @@
         copy.wait()
 
 
+ZEROS = (
+    jax.ShapeDtypeStruct((QRUNS, DH, ROWS), F32),
+    jax.ShapeDtypeStruct((QRUNS, DH, ROWS), F32),
+    jax.ShapeDtypeStruct((2, XLO * NZ, 2, RUN, DH), F32),
+)
+
+
 def gather(q, g, k, v, bal, lengths):
     hbm = pl.BlockSpec(memory_space=pltpu.HBM)
     vmem = pl.BlockSpec(memory_space=pltpu.VMEM)
@@ -211,9 +220,10 @@
             jax.ShapeDtypeStruct((XLO * NZ, 2, 2, RUN, DH), BF16),
             jax.ShapeDtypeStruct((8, SPANS), jnp.int32),
             jax.ShapeDtypeStruct((2, QRUNS, ROWS), jnp.int32),
+            *ZEROS,
         ),
         in_specs=[hbm] * 6,
-        out_specs=(vmem,) * 4,
+        out_specs=(vmem,) * 7,
         scratch_shapes=[
             pltpu.VMEM((SPANS // 2, BLK), jnp.int32),
             pltpu.SMEM((DOCS,), jnp.int32),
@@ -299,11 +309,10 @@
     return stats, old_acc * old_share + acc * share
 
 
-def forward_kernel(tab, row_tab, qg, kg, stats, out, held, held_gw):
+def forward_kernel(tab, row_tab, qg, kg, zeros, stats, out, held, held_gw):
     stats[0] = jnp.full((QRUNS, ROWS), FLOOR, F32)
     stats[1] = jnp.zeros((QRUNS, ROWS), F32)
     stats[2] = jnp.zeros((QRUNS, ROWS), F32)
-    out[...] = jnp.zeros_like(out)
 
     def combine(q_run, *new):
         at = pl.ds(q_run, 1)
@@ -314,7 +323,7 @@
     further_tiles(tab, forward_tile(tab, row_tab, qg, kg, held, held_gw, combine))
 
 
-def forward(tab, row_tab, qg, kg):
+def forward(tab, row_tab, qg, kg, zeros):
     smem = pl.BlockSpec(memory_space=pltpu.SMEM)
     vmem = pl.BlockSpec(memory_space=pltpu.VMEM)
     return pl.pallas_call(
@@ -325,11 +334,12 @@
             jax.ShapeDtypeStruct((ITEMS, TILE * RUN, ROWS), F32),
             jax.ShapeDtypeStruct((ITEMS, TILE * RUN, ROWS), F32),
         ),
-        in_specs=[smem, vmem, vmem, vmem],
+        in_specs=[smem] + [vmem] * 4,
         out_specs=(vmem,) * 4,
+        input_output_aliases={4: 1},
         compiler_params=pltpu.CompilerParams(vmem_limit_bytes=8 << 20),
         name="forward_stats",
-    )(tab, row_tab, qg, kg)
+    )(tab, row_tab, qg, kg, zeros)
 
 
 def exchange_kernel(tab, row_tab, qg, kg, part, part_acc, out, acc_out, held, held_gw, mine, lsem, send, recv):
@@ -379,11 +389,9 @@
 
 
 def backward_kernel(
-    tab, qg, kg, stats, held, held_gw, more, more_gw, share_out, grad_acc, kv_acc, row_stats
+    tab, qg, kg, stats, held, held_gw, more, more_gw, zeros_grad, zeros_kv, share_out, grad_acc, kv_acc, row_stats
 ):
     y = here()[2]
-    kv_acc[...] = jnp.zeros_like(kv_acc)
-    grad_acc[...] = jnp.zeros_like(grad_acc)
     top = jnp.maximum(jnp.maximum(stats[0, 0], stats[1, 0]), jnp.maximum(stats[2, 0], stats[3, 0]))
     shares = [jnp.exp2(stats[i, 0] - top) for i in range(NY)]
     total = sum(stats[i, 1] * shares[i] for i in range(NY))
@@ -415,7 +423,7 @@
     further_tiles(tab, functools.partial(process, more, more_gw))
 
 
-def backward(tab, qg, kg, stats, held, held_gw, more, more_gw):
+def backward(tab, qg, kg, stats, held, held_gw, more, more_gw, zeros_grad, zeros_kv):
     smem = pl.BlockSpec(memory_space=pltpu.SMEM)
     vmem = pl.BlockSpec(memory_space=pltpu.VMEM)
     return pl.pallas_call(
@@ -425,12 +433,13 @@
             jax.ShapeDtypeStruct((QRUNS, DH, ROWS), F32),
             jax.ShapeDtypeStruct((2, XLO * NZ, 2, RUN, DH), F32),
         ),
-        in_specs=[smem] + [vmem] * 7,
+        in_specs=[smem] + [vmem] * 9,
         out_specs=(vmem,) * 3,
+        input_output_aliases={8: 1, 9: 2},
         scratch_shapes=[pltpu.VMEM((2, QRUNS, ROWS), F32)],
         compiler_params=pltpu.CompilerParams(vmem_limit_bytes=8 << 20),
         name="backward_terms",
-    )(tab, qg, kg, stats, held, held_gw, more, more_gw)
+    )(tab, qg, kg, stats, held, held_gw, more, more_gw, zeros_grad, zeros_kv)
 
 
 AHEAD = (4, 3, 2)
@@ -441,14 +450,25 @@
 def reduce_kernel(
     acc, share, grad, kv, att, qgrad, kgrad, vgrad,
     rows, ybuf, ysum, nout, nbuf, oout, obuf, xout, xbuf, xsum, zsum, zbuf, last,
-    ysend, yrecv, nsend, nrecv, osend, orecv, xsend, xrecv, zsend, zrecv, hsend, hrecv,
+    ysend, yrecv, nsend, nrecv, osend, orecv, xsend, xrecv, zsend, zrecv, hsend, hrecv, z_word, x_word, z_far_word,
 ):
     h, xl, y, z = here()
     x = h * XLO + xl
     y_up, y_dn = device(x, (y + 1) % NY, z), device(x, (y + NY - 1) % NY, z)
     x_to = tuple(device((x + d) % NX, y, z) for d in (1, 2, 3))
     z_to = {d: device(x, y, (z + d) % NZ) for d in range(1, NZ)}
-    meet = greet([*z_to.values(), x_to[1], x_to[0], x_to[2], y_up, y_dn])
+    z_near = ((0, z_to[1]), (1, z_to[NZ - 1]))
+    x_near = ((0, x_to[0]), (1, x_to[2]))
+    meet = greet([z_to[1], z_to[NZ - 1], x_to[0], x_to[2], y_up, y_dn])
+
+    def tell(sem, targets):
+        for side, target in targets:
+            pl.semaphore_signal(sem.at[side], inc=1, device_id=target, device_id_type=MESH)
+
+    def hear(sem):
+        for side in (0, 1):
+            pl.semaphore_wait(sem.at[side], 1)
+
     started = []
 
     def go(copy):
@@ -489,6 +509,8 @@
         for i, offset in enumerate(offsets[way]):
             xout[0, way, i] = term(2, offset).astype(BF16)
     meet()
+    tell(z_word, z_near)
+    tell(x_word, x_near)
     near = []
     for lo in range(XLO):
         for side, offset in ((0, 1), (1, NZ - 1)):
@@ -498,19 +520,17 @@
         for way in (0, 1):
             if i < len(offsets[way]):
                 sent[0, way, i] = x_copy(0, way, i, xout.at[0, way, i])
-    y_far, y_next, y_prev = (y + 2) % NY, (y + 1) % NY, (y + NY - 1) % NY
-    put_rows(y_far)
-    y_a = go(remote(rows.at[y_far, 0], ybuf.at[0], ysend.at[0], yrecv.at[0], y_up))
-    y_b = go(remote(rows.at[y_far, 1], ybuf.at[1], ysend.at[1], yrecv.at[1], y_dn))
     for i in range(len(AHEAD)):
         for way in (0, 1):
             if i < len(offsets[1 - way]):
                 xout[1, way, i] = term(1 if way == 0 else 3, offsets[1 - way][i]).astype(BF16)
                 sent[1, way, i] = x_copy(1, way, i, xout.at[1, way, i])
-    put_rows(y_next)
-    put_rows(y_prev)
-    y_c = go(remote(rows.at[y_next, 1], ybuf.at[2], ysend.at[2], yrecv.at[2], y_up))
-    y_d = go(remote(rows.at[y_prev, 0], ybuf.at[3], ysend.at[3], yrecv.at[3], y_dn))
+    y_far, y_next, y_prev = (y + 2) % NY, (y + 1) % NY, (y + NY - 1) % NY
+    put_rows(y_far)
+    y_a = go(remote(rows.at[y_far, 0], ybuf.at[0], ysend.at[0], yrecv.at[0], y_up))
+    y_b = go(remote(rows.at[y_far, 1], ybuf.at[1], ysend.at[1], yrecv.at[1], y_dn))
+    hear(z_word)
+    tell(z_far_word, ((0, z_to[2]), (1, z_to[NZ - 2])))
     for i in range(len(AHEAD)):
         for way in (0, 1):
             if i < len(offsets[way]):
@@ -520,12 +540,18 @@
                 sent[2, way, i] = x_copy(2, way, i, xsum.at[way, i])
     for copy in near:
         copy.wait_recv()
+    hear(x_word)
     across = []
     for step in (2, 1, 3):
         oout[step - 1] = near_term(step).astype(BF16)
         sems = osend.at[step - 1], orecv.at[step - 1]
         across.append(go(remote(oout.at[step - 1], obuf.at[step - 1], *sems, x_to[step - 1])))
+    put_rows(y_next)
+    put_rows(y_prev)
+    y_c = go(remote(rows.at[y_next, 1], ybuf.at[2], ysend.at[2], yrecv.at[2], y_up))
+    y_d = go(remote(rows.at[y_prev, 0], ybuf.at[3], ysend.at[3], yrecv.at[3], y_dn))
     z_copies = []
+    hear(z_far_word)
     for i in range(len(AHEAD)):
         for way in (0, 1):
             if i < len(offsets[way]):
@@ -573,6 +599,7 @@
     dma = pltpu.SemaphoreType.DMA
     block = (BLK, DH)
     late = len(LATE)
+    word = pltpu.SemaphoreType.REGULAR((2,))
     return pl.pallas_call(
         reduce_kernel,
         out_shape=(
@@ -598,7 +625,7 @@
             pltpu.VMEM((late,) + block, BF16),
             pltpu.VMEM((2,) + block, BF16),
             dma((6,)), dma((6,)), dma((2, XLO)), dma((2, XLO)), dma((3,)), dma((3,)),
-            dma((3, 2, 3)), dma((3, 2, 3)), dma((late,)), dma((late,)), dma, dma,
+            dma((3, 2, 3)), dma((3, 2, 3)), dma((late,)), dma((late,)), dma, dma, word, word, word,
         ],
         compiler_params=pltpu.CompilerParams(collective_id=2, has_side_effects=True, vmem_limit_bytes=10 << 20),
         name="reduce_terms",
@@ -629,7 +656,7 @@
 def body(queries, key_rows, value_rows, out_grad, doc_lengths, balance):
     flat = (2 * ROWS, DH)
     bal = balance.reshape(SPANS // 2, BLK)
-    qg, kg, tab, row_tab = gather(
+    qg, kg, tab, row_tab, zeros_acc, zeros_grad, zeros_kv = gather(
         queries.reshape(flat),
         out_grad.reshape(flat),
         key_rows.reshape(2, RUN, DH),
@@ -637,9 +664,11 @@
         bal,
         doc_lengths,
     )
-    part, part_acc, more, more_gw = forward(tab, row_tab, qg, kg)
+    part, part_acc, more, more_gw = forward(tab, row_tab, qg, kg, zeros_acc)
     stats, acc, held, held_gw = exchange(tab, row_tab, qg, kg, part, part_acc)
-    share, grad, kv = backward(tab, qg, kg, stats, held, held_gw, more, more_gw)
+    share, grad, kv = backward(
+        tab, qg, kg, stats, held, held_gw, more, more_gw, zeros_grad, zeros_kv
+    )
     kv = kv.reshape(2, XLO * NZ, BLK, DH)
     attended, query_grad, key_grad, value_grad = store(*reduce(acc, share, grad, kv))
     return attended.reshape(queries.shape), query_grad.reshape(queries.shape), key_grad, value_grad

time: 55.3 us -> 53.7 us (0.971); the launches traced: 54.6 us -> 53.6 us
  Pallas kernels: 53.9 us -> 53 us
    pallas_call x1, Pallas kernels: 1.69 us -> 0.62 us  [forward(): pl.pallas_call(forward_kernel, out_shape=(jax.ShapeDtypeStruct((3, QRUNS,...]
    pallas_call x1, Pallas kernels: 6.84 us -> 7.85 us  [exchange(): pl.pallas_call(exchange_kernel, out_shape=(jax.ShapeDtypeStruct((NY,) + p...]
    pallas_call x1, Pallas kernels: 2.53 us -> 1.74 us  [backward(): pl.pallas_call(backward_kernel, out_shape=(jax.ShapeDtypeStruct((QRUNS, R...]
where the time goes in v5:
time: 53.7 us; the launch traced here: 53.6 us
  Pallas kernels  53 us (99%)
  between operations  0.67 us (1%)
    pallas_call x1, Pallas kernels, gather(): pl.pallas_call(gather_kernel, out_shape=(jax.ShapeDtypeStruct((NY, 2, 2 *...  21.7 us
    pallas_call x1, Pallas kernels, reduce(): pl.pallas_call(reduce_kernel, out_shape=(jax.ShapeDtypeStruct((2 * ROWS,...  20.3 us
    pallas_call x1, Pallas kernels, exchange(): pl.pallas_call(exchange_kernel, out_shape=(jax.ShapeDtypeStruct((NY,) + p...  7.85 us
    pallas_call x1, Pallas kernels, backward(): pl.pallas_call(backward_kernel, out_shape=(jax.ShapeDtypeStruct((QRUNS, R...  1.74 us

profile of v5, /device:TPU:2, one launch (start us, length us, event | category | flops | bytes accessed | tf_op | source)
XLA Modules:
  0.0 53.6 jit_solution(14371957838962057824)
XLA Ops:
  0.6 21.7 %gather_rows.1 = (bf16[4,2,512,128]{3,2,1,0:T(8,128)(2,1)S(1)}, bf16[16,2,2,64,128]{4,3,2,1,0:T(8,128)(2,1)S(1)}, s32[8,128]{1,0:T(8,128)S(1)}, s32[2,8,256]{2,1...) custom-call(bf16[512,128]{1,0:T(8,128)(2,1)} %bitcast.9, ...), custom_call_target="tpu_custom_call" | custom-call | tf_op jit(solution)/shard_map/gather_rows/pallas_call | solution.py:216
  22.4 0.6 %forward_stats.1 = (f32[3,8,256]{2,1,0:T(8,128)S(1)}, f32[8,128,256]{2,1,0:T(8,128)S(1)}, f32[56,256,256]{2,1,0:T(8,128)S(1)}, f32[56,256,256]{2,1,0:T(8,128)S(1)}) custom-call(s32[8,128]{1,0:T(8,128)S(1)} %get-tuple-element.30.tab, s32[2,8,256]{2,1,0:T(8,128)S(1)} %get-tuple-element.31.row_tab, ...), custom_call_target="tpu_custom_call", output_to_operand_aliasing={{1}: (4, {})} | custom-call | tf_op jit(solution)/shard_map/forward_stats/pallas_call | solution.py:329
  23.0 7.8 %exchange_stats.1 = (f32[4,3,8,256]{3,2,1,0:T(8,128)S(1)}, f32[8,128,256]{2,1,0:T(8,128)S(1)}, f32[8,256,256]{2,1,0:T(8,128)S(1)}, f32[8,256,256]{2,1,0:T(8,128)S(1)}) custom-call(s32[8,128]{1,0:T(8,128)S(1)} %get-tuple-element.30.tab, s32[2,8,256]{2,1,0:T(8,128)S(1)} %get-tuple-element.31.row_tab, bf16[4,2,512,128]{3,2,1,0:T(8,128)(2,1)S(1)} %get-tuple-element.32.qg, ...), custom_call_target="tpu_custom_call" | custom-call | tf_op jit(solution)/shard_map/exchange_stats/pallas_call | solution.py:375
  30.9 1.7 %backward_terms.1 = (f32[8,256]{1,0:T(8,128)S(1)}, f32[8,128,256]{2,1,0:T(8,128)S(1)}, f32[2,16,2,64,128]{4,3,2,1,0:T(8,128)S(1)}) custom-call(s32[8,128]{1,0:T(8,128)S(1)} %get-tuple-element.30.tab, bf16[4,2,512,128]{3,2,1,0:T(8,128)(2,1)S(1)} %get-tuple-element.32.qg, ...), custom_call_target="tpu_custom_call", output_to_operand_aliasing={{1}: (8, {}), {2}: (9, {})} | custom-call | tf_op jit(solution)/shard_map/backward_terms/pallas_call | solution.py:429
  32.6 20.3 %reduce_terms.1 = (bf16[512,128]{1,0:T(8,128)(2,1)S(1)}, bf16[512,128]{1,0:T(8,128)(2,1)S(1)}, bf16[128,128]{1,0:T(8,128)(2,1)S(1)}, bf16[128,128]{1,0:T(8,128)(2,1)S(1)}) custom-call(f32[8,128,256]{2,1,0:T(8,128)S(1)} %get-tuple-element.37.acc, f32[8,256]{1,0:T(8,128)S(1)} %get-tuple-element.45.share, f32[8,128,256]{2,1,0:T(8,128)S(1)} %get-tuple-element.46.grad, ...), custom_call_target="tpu_custom_call" | custom-call | tf_op jit(solution)/shard_map/reduce_terms/pallas_call | solution.py:603
  52.9 0.7 %store_outputs.1 = (bf16[512,128]{1,0:T(8,128)(2,1)}, bf16[512,128]{1,0:T(8,128)(2,1)}, bf16[128,128]{1,0:T(8,128)(2,1)}, bf16[128,128]{1,0:T(8,128)(2,1)}) custom-call(bf16[512,128]{1,0:T(8,128)(2,1)S(1)} %get-tuple-element.48.refs_0_, bf16[512,128]{1,0:T(8,128)(2,1)S(1)} %get-tuple-element.49.refs_1_, bf16[128,128]{1,0:T(8,128)(2,1)S(1)} %get-tuple-element.50.refs_2_, ...), custom_call_target="tpu_custom_call" | custom-call | tf_op jit(solution)/shard_map/store_outputs/pallas_call | solution.py:645

commit v6 on v5

--- a/solution.py
+++ b/solution.py
@@ -20,7 +20,6 @@
 TILE = 4
 SPANS = 128
 ITEMS = QRUNS * (KRUNS // TILE - 1)
-UNROLL = 4
 DOCS = 8
 NEGATIVE = -1e30
 FLOOR = -1e29
@@ -116,7 +115,6 @@
     z_to = {d: device(x, y, (z + d + NZ) % NZ) for d in (1, 2, -1, -2)}
     x_up, x_dn = device((x + 1) % NX, y, z), device((x + NX - 1) % NX, y, z)
     meet = greet([y_up, y_dn, x_up, x_dn] + list(z_to.values()))
-    kv = (k_ref, v_ref)
     started = []
 
     def go(copy):
@@ -126,13 +124,17 @@
 
     sent_z = {}
 
-    def z_send(sign, hops, dist, part):
-        block = (z - sign * (dist - hops) + NZ) % NZ
-        dst = kg.at[first + block, part]
-        src = kv[part] if dist == hops else dst
+    def part(j):
+        return (h + j) % 2
+
+    def behind(sign, dist):
+        return (z - sign * dist + NZ) % NZ
+
+    def z_send(sign, hops, dist, j):
+        ref = kg.at[first + behind(sign, dist - hops), part(j)]
         way = 0 if sign > 0 else 1
-        sems = zsend.at[way, dist - 1, part], zrecv.at[way, dist - 1, part]
-        sent_z[sign, dist, part] = go(remote(src, dst, *sems, z_to[sign * hops]))
+        sems = zsend.at[way, dist - 1, j], zrecv.at[way, dist - 1, j]
+        sent_z[sign, dist, j] = go(remote(ref, ref, *sems, z_to[sign * hops]))
 
     sent_x = []
 
@@ -146,52 +148,48 @@
         copy.start()
         return copy
 
-    own_kv = [local(kv[part], kg.at[first + z, part], part) for part in (0, 1)]
+    own_kv = [local(ref, kg.at[first + z, i], i) for i, ref in enumerate((k_ref, v_ref))]
     own_tab = [local(bal_ref, bal, 4), local(len_ref, lengths, 5)]
+    for copy in own_kv:
+        copy.wait()
     meet()
-    for part in (0, 1):
+    for j in (0, 1):
         for sign in (1, -1):
-            z_send(sign, 2, 2, part)
+            z_send(sign, 2, 2, j)
     y_q_up = go(remote(q_ref, qg.at[y, 0], ysend.at[0], yrecv.at[0], y_up))
     y_g_dn = go(remote(g_ref, qg.at[y, 1], ysend.at[2], yrecv.at[2], y_dn))
-    for part in (0, 1):
-        for sign in (1, -1):
-            z_send(sign, 1, 1, part)
+    x_send(0, z)
+    for sign in (1, -1):
+        z_send(sign, 1, 1, 0)
     y_g_up = go(remote(g_ref, qg.at[y, 1], ysend.at[1], yrecv.at[1], y_up))
     y_q_dn = go(remote(q_ref, qg.at[y, 0], ysend.at[3], yrecv.at[3], y_dn))
-    own_q = [local(ref, qg.at[y, part], 2 + part) for part, ref in ((0, q_ref), (1, g_ref))]
-    for copy in own_kv:
-        copy.wait()
-    x_send(0, z)
+    own_q = [local(ref, qg.at[y, i], 2 + i) for i, ref in enumerate((q_ref, g_ref))]
     for copy in own_tab:
         copy.wait()
     tables(bal, lengths, tab, row_tab, xl, y, z)
-    for ref in (zeros_acc, zeros_grad, zeros_kv):
-        ref[...] = jnp.zeros_like(ref)
-    for part in (0, 1):
+    for j in (0, 1):
         for sign in (1, -1):
-            sent_z[sign, 2, part].wait_recv()
-            z_send(sign, 1, 3, part)
-            if part == (0 if sign > 0 else 1):
-                z_send(sign, 2, 4, part)
-    x_send(1, (z - 2 + NZ) % NZ)
-    x_send(2, (z + 2) % NZ)
+            sent_z[sign, 2, j].wait_recv()
+            if j == (0 if sign > 0 else 1):
+                z_send(sign, 2, 4, j)
+            z_send(sign, 1, 3, j)
+            if j == 0:
+                x_send(1 if sign > 0 else 2, behind(sign, 2))
+    for sign in (1, -1):
+        z_send(sign, 1, 1, 1)
     y_q_up.wait_recv()
     q_on = qg.at[(y + NY - 1) % NY, 0]
     y_fwd_up = go(remote(q_on, q_on, ysend.at[4], yrecv.at[4], y_up))
     y_g_dn.wait_recv()
     g_on = qg.at[(y + 1) % NY, 1]
     y_fwd_dn = go(remote(g_on, g_on, ysend.at[5], yrecv.at[5], y_dn))
-    slot = 3
-    for dist in (1, 3):
-        for sign in (1, -1):
-            for part in (0, 1):
-                sent_z[sign, dist, part].wait_recv()
-            x_send(slot, (z - sign * dist + NZ) % NZ)
-            slot += 1
-    sent_z[1, 4, 0].wait_recv()
-    sent_z[-1, 4, 1].wait_recv()
-    x_send(7, (z + NZ // 2) % NZ)
+    for slot, (sign, dist) in enumerate(((1, 1), (-1, 1), (1, 4), (1, 3), (-1, 3))):
+        sent_z[sign, dist, 0].wait_recv()
+        x_send(3 + slot, behind(sign, dist))
+    for ref in (zeros_acc, zeros_grad, zeros_kv):
+        ref[...] = jnp.zeros_like(ref)
+    for sign, dist in ((1, 1), (-1, 1), (1, 3), (-1, 3), (-1, 4)):
+        sent_z[sign, dist, 1].wait_recv()
     for copy in (y_g_up, y_q_dn, y_fwd_up, y_fwd_dn):
         copy.wait_recv()
     for copy in sent_x:
@@ -259,20 +257,21 @@
 
 
 def first_tiles(process):
-    def step(i, _):
-        together(process, [(UNROLL * i + u, 0, UNROLL * i + u) for u in range(UNROLL)])
-        return 0
-
-    lax.fori_loop(0, QRUNS // UNROLL, step, 0)
+    together(process, [(q_run, 0, q_run) for q_run in range(QRUNS)])
 
 
 def further_tiles(tab, process):
-    def step(i, _):
-        slots = [UNROLL * i + u for u in range(UNROLL)]
-        together(process, [(tab[3, slot], tab[4, slot], slot) for slot in slots])
-        return 0
-
-    lax.fori_loop(0, (tab[5, 0] + UNROLL - 1) // UNROLL, step, 0)
+    def steps(unroll, first, count):
+        def step(i, _):
+            slots = [first + unroll * i + u for u in range(unroll)]
+            together(process, [(tab[3, slot], tab[4, slot], slot) for slot in slots])
+            return 0
+
+        lax.fori_loop(0, count, step, 0)
+
+    fours = tab[5, 0] // 4
+    steps(4, 0, fours)
+    steps(2, 4 * fours, (tab[5, 0] - 4 * fours + 1) // 2)
 
 
 def query_rows(qg, q_run, part):
@@ -511,15 +510,15 @@
     meet()
     tell(z_word, z_near)
     tell(x_word, x_near)
+    for i in range(len(AHEAD)):
+        for way in (0, 1):
+            if i < len(offsets[way]):
+                sent[0, way, i] = x_copy(0, way, i, xout.at[0, way, i])
     near = []
     for lo in range(XLO):
         for side, offset in ((0, 1), (1, NZ - 1)):
             sems = nsend.at[side, lo], nrecv.at[side, lo]
             near.append(go(remote(nout.at[side, lo], nbuf.at[side, lo], *sems, z_to[offset])))
-    for i in range(len(AHEAD)):
-        for way in (0, 1):
-            if i < len(offsets[way]):
-                sent[0, way, i] = x_copy(0, way, i, xout.at[0, way, i])
     for i in range(len(AHEAD)):
         for way in (0, 1):
             if i < len(offsets[1 - way]):

time: 53.7 us -> 53.1 us (0.989)
  Pallas kernels: 53 us -> 52.3 us
    pallas_call x1, Pallas kernels: 0.62 us -> 1.84 us  [forward(): pl.pallas_call(forward_kernel, out_shape=(jax.ShapeDtypeStruct((3, QRUNS,...]
    pallas_call x1, Pallas kernels: 21.7 us -> 20.5 us  [gather(): pl.pallas_call(gather_kernel, out_shape=(jax.ShapeDtypeStruct((NY, 2, 2 *...]
    pallas_call x1, Pallas kernels: 20.3 us -> 19.4 us  [reduce(): pl.pallas_call(reduce_kernel, out_shape=(jax.ShapeDtypeStruct((2 * ROWS,...]
    pallas_call x1, Pallas kernels: 1.74 us -> 2.31 us  [backward(): pl.pallas_call(backward_kernel, out_shape=(jax.ShapeDtypeStruct((QRUNS, R...]
where the time goes in v6:
time: 53.1 us; the launch traced here: 53 us
  Pallas kernels  52.3 us (98%)
  between operations  0.67 us (1%)
    pallas_call x1, Pallas kernels, gather(): pl.pallas_call(gather_kernel, out_shape=(jax.ShapeDtypeStruct((NY, 2, 2 *...  20.5 us
    pallas_call x1, Pallas kernels, reduce(): pl.pallas_call(reduce_kernel, out_shape=(jax.ShapeDtypeStruct((2 * ROWS,...  19.4 us
    pallas_call x1, Pallas kernels, exchange(): pl.pallas_call(exchange_kernel, out_shape=(jax.ShapeDtypeStruct((NY,) + p...  7.43 us
    pallas_call x1, Pallas kernels, backward(): pl.pallas_call(backward_kernel, out_shape=(jax.ShapeDtypeStruct((QRUNS, R...  2.31 us
    pallas_call x1, Pallas kernels, forward(): pl.pallas_call(forward_kernel, out_shape=(jax.ShapeDtypeStruct((3, QRUNS,...  1.84 us

profile of v6, /device:TPU:2, one launch (start us, length us, event | category | flops | bytes accessed | tf_op | source)
XLA Modules:
  0.0 53.0 jit_solution(6852548402697196346)
XLA Ops:
  0.6 20.5 %gather_rows.1 = (bf16[4,2,512,128]{3,2,1,0:T(8,128)(2,1)S(1)}, bf16[16,2,2,64,128]{4,3,2,1,0:T(8,128)(2,1)S(1)}, s32[8,128]{1,0:T(8,128)S(1)}, s32[2,8,256]{2,1...) custom-call(bf16[512,128]{1,0:T(8,128)(2,1)} %bitcast.9, ...), custom_call_target="tpu_custom_call" | custom-call | tf_op jit(solution)/shard_map/gather_rows/pallas_call | solution.py:214
  21.2 1.8 %forward_stats.1 = (f32[3,8,256]{2,1,0:T(8,128)S(1)}, f32[8,128,256]{2,1,0:T(8,128)S(1)}, f32[56,256,256]{2,1,0:T(8,128)S(1)}, f32[56,256,256]{2,1,0:T(8,128)S(1)}) custom-call(s32[8,128]{1,0:T(8,128)S(1)} %get-tuple-element.30.tab, s32[2,8,256]{2,1,0:T(8,128)S(1)} %get-tuple-element.31.row_tab, ...), custom_call_target="tpu_custom_call", output_to_operand_aliasing={{1}: (4, {})} | custom-call | tf_op jit(solution)/shard_map/forward_stats/pallas_call | solution.py:328
  23.0 7.4 %exchange_stats.1 = (f32[4,3,8,256]{3,2,1,0:T(8,128)S(1)}, f32[8,128,256]{2,1,0:T(8,128)S(1)}, f32[8,256,256]{2,1,0:T(8,128)S(1)}, f32[8,256,256]{2,1,0:T(8,128)S(1)}) custom-call(s32[8,128]{1,0:T(8,128)S(1)} %get-tuple-element.30.tab, s32[2,8,256]{2,1,0:T(8,128)S(1)} %get-tuple-element.31.row_tab, bf16[4,2,512,128]{3,2,1,0:T(8,128)(2,1)S(1)} %get-tuple-element.32.qg, ...), custom_call_target="tpu_custom_call" | custom-call | tf_op jit(solution)/shard_map/exchange_stats/pallas_call | solution.py:374
  30.5 2.3 %backward_terms.1 = (f32[8,256]{1,0:T(8,128)S(1)}, f32[8,128,256]{2,1,0:T(8,128)S(1)}, f32[2,16,2,64,128]{4,3,2,1,0:T(8,128)S(1)}) custom-call(s32[8,128]{1,0:T(8,128)S(1)} %get-tuple-element.30.tab, bf16[4,2,512,128]{3,2,1,0:T(8,128)(2,1)S(1)} %get-tuple-element.32.qg, ...), custom_call_target="tpu_custom_call", output_to_operand_aliasing={{1}: (8, {}), {2}: (9, {})} | custom-call | tf_op jit(solution)/shard_map/backward_terms/pallas_call | solution.py:428
  32.8 19.4 %reduce_terms.1 = (bf16[512,128]{1,0:T(8,128)(2,1)S(1)}, bf16[512,128]{1,0:T(8,128)(2,1)S(1)}, bf16[128,128]{1,0:T(8,128)(2,1)S(1)}, bf16[128,128]{1,0:T(8,128)(2,1)S(1)}) custom-call(f32[8,128,256]{2,1,0:T(8,128)S(1)} %get-tuple-element.37.acc, f32[8,256]{1,0:T(8,128)S(1)} %get-tuple-element.45.share, f32[8,128,256]{2,1,0:T(8,128)S(1)} %get-tuple-element.46.grad, ...), custom_call_target="tpu_custom_call" | custom-call | tf_op jit(solution)/shard_map/reduce_terms/pallas_call | solution.py:602
  52.2 0.7 %store_outputs.1 = (bf16[512,128]{1,0:T(8,128)(2,1)}, bf16[512,128]{1,0:T(8,128)(2,1)}, bf16[128,128]{1,0:T(8,128)(2,1)}, bf16[128,128]{1,0:T(8,128)(2,1)}) custom-call(bf16[512,128]{1,0:T(8,128)(2,1)S(1)} %get-tuple-element.48.refs_0_, bf16[512,128]{1,0:T(8,128)(2,1)S(1)} %get-tuple-element.49.refs_1_, bf16[128,128]{1,0:T(8,128)(2,1)S(1)} %get-tuple-element.50.refs_2_, ...), custom_call_target="tpu_custom_call" | custom-call | tf_op jit(solution)/shard_map/store_outputs/pallas_call | solution.py:644

commit v7 on v6

--- a/solution.py
+++ b/solution.py
@@ -17,9 +17,10 @@
 BLK = 2 * RUN
 KRUNS = XLO * NZ * 2
 QRUNS = NY * 2
-TILE = 4
+TILE = 3
 SPANS = 128
-ITEMS = QRUNS * (KRUNS // TILE - 1)
+MOST_TILES = (KRUNS + TILE - 1) // TILE
+ITEMS = QRUNS * (MOST_TILES - 1)
 DOCS = 8
 NEGATIVE = -1e30
 FLOOR = -1e29
@@ -97,7 +98,7 @@
     run_row = jnp.minimum(jnp.sum(jnp.where(passed, 1, 0), axis=0, keepdims=True), QRUNS - 1)
     tile_row = lane + 1 - jnp.sum(jnp.where(passed, more, 0), axis=0, keepdims=True)
     count = jnp.sum(more, axis=0, keepdims=True)
-    tile_row = jnp.where(lane >= count, KRUNS // TILE, tile_row)
+    tile_row = jnp.where(lane >= count, MOST_TILES, tile_row)
     values = [None, None, low_row, run_row, tile_row, jnp.where(lane == 0, count, 0)]
     out = sorted_runs
     for i in range(2, 6):
@@ -114,7 +115,7 @@
     y_up, y_dn = device(x, (y + 1) % NY, z), device(x, (y + NY - 1) % NY, z)
     z_to = {d: device(x, y, (z + d + NZ) % NZ) for d in (1, 2, -1, -2)}
     x_up, x_dn = device((x + 1) % NX, y, z), device((x + NX - 1) % NX, y, z)
-    meet = greet([y_up, y_dn, x_up, x_dn] + list(z_to.values()))
+    meet = greet([z_to[2], z_to[-2], z_to[1], z_to[-1], y_up, y_dn, x_up, x_dn])
     started = []
 
     def go(copy):
@@ -341,11 +342,16 @@
     )(tab, row_tab, qg, kg, zeros)
 
 
-def exchange_kernel(tab, row_tab, qg, kg, part, part_acc, out, acc_out, held, held_gw, mine, lsem, send, recv):
+def exchange_kernel(
+    tab_ref, row_tab, qg, kg, part, part_acc, out, acc_out, held, held_gw, tab, mine, lsem, send, recv
+):
     h, xl, y, z = here()
     x = h * XLO + xl
-    targets = [device(x, (y + d) % NY, z) for d in range(1, NY)]
+    targets = [device(x, (y + d) % NY, z) for d in (2, 1, 3)]
     meet = greet(targets)
+    table = pltpu.make_async_copy(tab_ref, tab, lsem)
+    table.start()
+    table.wait()
 
     def combine(q_run, *new):
         at = pl.ds(q_run, 1)
@@ -368,7 +374,6 @@
 
 
 def exchange(tab, row_tab, qg, kg, part, part_acc):
-    smem = pl.BlockSpec(memory_space=pltpu.SMEM)
     vmem = pl.BlockSpec(memory_space=pltpu.VMEM)
     dma = pltpu.SemaphoreType.DMA
     return pl.pallas_call(
@@ -379,9 +384,9 @@
             jax.ShapeDtypeStruct((QRUNS, TILE * RUN, ROWS), F32),
             jax.ShapeDtypeStruct((QRUNS, TILE * RUN, ROWS), F32),
         ),
-        in_specs=[smem] + [vmem] * 5,
+        in_specs=[vmem] * 6,
         out_specs=(vmem,) * 4,
-        scratch_shapes=[pltpu.VMEM(part.shape, F32), dma, dma((NY - 1,)), dma((NY - 1,))],
+        scratch_shapes=[pltpu.SMEM(tab.shape, jnp.int32), pltpu.VMEM(part.shape, F32), dma, dma((NY - 1,)), dma((NY - 1,))],
         compiler_params=pltpu.CompilerParams(collective_id=1, has_side_effects=True, vmem_limit_bytes=8 << 20),
         name="exchange_stats",
     )(tab, row_tab, qg, kg, part, part_acc)

time: 53.1 us -> 52.6 us (level)
  Pallas kernels: 52.3 us -> 51.3 us
    pallas_call x1, Pallas kernels: 7.43 us -> 5.74 us  [exchange(): pl.pallas_call(exchange_kernel, out_shape=(jax.ShapeDtypeStruct((NY,) + p...]
where the time goes in v7:
time: 52.6 us; the launch traced here: 52 us
  Pallas kernels  51.3 us (98%)
  between operations  0.67 us (1%)
    pallas_call x1, Pallas kernels, gather(): pl.pallas_call(gather_kernel, out_shape=(jax.ShapeDtypeStruct((NY, 2, 2 *...  20.7 us
    pallas_call x1, Pallas kernels, reduce(): pl.pallas_call(reduce_kernel, out_shape=(jax.ShapeDtypeStruct((2 * ROWS,...  20 us
    pallas_call x1, Pallas kernels, exchange(): pl.pallas_call(exchange_kernel, out_shape=(jax.ShapeDtypeStruct((NY,) + p...  5.74 us
    pallas_call x1, Pallas kernels, backward(): pl.pallas_call(backward_kernel, out_shape=(jax.ShapeDtypeStruct((QRUNS, R...  2.17 us
    pallas_call x1, Pallas kernels, forward(): pl.pallas_call(forward_kernel, out_shape=(jax.ShapeDtypeStruct((3, QRUNS,...  2.07 us

profile of v7, /device:TPU:2, one launch (start us, length us, event | category | flops | bytes accessed | tf_op | source)
XLA Modules:
  0.0 52.0 jit_solution(14343035157155510041)
XLA Ops:
  0.6 20.7 %gather_rows.1 = (bf16[4,2,512,128]{3,2,1,0:T(8,128)(2,1)S(1)}, bf16[16,2,2,64,128]{4,3,2,1,0:T(8,128)(2,1)S(1)}, s32[8,128]{1,0:T(8,128)S(1)}, s32[2,8,256]{2,1...) custom-call(bf16[512,128]{1,0:T(8,128)(2,1)} %bitcast.9, ...), custom_call_target="tpu_custom_call" | custom-call | tf_op jit(solution)/shard_map/gather_rows/pallas_call | solution.py:215
  21.3 2.1 %forward_stats.1 = (f32[3,8,256]{2,1,0:T(8,128)S(1)}, f32[8,128,256]{2,1,0:T(8,128)S(1)}, f32[80,192,256]{2,1,0:T(8,128)S(1)}, f32[80,192,256]{2,1,0:T(8,128)S(1)}) custom-call(s32[8,128]{1,0:T(8,128)S(1)} %get-tuple-element.30.tab.tab_ref, s32[2,8,256]{2,1,0:T(8,128)S(1)} %get-tuple-element.31.row_tab, ...), custom_call_target="tpu_custom_call", output_to_operand_aliasing={{1}: (4, {})} | custom-call | tf_op jit(solution)/shard_map/forward_stats/pallas_call | solution.py:329
  23.4 5.7 %exchange_stats.1 = (f32[4,3,8,256]{3,2,1,0:T(8,128)S(1)}, f32[8,128,256]{2,1,0:T(8,128)S(1)}, f32[8,192,256]{2,1,0:T(8,128)S(1)}, f32[8,192,256]{2,1,0:T(8,128)S(1)}) custom-call(s32[8,128]{1,0:T(8,128)S(1)} %get-tuple-element.30.tab.tab_ref, s32[2,8,256]{2,1,0:T(8,128)S(1)} %get-tuple-element.31.row_tab, ...), custom_call_target="tpu_custom_call" | custom-call | tf_op jit(solution)/shard_map/exchange_stats/pallas_call | solution.py:379
  29.1 2.2 %backward_terms.1 = (f32[8,256]{1,0:T(8,128)S(1)}, f32[8,128,256]{2,1,0:T(8,128)S(1)}, f32[2,16,2,64,128]{4,3,2,1,0:T(8,128)S(1)}) custom-call(s32[8,128]{1,0:T(8,128)S(1)} %get-tuple-element.30.tab.tab_ref, bf16[4,2,512,128]{3,2,1,0:T(8,128)(2,1)S(1)} %get-tuple-element.32.qg, ...), custom_call_target="tpu_custom_call", output_to_operand_aliasing={{1}: (8, {}), {2}: (9, {})} | custom-call | tf_op jit(solution)/shard_map/backward_terms/pallas_call | solution.py:433
  31.3 20.0 %reduce_terms.1 = (bf16[512,128]{1,0:T(8,128)(2,1)S(1)}, bf16[512,128]{1,0:T(8,128)(2,1)S(1)}, bf16[128,128]{1,0:T(8,128)(2,1)S(1)}, bf16[128,128]{1,0:T(8,128)(2,1)S(1)}) custom-call(f32[8,128,256]{2,1,0:T(8,128)S(1)} %get-tuple-element.37.acc, f32[8,256]{1,0:T(8,128)S(1)} %get-tuple-element.45.share, f32[8,128,256]{2,1,0:T(8,128)S(1)} %get-tuple-element.46.grad, ...), custom_call_target="tpu_custom_call" | custom-call | tf_op jit(solution)/shard_map/reduce_terms/pallas_call | solution.py:607
  51.3 0.7 %store_outputs.1 = (bf16[512,128]{1,0:T(8,128)(2,1)}, bf16[512,128]{1,0:T(8,128)(2,1)}, bf16[128,128]{1,0:T(8,128)(2,1)}, bf16[128,128]{1,0:T(8,128)(2,1)}) custom-call(bf16[512,128]{1,0:T(8,128)(2,1)S(1)} %get-tuple-element.48.refs_0_, bf16[512,128]{1,0:T(8,128)(2,1)S(1)} %get-tuple-element.49.refs_1_, bf16[128,128]{1,0:T(8,128)(2,1)S(1)} %get-tuple-element.50.refs_2_, ...), custom_call_target="tpu_custom_call" | custom-call | tf_op jit(solution)/shard_map/store_outputs/pallas_call | solution.py:649

commit v8 on v7

--- a/solution.py
+++ b/solution.py
@@ -17,9 +17,10 @@
 BLK = 2 * RUN
 KRUNS = XLO * NZ * 2
 QRUNS = NY * 2
+FIRST = 4
 TILE = 3
 SPANS = 128
-MOST_TILES = (KRUNS + TILE - 1) // TILE
+MOST_TILES = 1 + (KRUNS - FIRST + TILE - 1) // TILE
 ITEMS = QRUNS * (MOST_TILES - 1)
 DOCS = 8
 NEGATIVE = -1e30
@@ -87,7 +88,7 @@
     row_tab[1] = start
     low_run = jnp.sum(jnp.where((lane < first // RUN) & (has > 0), 1, 0), axis=1, keepdims=True)
     high_run = jnp.sum(jnp.where((lane <= low // RUN) & (has > 0), 1, 0), axis=1, keepdims=True)
-    tiles = jnp.maximum((high_run - low_run + TILE - 1) // TILE, 1)
+    tiles = 1 + jnp.maximum(high_run - low_run - FIRST + TILE - 1, 0) // TILE
     own_lane = lax.broadcasted_iota(jnp.int32, (QRUNS, 1), 0) == lane
     low_row = jnp.sum(jnp.where(own_lane, low_run, 0), axis=0, keepdims=True)
     more = tiles - 1
@@ -234,7 +235,10 @@
 
 
 def tile_runs(tab, low_run, t):
-    runs = [low_run + t * TILE + u for u in range(TILE)]
+    if t is None:
+        runs = [low_run + u for u in range(FIRST)]
+    else:
+        runs = [low_run + FIRST + (t - 1) * TILE + u for u in range(TILE)]
     return [(tab[1, r], tab[6, r]) for r in runs], [tab[0, r] * RUN for r in runs]
 
 
@@ -258,7 +262,7 @@
 
 
 def first_tiles(process):
-    together(process, [(q_run, 0, q_run) for q_run in range(QRUNS)])
+    together(process, [(q_run, None, q_run) for q_run in range(QRUNS)])
 
 
 def further_tiles(tab, process):
@@ -381,8 +385,8 @@
         out_shape=(
             jax.ShapeDtypeStruct((NY,) + part.shape, F32),
             jax.ShapeDtypeStruct(part_acc.shape, F32),
-            jax.ShapeDtypeStruct((QRUNS, TILE * RUN, ROWS), F32),
-            jax.ShapeDtypeStruct((QRUNS, TILE * RUN, ROWS), F32),
+            jax.ShapeDtypeStruct((QRUNS, FIRST * RUN, ROWS), F32),
+            jax.ShapeDtypeStruct((QRUNS, FIRST * RUN, ROWS), F32),
         ),
         in_specs=[vmem] * 6,
         out_specs=(vmem,) * 4,

time: 52.6 us -> 52.7 us (level); the launches traced: 52 us -> 52.8 us
  Pallas kernels: 51.3 us -> 52.1 us
    pallas_call x1, Pallas kernels: 5.74 us -> 6.79 us  [exchange(): pl.pallas_call(exchange_kernel, out_shape=(jax.ShapeDtypeStruct((NY,) + p...]
where the time goes in v8:
time: 52.7 us; the launch traced here: 52.8 us
  Pallas kernels  52.1 us (99%)
  between operations  0.67 us (1%)
    pallas_call x1, Pallas kernels, gather(): pl.pallas_call(gather_kernel, out_shape=(jax.ShapeDtypeStruct((NY, 2, 2 *...  20.7 us
    pallas_call x1, Pallas kernels, reduce(): pl.pallas_call(reduce_kernel, out_shape=(jax.ShapeDtypeStruct((2 * ROWS,...  20 us
    pallas_call x1, Pallas kernels, exchange(): pl.pallas_call(exchange_kernel, out_shape=(jax.ShapeDtypeStruct((NY,) + p...  6.79 us
    pallas_call x1, Pallas kernels, backward(): pl.pallas_call(backward_kernel, out_shape=(jax.ShapeDtypeStruct((QRUNS, R...  2.23 us
    pallas_call x1, Pallas kernels, forward(): pl.pallas_call(forward_kernel, out_shape=(jax.ShapeDtypeStruct((3, QRUNS,...  1.72 us

profile of v8, /device:TPU:2, one launch (start us, length us, event | category | flops | bytes accessed | tf_op | source)
XLA Modules:
  0.0 52.8 jit_solution(8168891711915765651)
XLA Ops:
  0.6 20.7 %gather_rows.1 = (bf16[4,2,512,128]{3,2,1,0:T(8,128)(2,1)S(1)}, bf16[16,2,2,64,128]{4,3,2,1,0:T(8,128)(2,1)S(1)}, s32[8,128]{1,0:T(8,128)S(1)}, s32[2,8,256]{2,1...) custom-call(bf16[512,128]{1,0:T(8,128)(2,1)} %bitcast.9, ...), custom_call_target="tpu_custom_call" | custom-call | tf_op jit(solution)/shard_map/gather_rows/pallas_call | solution.py:216
  21.3 1.7 %forward_stats.1 = (f32[3,8,256]{2,1,0:T(8,128)S(1)}, f32[8,128,256]{2,1,0:T(8,128)S(1)}, f32[80,192,256]{2,1,0:T(8,128)S(1)}, f32[80,192,256]{2,1,0:T(8,128)S(1)}) custom-call(s32[8,128]{1,0:T(8,128)S(1)} %get-tuple-element.30.tab.tab_ref, s32[2,8,256]{2,1,0:T(8,128)S(1)} %get-tuple-element.31.row_tab, ...), custom_call_target="tpu_custom_call", output_to_operand_aliasing={{1}: (4, {})} | custom-call | tf_op jit(solution)/shard_map/forward_stats/pallas_call | solution.py:333
  23.0 6.8 %exchange_stats.1 = (f32[4,3,8,256]{3,2,1,0:T(8,128)S(1)}, f32[8,128,256]{2,1,0:T(8,128)S(1)}, f32[8,256,256]{2,1,0:T(8,128)S(1)}, f32[8,256,256]{2,1,0:T(8,128)S(1)}) custom-call(s32[8,128]{1,0:T(8,128)S(1)} %get-tuple-element.30.tab.tab_ref, s32[2,8,256]{2,1,0:T(8,128)S(1)} %get-tuple-element.31.row_tab, ...), custom_call_target="tpu_custom_call" | custom-call | tf_op jit(solution)/shard_map/exchange_stats/pallas_call | solution.py:383
  29.8 2.2 %backward_terms.1 = (f32[8,256]{1,0:T(8,128)S(1)}, f32[8,128,256]{2,1,0:T(8,128)S(1)}, f32[2,16,2,64,128]{4,3,2,1,0:T(8,128)S(1)}) custom-call(s32[8,128]{1,0:T(8,128)S(1)} %get-tuple-element.30.tab.tab_ref, bf16[4,2,512,128]{3,2,1,0:T(8,128)(2,1)S(1)} %get-tuple-element.32.qg, ...), custom_call_target="tpu_custom_call", output_to_operand_aliasing={{1}: (8, {}), {2}: (9, {})} | custom-call | tf_op jit(solution)/shard_map/backward_terms/pallas_call | solution.py:437
  32.1 20.0 %reduce_terms.1 = (bf16[512,128]{1,0:T(8,128)(2,1)S(1)}, bf16[512,128]{1,0:T(8,128)(2,1)S(1)}, bf16[128,128]{1,0:T(8,128)(2,1)S(1)}, bf16[128,128]{1,0:T(8,128)(2,1)S(1)}) custom-call(f32[8,128,256]{2,1,0:T(8,128)S(1)} %get-tuple-element.37.acc, f32[8,256]{1,0:T(8,128)S(1)} %get-tuple-element.45.share, f32[8,128,256]{2,1,0:T(8,128)S(1)} %get-tuple-element.46.grad, ...), custom_call_target="tpu_custom_call" | custom-call | tf_op jit(solution)/shard_map/reduce_terms/pallas_call | solution.py:611
  52.0 0.7 %store_outputs.1 = (bf16[512,128]{1,0:T(8,128)(2,1)}, bf16[512,128]{1,0:T(8,128)(2,1)}, bf16[128,128]{1,0:T(8,128)(2,1)}, bf16[128,128]{1,0:T(8,128)(2,1)}) custom-call(bf16[512,128]{1,0:T(8,128)(2,1)S(1)} %get-tuple-element.48.refs_0_, bf16[512,128]{1,0:T(8,128)(2,1)S(1)} %get-tuple-element.49.refs_1_, bf16[128,128]{1,0:T(8,128)(2,1)S(1)} %get-tuple-element.50.refs_2_, ...), custom_call_target="tpu_custom_call" | custom-call | tf_op jit(solution)/shard_map/store_outputs/pallas_call | solution.py:653
